TPU v7x, 32 devices: a whole 2x2x4 slice. The times are simulated.
32 devices in a mesh: seq: 2 (over x), ctx: 8 (over z, y), fsdp: 2 (over core).
Axes of the slice: x: 2, y: 2, z: 4, core: 2. Of those that a mesh axis runs over, the one named last changes fastest.
Arguments:
- hidden: bfloat16 [4, 1280, 768], P(('seq', 'fsdp'), 'ctx'), may hold values from -6 to 6
- segment_ids: int32 [4, 1280], P(('seq', 'fsdp')), may hold values from 0 to 15, never falling along the last dimension, each value on 1 to 960 neighbouring positions
- out_grad: bfloat16 [4, 1280, 768], P(('seq', 'fsdp'), 'ctx'), may hold values from -6 to 6
- w_qkv: bfloat16 [768, 2304], P('fsdp'), may hold values from -0.21875 to 0.21875
- bias_query: bfloat16 [768], P('fsdp'), may hold values from -3 to 3
- bias_value: bfloat16 [768], P('fsdp'), may hold values from -3 to 3
- w_out: bfloat16 [768, 768], P('fsdp'), may hold values from -0.625 to 0.625
- bias_out: bfloat16 [768], P('fsdp'), may hold values from -2 to 2
- gain_one: bfloat16 [768], P('fsdp'), may hold values from 0.25 to 1.75
- shift_one: bfloat16 [768], P('fsdp'), may hold values from -2 to 2
- w_up: bfloat16 [768, 3072], P('fsdp'), may hold values from -0.21875 to 0.21875
- bias_up: bfloat16 [3072], P('fsdp'), may hold values from -3 to 3
- w_down: bfloat16 [3072, 768], P('fsdp'), may hold values from -0.109375 to 0.109375
- bias_down: bfloat16 [768], P('fsdp'), may hold values from -2 to 2
- gain_two: bfloat16 [768], P('fsdp'), may hold values from 0.25 to 1.75
- shift_two: bfloat16 [768], P('fsdp'), may hold values from -2 to 2
Outputs:
- output: bfloat16 [4, 1280, 768], P(('seq', 'fsdp'), 'ctx')
- grad_hidden: float32 [4, 1280, 768], P(('seq', 'fsdp'), 'ctx')
- grad_w_qkv: float32 [768, 2304], P(('ctx', 'fsdp'))
- grad_bias_query: float32 [768], P(('ctx', 'fsdp'))
- grad_bias_value: float32 [768], P(('ctx', 'fsdp'))
- grad_w_out: float32 [768, 768], P(('ctx', 'fsdp'))
- grad_bias_out: float32 [768], P(('ctx', 'fsdp'))
- grad_gain_one: float32 [768], P(('ctx', 'fsdp'))
- grad_shift_one: float32 [768], P(('ctx', 'fsdp'))
- grad_w_up: float32 [768, 3072], P(('ctx', 'fsdp'))
- grad_bias_up: float32 [3072], P(('ctx', 'fsdp'))
- grad_w_down: float32 [3072, 768], P(('ctx', 'fsdp'))
- grad_bias_down: float32 [768], P(('ctx', 'fsdp'))
- grad_gain_two: float32 [768], P(('ctx', 'fsdp'))
- grad_shift_two: float32 [768], P(('ctx', 'fsdp'))
Inputs may be any that keep to these rules, and one draw needn't show every extreme that they name: `segment_ids`: each row numbers its 16 documents 0 to 15 in order, never falling, each document a run of consecutive tokens; the longest has exactly 960 tokens.
All inputs are finite; a program needn't handle non-finite values.
Results may differ from a plain program's by a relative error of at most 0.015.
Values may be sent and summed in bfloat16 or wider, within the bound.
A program may use at most 256 MiB of HBM per device.

v0:
```python
import jax
import jax.numpy as jnp
from jax import lax
from jax.sharding import PartitionSpec as P

HEAD = 64


EPSILON = 1e-12
NEGATIVE = -1e30
LOG_TWO = 0.6931471805599453
LOG2_E = 1.4426950408889634


def norm_forward(rows_in, gain_vec, shift_vec):
    row_mean = jnp.mean(rows_in, axis=-1, keepdims=True)
    centered = rows_in - row_mean
    variance = jnp.mean(centered * centered, axis=-1, keepdims=True)
    scaled = lax.rsqrt(variance + EPSILON)
    normed = centered * scaled
    return (normed * gain_vec + shift_vec, normed, scaled)


def norm_backward(grad_rows, normed, scaled, gain_vec):
    grad_normed = grad_rows * gain_vec
    inner_part = (
        grad_normed
        - jnp.mean(grad_normed, axis=-1, keepdims=True)
        - normed * jnp.mean(grad_normed * normed, axis=-1, keepdims=True)
    )
    return (inner_part * scaled, jnp.sum(grad_rows * normed, axis=0), jnp.sum(grad_rows, axis=0))


def head_scores(query_heads, key_heads):
    return (
        jnp.einsum("qhd,khd->hqk", query_heads, key_heads, preferred_element_type=jnp.float32)
        * 0.125
    )


def column_sums(rows_b):
    return jnp.sum(rows_b.astype(jnp.float32), axis=0)


def sweep(steps_total, advance, start_carry):

    def advance_one(running, block_index):
        running = advance(running, block_index)
        return (running, None)

    return lax.scan(advance_one, start_carry, jnp.arange(steps_total))[0]


def local_grads(scores, allowed, shift_rows, ratio_rows, grad_heads, value_heads):
    unnorm = jnp.where(allowed, jnp.exp(scores - shift_rows[..., None]), 0.0)
    grad_weights = jnp.einsum(
        "qhd,khd->hqk", grad_heads, value_heads, preferred_element_type=jnp.float32
    )
    grad_scores = (unnorm * (grad_weights - ratio_rows[..., None])).astype(jnp.bfloat16)
    return (unnorm.astype(jnp.bfloat16), grad_scores)


def on_device(
    hidden,
    segment_ids,
    out_grad,
    w_qkv,
    bias_query,
    bias_value,
    w_out,
    bias_out,
    gain_one,
    shift_one,
    w_up,
    bias_up,
    w_down,
    bias_down,
    gain_two,
    shift_two,
):
    (
        w_qkv,
        bias_query,
        bias_value,
        w_out,
        bias_out,
        gain_one,
        shift_one,
        w_up,
        bias_up,
        w_down,
        bias_down,
        gain_two,
        shift_two,
    ) = (
        lax.all_gather(w_qkv, "fsdp", axis=0, tiled=True),
        lax.all_gather(bias_query, "fsdp", axis=0, tiled=True),
        lax.all_gather(bias_value, "fsdp", axis=0, tiled=True),
        lax.all_gather(w_out, "fsdp", axis=0, tiled=True),
        lax.all_gather(bias_out, "fsdp", axis=0, tiled=True),
        lax.all_gather(gain_one, "fsdp", axis=0, tiled=True),
        lax.all_gather(shift_one, "fsdp", axis=0, tiled=True),
        lax.all_gather(w_up, "fsdp", axis=0, tiled=True),
        lax.all_gather(bias_up, "fsdp", axis=0, tiled=True),
        lax.all_gather(w_down, "fsdp", axis=0, tiled=True),
        lax.all_gather(bias_down, "fsdp", axis=0, tiled=True),
        lax.all_gather(gain_two, "fsdp", axis=0, tiled=True),
        lax.all_gather(shift_two, "fsdp", axis=0, tiled=True),
    )
    f32 = jnp.float32
    bf16 = jnp.bfloat16
    tokens = hidden[0]
    tok_rows = tokens.shape[0]
    model_width = tokens.shape[1]
    head_count = model_width // HEAD
    seq_rows = tok_rows * lax.axis_size("ctx")
    key_span = 4 * tok_rows
    block_total = seq_rows // key_span
    doc_ids = segment_ids[0]
    own_ids = lax.dynamic_slice_in_dim(doc_ids, lax.axis_index("ctx") * tok_rows, tok_rows)
    mixed_rows = jnp.dot(tokens, w_qkv, preferred_element_type=f32)
    query_rows = (mixed_rows[:, :model_width] + bias_query.astype(f32)).astype(bf16)
    key_value = jnp.concatenate(
        [
            mixed_rows[:, model_width : 2 * model_width],
            mixed_rows[:, 2 * model_width :] + bias_value.astype(f32),
        ],
        axis=1,
    ).astype(bf16)
    all_kv = lax.all_gather(key_value, "ctx", axis=0, tiled=True)
    query_heads = query_rows.reshape(tok_rows, head_count, HEAD)

    def key_block(block_index):
        kv_piece = lax.dynamic_slice_in_dim(all_kv, block_index * key_span, key_span, 0)
        key_ids = lax.dynamic_slice_in_dim(doc_ids, block_index * key_span, key_span)
        return (
            kv_piece[:, :model_width].reshape(key_span, head_count, HEAD),
            kv_piece[:, model_width:].reshape(key_span, head_count, HEAD),
            key_ids,
        )

    def forward_step(running, block_index):
        level_run, total_run, sum_run = running
        key_heads, value_heads, key_ids = key_block(block_index)
        allowed = (own_ids[:, None] == key_ids[None, :])[None]
        scores = jnp.where(allowed, head_scores(query_heads, key_heads), NEGATIVE)
        level_new = jnp.maximum(level_run, jnp.ceil(jnp.max(scores, axis=-1) * LOG2_E))
        rescale = jnp.exp(LOG_TWO * (level_run - level_new))
        unnorm = jnp.where(allowed, jnp.exp(scores - (LOG_TWO * level_new)[..., None]), 0.0)
        total_new = total_run * rescale + jnp.sum(unnorm, axis=-1)
        sum_new = sum_run * jnp.transpose(rescale)[:, :, None] + jnp.einsum(
            "hqk,khd->qhd", unnorm.astype(bf16), value_heads, preferred_element_type=f32
        )
        return (level_new, total_new, sum_new)

    start_state = (
        jnp.full((head_count, tok_rows), NEGATIVE, f32),
        jnp.zeros((head_count, tok_rows), f32),
        jnp.zeros((tok_rows, head_count, HEAD), f32),
    )
    level_end, row_total, raw_sum = sweep(block_total, forward_step, start_state)
    row_shift = LOG_TWO * level_end
    att_sum = raw_sum / jnp.transpose(row_total)[:, :, None]
    attended = att_sum.reshape(tok_rows, model_width).astype(bf16)
    branch = jnp.dot(attended, w_out, preferred_element_type=f32) + bias_out.astype(f32)
    normed_one, norm_one, scale_one = norm_forward(
        tokens.astype(f32) + branch, gain_one.astype(f32), shift_one.astype(f32)
    )
    normed_b = normed_one.astype(bf16)
    up_rows = jnp.dot(normed_b, w_up, preferred_element_type=f32) + bias_up.astype(f32)
    active, gelu_back = jax.vjp(lambda pre_act: jax.nn.gelu(pre_act, approximate=False), up_rows)
    active_b = active.astype(bf16)
    second = (
        normed_one + jnp.dot(active_b, w_down, preferred_element_type=f32) + bias_down.astype(f32)
    )
    result, norm_two, scale_two = norm_forward(second, gain_two.astype(f32), shift_two.astype(f32))
    grad_second, grad_gain_two, grad_shift_two = norm_backward(
        out_grad[0].astype(f32), norm_two, scale_two, gain_two.astype(f32)
    )
    grad_ffn = grad_second.astype(bf16)
    grad_bias_down = column_sums(grad_ffn)
    grad_w_down = jnp.dot(active_b.T, grad_ffn, preferred_element_type=f32)
    grad_active = jnp.dot(grad_ffn, w_down.T, preferred_element_type=f32)
    grad_up = gelu_back(grad_active)[0].astype(bf16)
    grad_bias_up = column_sums(grad_up)
    grad_w_up = jnp.dot(normed_b.T, grad_up, preferred_element_type=f32)
    grad_normed = grad_second + jnp.dot(grad_up, w_up.T, preferred_element_type=f32)
    grad_first, grad_gain_one, grad_shift_one = norm_backward(
        grad_normed, norm_one, scale_one, gain_one.astype(f32)
    )
    grad_branch = grad_first.astype(bf16)
    grad_bias_out = column_sums(grad_branch)
    grad_w_out = jnp.dot(attended.T, grad_branch, preferred_element_type=f32)
    grad_attended = jnp.dot(grad_branch, w_out.T, preferred_element_type=f32).astype(bf16)
    grad_att_f32 = grad_attended.reshape(tok_rows, head_count, HEAD).astype(f32)
    delta = jnp.einsum("qhd,qhd->hq", grad_att_f32, att_sum)
    delta_ratio = delta / row_total
    grad_scaled = (grad_att_f32 / jnp.transpose(row_total)[:, :, None]).astype(bf16)
    zero_query = jnp.zeros((tok_rows, head_count, HEAD), f32)

    def full_step(running, block_index):
        grad_query, grad_kv = running
        key_heads, value_heads, key_ids = key_block(block_index)
        allowed = (own_ids[:, None] == key_ids[None, :])[None]
        unnorm_b, grad_scores = local_grads(
            head_scores(query_heads, key_heads),
            allowed,
            row_shift,
            delta_ratio,
            grad_scaled,
            value_heads,
        )
        grad_query = (
            grad_query
            + jnp.einsum("hqk,khd->qhd", grad_scores, key_heads, preferred_element_type=f32) * 0.125
        )
        grad_keys = (
            jnp.einsum("hqk,qhd->khd", grad_scores, query_heads, preferred_element_type=f32) * 0.125
        )
        grad_values = jnp.einsum("hqk,qhd->khd", unnorm_b, grad_scaled, preferred_element_type=f32)
        both_grads = jnp.concatenate(
            [grad_keys.reshape(key_span, model_width), grad_values.reshape(key_span, model_width)],
            axis=1,
        )
        grad_kv = lax.dynamic_update_slice_in_dim(grad_kv, both_grads, block_index * key_span, 0)
        return (grad_query, grad_kv)

    start_full = (zero_query, jnp.zeros((seq_rows, 2 * model_width), f32))
    grad_query, grad_kv = sweep(block_total, full_step, start_full)
    own_kv = lax.psum_scatter(grad_kv, "ctx", scatter_dimension=0, tiled=True)
    grad_query_b = grad_query.reshape(tok_rows, model_width).astype(bf16)
    grad_kv_b = own_kv.astype(bf16)
    grad_mixed = jnp.concatenate([grad_query_b, grad_kv_b], axis=1)
    grad_tokens = grad_first + jnp.dot(grad_mixed, w_qkv.T, preferred_element_type=f32)
    grad_w_qkv = jnp.dot(tokens.T, grad_mixed, preferred_element_type=f32)
    grad_bias_query = column_sums(grad_query_b)
    grad_bias_value = column_sums(grad_kv_b[:, model_width:])
    shares = (
        lax.psum_scatter(grad_w_qkv, ("ctx", "fsdp"), scatter_dimension=0, tiled=True),
        lax.psum_scatter(grad_bias_query, ("ctx", "fsdp"), scatter_dimension=0, tiled=True),
        lax.psum_scatter(grad_bias_value, ("ctx", "fsdp"), scatter_dimension=0, tiled=True),
        lax.psum_scatter(grad_w_out, ("ctx", "fsdp"), scatter_dimension=0, tiled=True),
        lax.psum_scatter(grad_bias_out, ("ctx", "fsdp"), scatter_dimension=0, tiled=True),
        lax.psum_scatter(grad_gain_one, ("ctx", "fsdp"), scatter_dimension=0, tiled=True),
        lax.psum_scatter(grad_shift_one, ("ctx", "fsdp"), scatter_dimension=0, tiled=True),
        lax.psum_scatter(grad_w_up, ("ctx", "fsdp"), scatter_dimension=0, tiled=True),
        lax.psum_scatter(grad_bias_up, ("ctx", "fsdp"), scatter_dimension=0, tiled=True),
        lax.psum_scatter(grad_w_down, ("ctx", "fsdp"), scatter_dimension=0, tiled=True),
        lax.psum_scatter(grad_bias_down, ("ctx", "fsdp"), scatter_dimension=0, tiled=True),
        lax.psum_scatter(grad_gain_two, ("ctx", "fsdp"), scatter_dimension=0, tiled=True),
        lax.psum_scatter(grad_shift_two, ("ctx", "fsdp"), scatter_dimension=0, tiled=True),
    )
    summed = (
        lax.psum(shares[0].astype(jnp.bfloat16), "seq").astype(jnp.float32),
        lax.psum(shares[1].astype(jnp.bfloat16), "seq").astype(jnp.float32),
        lax.psum(shares[2].astype(jnp.bfloat16), "seq").astype(jnp.float32),
        lax.psum(shares[3].astype(jnp.bfloat16), "seq").astype(jnp.float32),
        lax.psum(shares[4].astype(jnp.bfloat16), "seq").astype(jnp.float32),
        lax.psum(shares[5].astype(jnp.bfloat16), "seq").astype(jnp.float32),
        lax.psum(shares[6].astype(jnp.bfloat16), "seq").astype(jnp.float32),
        lax.psum(shares[7].astype(jnp.bfloat16), "seq").astype(jnp.float32),
        lax.psum(shares[8].astype(jnp.bfloat16), "seq").astype(jnp.float32),
        lax.psum(shares[9].astype(jnp.bfloat16), "seq").astype(jnp.float32),
        lax.psum(shares[10].astype(jnp.bfloat16), "seq").astype(jnp.float32),
        lax.psum(shares[11].astype(jnp.bfloat16), "seq").astype(jnp.float32),
        lax.psum(shares[12].astype(jnp.bfloat16), "seq").astype(jnp.float32),
    )
    return (
        result.astype(bf16)[None],
        grad_tokens[None],
        summed[0],
        summed[1],
        summed[2],
        summed[3],
        summed[4],
        summed[5],
        summed[6],
        summed[7],
        summed[8],
        summed[9],
        summed[10],
        summed[11],
        summed[12],
    )


def solution(mesh):
    return jax.shard_map(
        on_device,
        mesh=mesh,
        in_specs=(
            P(("seq", "fsdp"), "ctx", None),
            P(("seq", "fsdp"), None),
            P(("seq", "fsdp"), "ctx", None),
            P("fsdp", None),
            P("fsdp"),
            P("fsdp"),
            P("fsdp", None),
            P("fsdp"),
            P("fsdp"),
            P("fsdp"),
            P("fsdp", None),
            P("fsdp"),
            P("fsdp", None),
            P("fsdp"),
            P("fsdp"),
            P("fsdp"),
        ),
        out_specs=(
            P(("seq", "fsdp"), "ctx", None),
            P(("seq", "fsdp"), "ctx", None),
            P(("ctx", "fsdp"), None),
            P(("ctx", "fsdp")),
            P(("ctx", "fsdp")),
            P(("ctx", "fsdp"), None),
            P(("ctx", "fsdp")),
            P(("ctx", "fsdp")),
            P(("ctx", "fsdp")),
            P(("ctx", "fsdp"), None),
            P(("ctx", "fsdp")),
            P(("ctx", "fsdp"), None),
            P(("ctx", "fsdp")),
            P(("ctx", "fsdp")),
            P(("ctx", "fsdp")),
        ),
        check_vma=False,
    )
```

profile of v0, /device:TPU:0, one launch (start us, length us, event | category | flops | bytes accessed | tf_op | source)
XLA Modules:
  0.0 833.4 jit_solution(2394509525906658295)
XLA Ops:
  8.7 2.0 all-gather.1
  11.3 1.8 all-gather
  13.2 11.8 %all-gather.15.cloned.1.call-done = bf16[768,2304]{1,0:T(8,128)(2,1)} async-done(((bf16[384,2304]{1,0:T(8,128)(2,1)}), bf16[768,2304]{1,0:T(8,128)(2,1)}) %all-gather.15.cloned.1.call-update) | async-done | bytes 3538960 | tf_op jit(solution)/shard_map/all_gather | solution.py:96
  25.0 2.7 fusion.54
  30.9 1.8 all-gather.2
  32.8 1.8 all-gather.3
  34.7 1.8 all-gather.4
  36.6 1.8 all-gather.6
  38.5 1.8 all-gather.7
  40.4 1.8 all-gather.8
  42.3 1.8 all-gather.5
  44.3 55.3 %all-gather.17.cloned.1.call-done = bf16[1280,1536]{1,0:T(8,128)(2,1)} async-done(((bf16[160,1536]{1,0:T(8,128)(2,1)}), bf16[1280,1536]{1,0:T(8,128)(2,1)}) %all-gather.17.cloned.1.call-update) | async-done | bytes 3932176 | tf_op jit(solution)/shard_map/all_gather | solution.py:130
  99.5 6.2 copy.43
  105.7 15.4 %while.28 = (s32[]{:T(128)}, f32[12,160]{1,0:T(8,128)S(1)}, f32[12,160]{1,0:T(8,128)S(1)}, f32[160,12,64]{0,2,1:T(8,128)S(1)}, s32[160]{0:T(256)S(1)}, /*index=5...) while((s32[]{:T(128)}, f32[12,160]{1,0:T(8,128)S(1)}, ...), condition=%wide.region_3.4_spmd.clone, body=%wide.region_0.3_spmd.clone.sunk | while | flops 331039360 | bytes 22429036 | solution.py:51
  107.2 1.8 fusion.132
  110.1 1.7 fusion.137
  111.8 1.7 fusion.135
  114.9 1.7 fusion.132
  117.8 1.7 fusion.137
  119.4 1.7 fusion.135
  121.3 2.1 fusion.74
  124.3 1.7 all-gather.21.cloned.1.call-done
  126.0 8.0 multiply_convert_fusion
  134.0 9.0 %all-gather.23.cloned.1.call-done = bf16[3072,768]{1,0:T(8,128)(2,1)} async-done(((bf16[1536,768]{1,0:T(8,128)(2,1)}), bf16[3072,768]{1,0:T(8,128)(2,1)}) %all-gather.23.cloned.1.call-update) | async-done | bytes 4718608 | tf_op jit(solution)/shard_map/all_gather | solution.py:105
  143.0 3.6 fusion.75
  147.7 1.5 convert_reduce_fusion.4
  149.3 2.5 convert_reduce_fusion
  151.8 2.4 multiply_reduce_fusion
  154.2 1.6 convert_reduce_fusion.5
  158.2 1.4 fusion.38
  161.8 4.2 broadcast_in_dim.44.clone
  166.0 46.0 %while.29 = (s32[]{:T(128)}, f32[160,12,64]{0,2,1:T(8,128)S(1)}, f32[1280,1536]{1,0:T(8,128)}, s32[2]{0:T(128)}, bf16[1280,1536]{0,1:T(8,128)(2,1)}, /*index=5*/...) while((s32[]{:T(128)}, f32[160,12,64]{0,2,1:T(8,128)S(1)}, ...), condition=%wide.region_13.14_spmd.clone, body=%wide.region_12.13_spmd.clone.sunk | while | flops 800665600 | bytes 58860440 | solution.py:51
  169.4 1.7 fusion.148
  172.0 2.1 fusion.150
  177.1 2.1 pad_maximum_fusion.6
  179.2 5.5 copy.80
  184.7 4.3 constant_dynamic-update-slice_fusion.2
  192.4 1.7 fusion.148
  195.0 2.1 fusion.150
  197.1 1.3 fusion.152
  200.1 2.1 pad_maximum_fusion.6
  202.2 5.5 copy.80
  207.7 4.3 constant_dynamic-update-slice_fusion.2
  213.0 1.9 fusion.58
  215.6 6.5 fusion.67
  223.2 5.1 fusion.61
  228.6 125.0 %reduce-scatter.16.cloned.1.call-done = f32[160,1536]{1,0:T(8,128)} async-done(((f32[1280,1536]{1,0:T(8,128)}), f32[160,1536]{1,0:T(8,128)}) %reduce-scatter.16.cloned.1.call-update) | async-done | bytes 983056
  353.6 1.5 copy.56
  355.1 3.9 convolution_bitcast_fusion
  359.0 8.1 copy.57
  367.2 52.5 %reduce-scatter.10.cloned.1.call-done = f32[48,768]{1,0:T(8,128)} async-done(((f32[768,768]{1,0:T(8,128)}), f32[48,768]{1,0:T(8,128)}) %reduce-scatter.10.cloned.1.call-update) | async-done | bytes 147472 | tf_op jit(solution)/shard_map/reduce_scatter | solution.py:242
  419.7 1.6 convert_element_type.223
  421.2 112.7 %reduce-scatter.12.cloned.1.call-done = f32[48,3072]{1,0:T(8,128)} async-done(((f32[768,3072]{1,0:T(8,128)}), f32[48,3072]{1,0:T(8,128)}) %reduce-scatter.12.cloned.1.call-update) | async-done | bytes 589840 | tf_op jit(solution)/shard_map/reduce_scatter | solution.py:246
  533.9 1.8 convert_element_type.232
  535.8 113.1 %reduce-scatter.14.cloned.1.call-done = f32[192,768]{1,0:T(8,128)} async-done(((f32[3072,768]{1,0:T(8,128)}), f32[192,768]{1,0:T(8,128)}) %reduce-scatter.14.cloned.1.call-update) | async-done | bytes 589840 | tf_op jit(solution)/shard_map/reduce_scatter | solution.py:248
  648.9 1.8 convert_element_type.237
  650.7 91.6 %reduce-scatter.18.cloned.1.call-done = f32[48,2304]{1,0:T(8,128)} async-done(((f32[768,2304]{1,0:T(8,128)}), f32[48,2304]{1,0:T(8,128)}) %reduce-scatter.18.cloned.1.call-update) | async-done | bytes 442384
  742.3 2.1 copy.58
  746.7 59.4 %all-reduce.9 = (bf16[768]{0:T(1024)(128)(2,1)S(1)}, bf16[768]{0:T(1024)(128)(2,1)S(1)}, bf16[768]{0:T(1024)(128)(2,1)S(1)}, bf16[768]{0:T(1024)(128)(2,1)S(1)},...) all-reduce(f32[768]{0:T(1024)S(1)} %reduce_sum.173, ...), channel_id=4, replica_groups=mesh['seq'=2,'ctx'=8,'fsdp'=2] {'ctx','fsdp'}, use_global_device_ids=true, to_apply=%region_18.19.clone | all-reduce | flops 9216 | bytes 55296
  806.8 5.0 all-reduce.10
  816.4 4.1 fusion.36
  820.5 2.1 copy.46
  822.6 1.6 convert_element_type.224
  824.2 1.8 convert_element_type.233
  (227 shorter events, 38.1 us)
Async XLA Ops:
  7.2 17.8 %copy-start.10 = (bf16[1,160,768]{2,1,0:T(8,128)(2,1)S(1)}, bf16[1,160,768]{2,1,0:T(8,128)(2,1)}, u32[]{:S(2)}) copy-start(bf16[1,160,768]{2,1,0:T(8,128)(2,1)} %param.20) | copy-start | bytes 737284
  7.2 17.8 %all-gather.15.cloned.1.call-start = ((), (), s32[]{:S(2)}) async-start(), calls=%async_computation.5 | async-start | bytes 5308416 | tf_op jit(solution)/shard_map/all_gather | solution.py:96
  7.9 91.6 %all-gather.17.cloned.1.call-start = ((), (), s32[]{:S(2)}) async-start(), calls=%async_computation.6 | async-start | bytes 4423680 | tf_op jit(solution)/shard_map/all_gather | solution.py:130
  28.7 92.6 %all-gather.19.cloned.1.call-start = ((), (), s32[]{:S(2)}) async-start(), calls=%async_computation.7 | async-start | bytes 1769472 | tf_op jit(solution)/shard_map/all_gather | solution.py:99
  29.4 1.4 copy-start.31
  29.5 1.5 copy-start.33
  29.5 3.3 copy-start.34
  29.5 5.2 copy-start.35
  29.5 7.1 copy-start.36
  29.5 9.0 %copy-start.37 = (bf16[384]{0:T(512)(128)(2,1)S(1)}, bf16[384]{0:T(512)(128)(2,1)}, u32[]{:S(2)}) copy-start(bf16[384]{0:T(512)(128)(2,1)} %param.34) | copy-start | bytes 2308
  29.5 10.8 %copy-start.38 = (bf16[384]{0:T(512)(128)(2,1)S(1)}, bf16[384]{0:T(512)(128)(2,1)}, u32[]{:S(2)}) copy-start(bf16[384]{0:T(512)(128)(2,1)} %param.35) | copy-start | bytes 2308
  29.5 12.7 %copy-start.32 = (bf16[1536]{0:T(1024)(128)(2,1)S(1)}, bf16[1536]{0:T(1024)(128)(2,1)}, u32[]{:S(2)}) copy-start(bf16[1536]{0:T(1024)(128)(2,1)} %param.31) | copy-start | bytes 9220
  29.5 96.5 %all-gather.21.cloned.1.call-start = ((), (), s32[]{:S(2)}) async-start(), calls=%async_computation.8 | async-start | bytes 7077888 | tf_op jit(solution)/shard_map/all_gather | solution.py:103
  30.1 112.9 %all-gather.23.cloned.1.call-start = ((), (), s32[]{:S(2)}) async-start(), calls=%async_computation.9 | async-start | bytes 7077888 | tf_op jit(solution)/shard_map/all_gather | solution.py:105
  30.7 322.9 %reduce-scatter.16.cloned.1.call-start = ((), (), s32[]{:S(2)}) async-start(), calls=%async_computation.13 | async-start | bytes 8847360
  34.7 117.1 %copy-start.15 = (f32[768]{0:T(1024)}, f32[768]{0:T(1024)S(1)}, u32[]{:S(2)}) copy-start(f32[768]{0:T(1024)S(1)} %reshape.196) | copy-start | bytes 9220
  36.6 106.5 %copy-start.17 = (f32[768]{0:T(1024)}, f32[768]{0:T(1024)S(1)}, u32[]{:S(2)}) copy-start(f32[768]{0:T(1024)S(1)} %reshape.197) | copy-start | bytes 9220
  121.1 2.5 copy-start.7
  121.1 2.5 copy-start.14
  121.1 2.5 copy-start.19
  121.2 12.8 %copy-start.5 = (bf16[160,12,64]{0,2,1:T(8,128)(2,1)}, bf16[160,12,64]{0,2,1:T(8,128)(2,1)S(1)}, u32[]{:S(2)}) copy-start(bf16[160,12,64]{0,2,1:T(8,128)(2,1)S(1)} %fusion.51) | copy-start | bytes 737284
  123.4 28.3 %copy-start.20 = (f32[160]{0:T(256)}, f32[160]{0:T(256)S(1)}, u32[]{:S(2)}) copy-start(f32[160]{0:T(256)S(1)} %broadcast_multiply_fusion.7) | copy-start | bytes 1924
  123.7 28.1 %copy-start.22 = (f32[160]{0:T(256)}, f32[160]{0:T(256)S(1)}, u32[]{:S(2)}) copy-start(f32[160]{0:T(256)S(1)} %add_rsqrt_fusion.1) | copy-start | bytes 1924
  143.0 6.2 slice-start.2
  143.0 3.8 copy-start.8
  143.0 6.2 slice-start.3
  143.0 6.2 copy-start.41
  146.6 2.6 copy-start.40
  147.7 4.1 slice-start
  149.2 2.6 copy-start.1
  149.2 2.5 slice-start.1
  151.8 2.5 copy-start.3
  154.2 1.6 copy-start
  158.2 2.1 copy-start.4
  161.8 4.2 copy-start.12
  171.1 0.9 copy-start.29
  194.1 0.9 copy-start.29
  212.0 1.0 copy-start.6
  212.0 207.6 %reduce-scatter.10.cloned.1.call-start = ((), (), s32[]{:S(2)}) async-start(), calls=%async_computation.10 | async-start | bytes 2506752 | tf_op jit(solution)/shard_map/reduce_scatter | solution.py:242
  214.9 0.7 copy-start.16
  214.9 0.7 copy-start.18
  214.9 0.7 copy-start.21
  214.9 0.7 copy-start.23
  214.9 319.0 %reduce-scatter.12.cloned.1.call-start = ((), (), s32[]{:S(2)}) async-start(), calls=%async_computation.11 | async-start | bytes 10027008 | tf_op jit(solution)/shard_map/reduce_scatter | solution.py:246
  222.2 1.0 copy-start.2
  222.2 426.7 %reduce-scatter.14.cloned.1.call-start = ((), (), s32[]{:S(2)}) async-start(), calls=%async_computation.12 | async-start | bytes 10027008 | tf_op jit(solution)/shard_map/reduce_scatter | solution.py:248
  228.3 126.7 %copy-start.11 = (bf16[1,160,768]{2,1,0:T(8,128)(2,1)S(1)}, bf16[1,160,768]{2,1,0:T(8,128)(2,1)}, u32[]{:S(2)}) copy-start(bf16[1,160,768]{2,1,0:T(8,128)(2,1)} %param.20) | copy-start | bytes 737284
  228.3 514.0 %reduce-scatter.18.cloned.1.call-start = ((), (), s32[]{:S(2)}) async-start(), calls=%async_computation.14 | async-start | bytes 7520256
  367.1 453.4 %all-reduce.14.cloned.1.call-start = ((), (), s32[]{:S(2)}) async-start(), calls=%async_computation.15 | async-start | bytes 2506752 | tf_op jit(solution)/shard_map/psum | solution.py:254
  421.2 323.2 %copy-start.39 = (u32[32]{0:T(128)S(1)}, u32[32]{0:T(128)}, u32[]{:S(2)}) copy-start(u32[32]{0:T(128)} %constant.141) | copy-start | bytes 388
  421.2 325.1 %copy-start.9 = (bf16[1,160,768]{2,1,0:T(8,128)(2,1)S(1)}, bf16[1,160,768]{2,1,0:T(8,128)(2,1)}, u32[]{:S(2)}) copy-start(bf16[1,160,768]{2,1,0:T(8,128)(2,1)} %param.22) | copy-start | bytes 737284
  535.7 210.9 %copy-start.24 = (f32[768]{0:T(1024)S(1)}, f32[768]{0:T(1024)}, u32[]{:S(2)}) copy-start(f32[768]{0:T(1024)} %get-tuple-element.298) | copy-start | bytes 9220
  535.7 210.9 %copy-start.25 = (f32[768]{0:T(1024)S(1)}, f32[768]{0:T(1024)}, u32[]{:S(2)}) copy-start(f32[768]{0:T(1024)} %get-tuple-element.303) | copy-start | bytes 9220
  535.8 210.9 %copy-start.26 = (f32[768]{0:T(1024)S(1)}, f32[768]{0:T(1024)}, u32[]{:S(2)}) copy-start(f32[768]{0:T(1024)} %get-tuple-element.300) | copy-start | bytes 9220
  535.8 210.9 %copy-start.27 = (f32[768]{0:T(1024)S(1)}, f32[768]{0:T(1024)}, u32[]{:S(2)}) copy-start(f32[768]{0:T(1024)} %get-tuple-element.369) | copy-start | bytes 9220
  535.8 210.9 %copy-start.28 = (f32[768]{0:T(1024)S(1)}, f32[768]{0:T(1024)}, u32[]{:S(2)}) copy-start(f32[768]{0:T(1024)} %get-tuple-element.371) | copy-start | bytes 9220
  535.8 210.9 %copy-start.30 = (f32[3072]{0:T(1024)S(1)}, f32[3072]{0:T(1024)}, u32[]{:S(2)}) copy-start(f32[3072]{0:T(1024)} %get-tuple-element.392) | copy-start | bytes 36868
  820.5 5.5 copy-start.13
Sparse Core Ops, SparseCore 0:
  9.5 15.4 all-gather.14
  28.8 70.6 all-gather.16
  101.1 7.8 all-gather.18
  110.3 15.6 all-gather.20
  127.4 15.6 all-gather.22
  212.2 141.3 reduce-scatter.15
  357.3 62.2 reduce-scatter.9
  423.8 110.1 reduce-scatter.11
  538.0 110.8 reduce-scatter.13
  652.8 89.4 reduce-scatter.17
  746.0 44.3 all-reduce.13
where the time goes:
time: 835 us; the launch traced here: 833 us
  waiting for transfers between devices  575 us (69%)
  blocking collectives  81 us (10%)
  local copies, waits for them, and re-layouts  63 us (8%)
  matrix products  61.6 us (7%)
  other arithmetic  33.1 us (4%)
  between operations  15.9 us (2%)
    unnamed x13, waiting for transfers between devices  219 us
    reduce_scatter x1, waiting for transfers between devices, on_device(): lax.psum_scatter(grad_w_down, ('ctx', 'fsdp'), scatter_dimension=0, tiled...  113 us
    reduce_scatter x1, waiting for transfers between devices, on_device(): lax.psum_scatter(grad_w_up, ('ctx', 'fsdp'), scatter_dimension=0, tiled=T...  113 us
    unnamed x1, blocking collectives  59.4 us
    all_gather x1, waiting for transfers between devices, on_device(): all_kv = lax.all_gather(key_value, 'ctx', axis=0, tiled=True)  55.3 us
    reduce_scatter x1, waiting for transfers between devices, on_device(): lax.psum_scatter(grad_w_out, ('ctx', 'fsdp'), scatter_dimension=0, tiled=...  52.5 us
    unnamed x114, local copies, waits for them, and re-layouts  25 us
    dynamic_update_slice x4, local copies, waits for them, and re-layouts, full_step(): lax.dynamic_update_slice_in_dim(grad_kv, both_grads, block_index * key_sp...  19.6 us
  transfers between devices with their start and end apart: 11, of which 9 were waited for; matrix products, arithmetic and copies ran while one was open for 9% of the time, Pallas kernels for 0%

commit v1 on v0

--- a/solution.py
+++ b/solution.py
@@ -1,6 +1,10 @@
+import functools
+
 import jax
 import jax.numpy as jnp
 from jax import lax
+from jax.experimental import pallas as pl
+from jax.experimental.pallas import tpu as pltpu
 from jax.sharding import PartitionSpec as P
 
 HEAD = 64
@@ -284,9 +288,500 @@
     )
 
 
+MESH_ID = pl.DeviceIdType.MESH
+LINE = 4
+
+
+def remote(src, dst, send, recv, target):
+    return pltpu.make_async_remote_copy(
+        src_ref=src,
+        dst_ref=dst,
+        send_sem=send,
+        recv_sem=recv,
+        device_id=target,
+        device_id_type=MESH_ID,
+    )
+
+
+def weight_grad_kernel(dims, *refs):
+    count = len(dims)
+    a_refs, b_refs, vec_ref = refs[:count], refs[count : 2 * count], refs[2 * count]
+    outs = refs[2 * count + 1 : 3 * count + 1]
+    vec_out = refs[3 * count + 1]
+    rest = refs[3 * count + 2 :]
+    units = count + 1
+    parts, from_core = rest[:units], rest[units : 2 * units]
+    from_pair, from_low = rest[2 * units : 3 * units], rest[3 * units : 4 * units]
+    from_high = rest[4 * units : 5 * units]
+    vec_seq = rest[5 * units]
+    sems = rest[5 * units + 1 :]
+    core_out, core_in, pair_out, pair_in, low_out, low_in, high_out, high_in, seq_out, seq_in = sems
+    place = lax.axis_index("ctx")
+    core = lax.axis_index("fsdp")
+    group = lax.axis_index("seq")
+    line = place // 2
+    side = place % 2
+    to_core = {"fsdp": 1 - core}
+    to_pair = {"ctx": place + 1 - 2 * side}
+    to_seq = {"seq": 1 - group}
+    to_up = {"ctx": lax.rem(place + 2, 2 * LINE)}
+    to_down = {"ctx": lax.rem(place + 2 * LINE - 2, 2 * LINE)}
+    has_low, has_high = line > 0, line < LINE - 1
+
+    barrier = pltpu.get_barrier_semaphore()
+    for target in (to_core, to_pair, to_seq):
+        pl.semaphore_signal(barrier, inc=1, device_id=target, device_id_type=MESH_ID)
+
+    @pl.when(has_high)
+    def _():
+        pl.semaphore_signal(barrier, inc=1, device_id=to_up, device_id_type=MESH_ID)
+
+    @pl.when(has_low)
+    def _():
+        pl.semaphore_signal(barrier, inc=1, device_id=to_down, device_id_type=MESH_ID)
+
+    pl.semaphore_wait(barrier, 3 + has_high.astype(jnp.int32) + has_low.astype(jnp.int32))
+
+    def core_copy(u):
+        return remote(parts[u].at[1 - core], from_core[u], core_out.at[u], core_in.at[u], to_core)
+
+    def pair_copy(u, k):
+        return remote(
+            parts[u].at[core, k, 1 - side],
+            from_pair[u].at[k],
+            pair_out.at[u, k],
+            pair_in.at[u, k],
+            to_pair,
+        )
+
+    def up_copy(u, k):
+        return remote(
+            parts[u].at[core, k, side],
+            from_low[u].at[k - 1],
+            low_out.at[u, k - 1],
+            low_in.at[u, k - 1],
+            to_up,
+        )
+
+    def down_copy(u, k):
+        return remote(
+            parts[u].at[core, k, side],
+            from_high[u].at[k],
+            high_out.at[u, k],
+            high_in.at[u, k],
+            to_down,
+        )
+
+    def seq_copy(u):
+        if u == count:
+            return remote(parts[u].at[core, line, side], vec_seq, seq_out.at[u], seq_in.at[u], to_seq)
+        rows, columns, wide = dims[u]
+        if wide:
+            where = outs[u].at[:, pl.ds(pl.multiple_of(group * columns, 128), columns)]
+        else:
+            where = outs[u].at[pl.ds(pl.multiple_of(group * rows, 16), rows)]
+        return remote(parts[u].at[core, line, side], where, seq_out.at[u], seq_in.at[u], to_seq)
+
+    def multiply(u):
+        if u == count:
+            parts[u][...] = vec_ref[...]
+        else:
+            rows, columns, _ = dims[u]
+            step = 384
+            for first in range(0, columns, step):
+                product = lax.dot_general(
+                    a_refs[u][...],
+                    b_refs[u][:, first : first + step],
+                    (((0,), (0,)), ((), ())),
+                    preferred_element_type=jnp.float32,
+                ).astype(jnp.bfloat16)
+                for j in range(4 * LINE):
+                    parts[u][j % 2, j // 4, (j // 2) % 2, :, first : first + step] = product[
+                        j * rows : (j + 1) * rows
+                    ]
+        core_copy(u).start()
+
+    def add_core(u):
+        core_copy(u).wait_recv()
+        for k in (3, 0, 2, 1):
+            parts[u][core, k, 1 - side] += from_core[u][k, 1 - side]
+            pair_copy(u, k).start()
+        for k in range(LINE):
+            parts[u][core, k, side] += from_core[u][k, side]
+
+    def add_pair(u):
+        for k in (3, 0, 2, 1):
+            pair_copy(u, k).wait_recv()
+            parts[u][core, k, side] += from_pair[u][k]
+
+        @pl.when(line == 0)
+        def _():
+            for k in range(LINE - 1, 0, -1):
+                up_copy(u, k).start()
+
+        @pl.when(line == LINE - 1)
+        def _():
+            for k in range(LINE - 1):
+                down_copy(u, k).start()
+
+    def pass_up(u, k):
+        up_copy(u, k).wait_recv()
+        parts[u][core, k, side] += from_low[u][k - 1]
+        up_copy(u, k).start()
+
+    def pass_down(u, k):
+        down_copy(u, k).wait_recv()
+        parts[u][core, k, side] += from_high[u][k]
+        down_copy(u, k).start()
+
+    def first_hop(u):
+        @pl.when(line == 1)
+        def _():
+            pass_up(u, 3)
+            pass_up(u, 2)
+
+        @pl.when(line == 2)
+        def _():
+            pass_down(u, 0)
+            pass_down(u, 1)
+
+    def second_hop(u):
+        @pl.when(line == 2)
+        def _():
+            pass_up(u, 3)
+
+        @pl.when(line == 1)
+        def _():
+            pass_down(u, 0)
+
+    def finish(u):
+        for k in range(LINE):
+
+            @pl.when(line == k)
+            def _(k=k):
+                if k > 0:
+                    up_copy(u, k).wait_recv()
+                    parts[u][core, k, side] += from_low[u][k - 1]
+                if k < LINE - 1:
+                    down_copy(u, k).wait_recv()
+                    parts[u][core, k, side] += from_high[u][k]
+
+        seq_copy(u).start()
+        if u < count:
+            rows, columns, wide = dims[u]
+            if wide:
+                start = pl.multiple_of(group * columns, 128)
+                outs[u][:, pl.ds(start, columns)] = parts[u][core, line, side]
+            else:
+                start = pl.multiple_of(group * rows, 16)
+                outs[u][pl.ds(start, rows)] = parts[u][core, line, side]
+
+    multiply(0)
+    for u in range(units):
+        if u + 1 < units:
+            multiply(u + 1)
+        add_core(u)
+    for s in range(units + 3):
+        if s < units:
+            add_pair(s)
+        if 0 <= s - 1 < units:
+            first_hop(s - 1)
+        if 0 <= s - 2 < units:
+            second_hop(s - 2)
+        if 0 <= s - 3 < units:
+            finish(s - 3)
+    for u in range(units):
+        seq_copy(u).wait_recv()
+    vec_out[...] = parts[count][core, line, side] + vec_seq[...]
+    for u in range(units):
+        core_copy(u).wait_send()
+        seq_copy(u).wait_send()
+        for k in range(LINE):
+            pair_copy(u, k).wait_send()
+        for k in range(1, LINE):
+
+            @pl.when(line < k)
+            def _(k=k):
+                up_copy(u, k).wait_send()
+
+        for k in range(LINE - 1):
+
+            @pl.when(line > k)
+            def _(k=k):
+                down_copy(u, k).wait_send()
+
+
+def weight_grads(a_list, b_list, vec):
+    widths = [(a.shape[1], b.shape[1]) for a, b in zip(a_list, b_list)]
+    dims, shapes = [], []
+    for a_width, b_width in widths:
+        rows = a_width // (4 * LINE)
+        wide = a_width == a_list[0].shape[1]
+        dims.append((rows, b_width, wide))
+        shapes.append((rows, 2 * b_width) if wide else (2 * rows, b_width))
+    blocks = [((rows, columns), jnp.bfloat16) for rows, columns, _ in dims]
+    blocks.append(((8, 128), jnp.float32))
+    units = len(blocks)
+    scratch = []
+    for lead in ((2, LINE, 2), (LINE, 2), (LINE,), (LINE - 1,), (LINE - 1,)):
+        scratch += [pltpu.VMEM(lead + block, kind) for block, kind in blocks]
+    scratch.append(pltpu.VMEM((8, 128), jnp.float32))
+    for lead in ((), (LINE,), (LINE - 1,), (LINE - 1,), ()):
+        scratch += [pltpu.SemaphoreType.DMA((units,) + lead)] * 2
+    return pl.pallas_call(
+        functools.partial(weight_grad_kernel, dims),
+        out_shape=[jax.ShapeDtypeStruct(shape, jnp.bfloat16) for shape in shapes]
+        + [jax.ShapeDtypeStruct((8, 128), jnp.float32)],
+        in_specs=[pl.BlockSpec(memory_space=pltpu.VMEM)] * (2 * len(dims) + 1),
+        out_specs=[pl.BlockSpec(memory_space=pltpu.VMEM)] * (len(dims) + 1),
+        scratch_shapes=scratch,
+        compiler_params=pltpu.CompilerParams(
+            collective_id=0, has_side_effects=True, vmem_limit_bytes=60 << 20
+        ),
+        name="weight_grads",
+    )(*a_list, *b_list, vec)
+
+
+def block_device(
+    hidden,
+    segment_ids,
+    out_grad,
+    w_qkv,
+    bias_query,
+    bias_value,
+    w_out,
+    bias_out,
+    gain_one,
+    shift_one,
+    w_up,
+    bias_up,
+    w_down,
+    bias_down,
+    gain_two,
+    shift_two,
+):
+    (
+        w_qkv,
+        bias_query,
+        bias_value,
+        w_out,
+        bias_out,
+        gain_one,
+        shift_one,
+        w_up,
+        bias_up,
+        w_down,
+        bias_down,
+        gain_two,
+        shift_two,
+    ) = (
+        lax.all_gather(w_qkv, "fsdp", axis=0, tiled=True),
+        lax.all_gather(bias_query, "fsdp", axis=0, tiled=True),
+        lax.all_gather(bias_value, "fsdp", axis=0, tiled=True),
+        lax.all_gather(w_out, "fsdp", axis=0, tiled=True),
+        lax.all_gather(bias_out, "fsdp", axis=0, tiled=True),
+        lax.all_gather(gain_one, "fsdp", axis=0, tiled=True),
+        lax.all_gather(shift_one, "fsdp", axis=0, tiled=True),
+        lax.all_gather(w_up, "fsdp", axis=0, tiled=True),
+        lax.all_gather(bias_up, "fsdp", axis=0, tiled=True),
+        lax.all_gather(w_down, "fsdp", axis=0, tiled=True),
+        lax.all_gather(bias_down, "fsdp", axis=0, tiled=True),
+        lax.all_gather(gain_two, "fsdp", axis=0, tiled=True),
+        lax.all_gather(shift_two, "fsdp", axis=0, tiled=True),
+    )
+    f32 = jnp.float32
+    bf16 = jnp.bfloat16
+    tokens = hidden[0]
+    tok_rows = tokens.shape[0]
+    model_width = tokens.shape[1]
+    head_count = model_width // HEAD
+    seq_rows = tok_rows * lax.axis_size("ctx")
+    key_span = 4 * tok_rows
+    block_total = seq_rows // key_span
+    doc_ids = segment_ids[0]
+    own_ids = lax.dynamic_slice_in_dim(doc_ids, lax.axis_index("ctx") * tok_rows, tok_rows)
+    mixed_rows = jnp.dot(tokens, w_qkv, preferred_element_type=f32)
+    query_rows = (mixed_rows[:, :model_width] + bias_query.astype(f32)).astype(bf16)
+    key_value = jnp.concatenate(
+        [
+            mixed_rows[:, model_width : 2 * model_width],
+            mixed_rows[:, 2 * model_width :] + bias_value.astype(f32),
+        ],
+        axis=1,
+    ).astype(bf16)
+    all_kv = lax.all_gather(key_value, "ctx", axis=0, tiled=True)
+    query_heads = query_rows.reshape(tok_rows, head_count, HEAD)
+
+    def key_block(block_index):
+        kv_piece = lax.dynamic_slice_in_dim(all_kv, block_index * key_span, key_span, 0)
+        key_ids = lax.dynamic_slice_in_dim(doc_ids, block_index * key_span, key_span)
+        return (
+            kv_piece[:, :model_width].reshape(key_span, head_count, HEAD),
+            kv_piece[:, model_width:].reshape(key_span, head_count, HEAD),
+            key_ids,
+        )
+
+    def forward_step(running, block_index):
+        level_run, total_run, sum_run = running
+        key_heads, value_heads, key_ids = key_block(block_index)
+        allowed = (own_ids[:, None] == key_ids[None, :])[None]
+        scores = jnp.where(allowed, head_scores(query_heads, key_heads), NEGATIVE)
+        level_new = jnp.maximum(level_run, jnp.ceil(jnp.max(scores, axis=-1) * LOG2_E))
+        rescale = jnp.exp(LOG_TWO * (level_run - level_new))
+        unnorm = jnp.where(allowed, jnp.exp(scores - (LOG_TWO * level_new)[..., None]), 0.0)
+        total_new = total_run * rescale + jnp.sum(unnorm, axis=-1)
+        sum_new = sum_run * jnp.transpose(rescale)[:, :, None] + jnp.einsum(
+            "hqk,khd->qhd", unnorm.astype(bf16), value_heads, preferred_element_type=f32
+        )
+        return (level_new, total_new, sum_new)
+
+    start_state = (
+        jnp.full((head_count, tok_rows), NEGATIVE, f32),
+        jnp.zeros((head_count, tok_rows), f32),
+        jnp.zeros((tok_rows, head_count, HEAD), f32),
+    )
+    level_end, row_total, raw_sum = sweep(block_total, forward_step, start_state)
+    row_shift = LOG_TWO * level_end
+    att_sum = raw_sum / jnp.transpose(row_total)[:, :, None]
+    attended = att_sum.reshape(tok_rows, model_width).astype(bf16)
+    branch = jnp.dot(attended, w_out, preferred_element_type=f32) + bias_out.astype(f32)
+    normed_one, norm_one, scale_one = norm_forward(
+        tokens.astype(f32) + branch, gain_one.astype(f32), shift_one.astype(f32)
+    )
+    normed_b = normed_one.astype(bf16)
+    up_rows = jnp.dot(normed_b, w_up, preferred_element_type=f32) + bias_up.astype(f32)
+    active, gelu_back = jax.vjp(lambda pre_act: jax.nn.gelu(pre_act, approximate=False), up_rows)
+    active_b = active.astype(bf16)
+    second = (
+        normed_one + jnp.dot(active_b, w_down, preferred_element_type=f32) + bias_down.astype(f32)
+    )
+    result, norm_two, scale_two = norm_forward(second, gain_two.astype(f32), shift_two.astype(f32))
+    grad_second, grad_gain_two, grad_shift_two = norm_backward(
+        out_grad[0].astype(f32), norm_two, scale_two, gain_two.astype(f32)
+    )
+    grad_ffn = grad_second.astype(bf16)
+    grad_bias_down = column_sums(grad_ffn)
+    grad_active = jnp.dot(grad_ffn, w_down.T, preferred_element_type=f32)
+    grad_up = gelu_back(grad_active)[0].astype(bf16)
+    grad_bias_up = column_sums(grad_up)
+    grad_normed = grad_second + jnp.dot(grad_up, w_up.T, preferred_element_type=f32)
+    grad_first, grad_gain_one, grad_shift_one = norm_backward(
+        grad_normed, norm_one, scale_one, gain_one.astype(f32)
+    )
+    grad_branch = grad_first.astype(bf16)
+    grad_bias_out = column_sums(grad_branch)
+    grad_attended = jnp.dot(grad_branch, w_out.T, preferred_element_type=f32).astype(bf16)
+    grad_att_f32 = grad_attended.reshape(tok_rows, head_count, HEAD).astype(f32)
+    delta = jnp.einsum("qhd,qhd->hq", grad_att_f32, att_sum)
+    delta_ratio = delta / row_total
+    grad_scaled = (grad_att_f32 / jnp.transpose(row_total)[:, :, None]).astype(bf16)
+    zero_query = jnp.zeros((tok_rows, head_count, HEAD), f32)
+
+    def full_step(running, block_index):
+        grad_query, grad_kv = running
+        key_heads, value_heads, key_ids = key_block(block_index)
+        allowed = (own_ids[:, None] == key_ids[None, :])[None]
+        unnorm_b, grad_scores = local_grads(
+            head_scores(query_heads, key_heads),
+            allowed,
+            row_shift,
+            delta_ratio,
+            grad_scaled,
+            value_heads,
+        )
+        grad_query = (
+            grad_query
+            + jnp.einsum("hqk,khd->qhd", grad_scores, key_heads, preferred_element_type=f32) * 0.125
+        )
+        grad_keys = (
+            jnp.einsum("hqk,qhd->khd", grad_scores, query_heads, preferred_element_type=f32) * 0.125
+        )
+        grad_values = jnp.einsum("hqk,qhd->khd", unnorm_b, grad_scaled, preferred_element_type=f32)
+        both_grads = jnp.concatenate(
+            [grad_keys.reshape(key_span, model_width), grad_values.reshape(key_span, model_width)],
+            axis=1,
+        )
+        grad_kv = lax.dynamic_update_slice_in_dim(grad_kv, both_grads, block_index * key_span, 0)
+        return (grad_query, grad_kv)
+
+    start_full = (zero_query, jnp.zeros((seq_rows, 2 * model_width), f32))
+    grad_query, grad_kv = sweep(block_total, full_step, start_full)
+    own_kv = lax.psum_scatter(grad_kv, "ctx", scatter_dimension=0, tiled=True)
+    grad_query_b = grad_query.reshape(tok_rows, model_width).astype(bf16)
+    grad_kv_b = own_kv.astype(bf16)
+    grad_mixed = jnp.concatenate([grad_query_b, grad_kv_b], axis=1)
+    grad_tokens = grad_first + jnp.dot(grad_mixed, w_qkv.T, preferred_element_type=f32)
+    grad_bias_query = column_sums(grad_query_b)
+    grad_bias_value = column_sums(grad_kv_b[:, model_width:])
+    group = lax.axis_index("seq")
+    pick = active_b.reshape(tok_rows, 16, 2, active_b.shape[1] // 32)
+
+    def halves(values):
+        width = values.shape[1] // 2
+        own = lax.dynamic_slice_in_dim(values, group * width, width, 1)
+        return own, lax.dynamic_slice_in_dim(values, (1 - group) * width, width, 1)
+
+    def with_partner(own, sent):
+        return jnp.concatenate([own, lax.ppermute(sent, "seq", [(0, 1), (1, 0)])], axis=0)
+
+    def blocks_of(which):
+        return lax.dynamic_index_in_dim(pick, which, 2, False).reshape(tok_rows, -1)
+
+    a_list = [
+        with_partner(normed_b, normed_b),
+        with_partner(blocks_of(group), blocks_of(1 - group)),
+        with_partner(tokens, tokens),
+        with_partner(attended, attended),
+    ]
+    b_list = [
+        with_partner(*halves(grad_up)),
+        with_partner(grad_ffn, grad_ffn),
+        with_partner(*halves(grad_mixed)),
+        with_partner(*halves(grad_branch)),
+    ]
+    vectors = [
+        grad_bias_query,
+        grad_bias_value,
+        grad_bias_out,
+        grad_gain_one,
+        grad_shift_one,
+        grad_bias_up,
+        grad_bias_down,
+        grad_gain_two,
+        grad_shift_two,
+    ]
+    packed = jnp.concatenate([v.reshape(16, -1) for v in vectors], axis=1)
+    packed = jnp.pad(packed, ((0, 0), (0, 1024 - packed.shape[1])))
+    packed = jnp.transpose(packed.reshape(LINE, 2, 2, 8, 128), (2, 0, 1, 3, 4))
+    up_own, down_own, qkv_own, out_own, vec_own = weight_grads(a_list, b_list, packed)
+    flat = vec_own.reshape(-1)
+    summed, at = [], 0
+    for v in vectors:
+        summed.append(lax.slice_in_dim(flat, at, at + v.shape[0] // 16))
+        at += v.shape[0] // 16
+    return (
+        result.astype(bf16)[None],
+        grad_tokens[None],
+        qkv_own.astype(f32),
+        summed[0],
+        summed[1],
+        out_own.astype(f32),
+        summed[2],
+        summed[3],
+        summed[4],
+        up_own.astype(f32),
+        summed[5],
+        down_own.astype(f32),
+        summed[6],
+        summed[7],
+        summed[8],
+    )
+
+
 def solution(mesh):
+    small = (mesh.shape["seq"], mesh.shape["ctx"], mesh.shape["fsdp"]) == (2, 8, 2)
     return jax.shard_map(
-        on_device,
+        block_device if small else on_device,
         mesh=mesh,
         in_specs=(
             P(("seq", "fsdp"), "ctx", None),

time: 835 us -> 464 us (0.56)
  waiting for transfers between devices: 575 us -> 170 us
  Pallas kernels: 0 us -> 68.4 us
  blocking collectives: 81 us -> 16.6 us
  starting transfers between devices: 0.66 us -> 11 us
  other arithmetic: 33.1 us -> 43.3 us
  local copies, waits for them, and re-layouts: 63 us -> 72.2 us
    unnamed x13 -> x6, waiting for transfers between devices: 219 us -> 2.45 us
    reduce_scatter x3 -> x1, waiting for transfers between devices: 278 us -> 84.4 us  [block_device(): own_kv = lax.psum_scatter(grad_kv, 'ctx', scatter_dimension=0, tiled=True)]
    pallas_call x0 -> x1, Pallas kernels: none -> 68.4 us  [weight_grads(): pl.pallas_call(functools.partial(weight_grad_kernel, dims), out_shape=[ja...]
    unnamed x1 -> x0, blocking collectives: 59.4 us -> none
    dot_general x12 -> x8, matrix products: 44.2 us -> 27 us  [the longest x1 9.82 us: block_device(): jnp.dot(normed_b, w_up, preferred_element_type=f32) + bias_up.astype(f32)]
    unnamed x114 -> x96, local copies, waits for them, and re-layouts: 25 us -> 9.57 us
    ppermute x0 -> x8, waiting for transfers between devices: none -> 15.1 us  [with_partner(): lax.ppermute(sent, 'seq', [(0, 1), (1, 0)])]
    concatenate x1 -> x10, other arithmetic: 0.81 us -> 15.9 us  [the longest x8 13 us: with_partner(): jnp.concatenate([own, lax.ppermute(sent, 'seq', [(0, 1), (1, 0)])], axis=0)]
  transfers between devices with their start and end apart: 11 -> 14, of which waited for: 9 -> 8; matrix products, arithmetic and copies ran while one was open for 9% -> 18% of each run, Pallas kernels for 0% -> 0%
where the time goes in v1:
time: 464 us; the launch traced here: 455 us
  waiting for transfers between devices  170 us (37%)
  local copies, waits for them, and re-layouts  72.2 us (16%)
  Pallas kernels  68.4 us (15%)
  matrix products  55.5 us (12%)
  other arithmetic  43.3 us (9%)
  blocking collectives  16.6 us (4%)
  between operations  15.2 us (3%)
  starting transfers between devices  11 us (2%)
    reduce_scatter x1, waiting for transfers between devices, block_device(): own_kv = lax.psum_scatter(grad_kv, 'ctx', scatter_dimension=0, tiled=True)  84.4 us
    pallas_call x1, Pallas kernels, weight_grads(): pl.pallas_call(functools.partial(weight_grad_kernel, dims), out_shape=[ja...  68.4 us
    all_gather x1, waiting for transfers between devices, block_device(): all_kv = lax.all_gather(key_value, 'ctx', axis=0, tiled=True)  55.3 us
    dynamic_update_slice x4, local copies, waits for them, and re-layouts, full_step(): lax.dynamic_update_slice_in_dim(grad_kv, both_grads, block_index * key_sp...  19.7 us
    ppermute x8, waiting for transfers between devices, with_partner(): lax.ppermute(sent, 'seq', [(0, 1), (1, 0)])  15.1 us
    concatenate x8, other arithmetic, with_partner(): jnp.concatenate([own, lax.ppermute(sent, 'seq', [(0, 1), (1, 0)])], axis=0)  13 us
    all_gather x1, waiting for transfers between devices, block_device(): lax.all_gather(w_qkv, 'fsdp', axis=0, tiled=True)  11.8 us
    ppermute x8, starting transfers between devices, with_partner(): lax.ppermute(sent, 'seq', [(0, 1), (1, 0)])  10.7 us
  transfers between devices with their start and end apart: 14, of which 8 were waited for; matrix products, arithmetic and copies ran while one was open for 18% of the time, Pallas kernels for 0%

profile of v1, /device:TPU:0, one launch (start us, length us, event | category | flops | bytes accessed | tf_op | source)
XLA Modules:
  0.0 455.1 jit_solution(221021356788972301)
XLA Ops:
  8.7 2.0 all-gather.1
  11.3 1.8 all-gather
  13.2 11.8 %all-gather.15.cloned.1.call-done = bf16[768,2304]{1,0:T(8,128)(2,1)} async-done(((bf16[384,2304]{1,0:T(8,128)(2,1)}), bf16[768,2304]{1,0:T(8,128)(2,1)}) %all-gather.15.cloned.1.call-update) | async-done | bytes 3538960 | tf_op jit(solution)/shard_map/all_gather | solution.py:578
  25.0 2.8 fusion.56
  30.8 1.8 all-gather.6
  32.7 1.8 all-gather.5
  34.6 1.8 all-gather.2
  36.6 1.8 all-gather.4
  38.4 1.8 all-gather.3
  40.3 1.8 all-gather.7
  42.2 1.8 all-gather.8
  44.3 55.3 %all-gather.17.cloned.1.call-done = bf16[1280,1536]{1,0:T(8,128)(2,1)} async-done(((bf16[160,1536]{1,0:T(8,128)(2,1)}), bf16[1280,1536]{1,0:T(8,128)(2,1)}) %all-gather.17.cloned.1.call-update) | async-done | bytes 3932176 | tf_op jit(solution)/shard_map/all_gather | solution.py:612
  99.5 6.3 %copy.51 = bf16[1280,1536]{0,1:T(8,128)(2,1)} copy(bf16[1280,1536]{1,0:T(8,128)(2,1)} %all-gather.17.cloned.1.call-done) | data formatting | bytes 7864320
  105.8 24.3 %while.28 = (s32[]{:T(128)}, f32[12,160]{1,0:T(8,128)S(1)}, f32[12,160]{1,0:T(8,128)S(1)}, f32[160,12,64]{0,2,1:T(8,128)S(1)}, s32[160]{0:T(256)S(1)}, /*index=5...) while((s32[]{:T(128)}, f32[12,160]{1,0:T(8,128)S(1)}, ...), condition=%wide.region_3.4_spmd.clone, body=%wide.region_0.3_spmd.clone.sunk | while | flops 331039360 | bytes 42089860 | solution.py:55
  107.3 1.7 fusion.122
  109.0 3.2 fusion.123
  112.2 3.6 fusion.125
  116.1 1.7 fusion.127
  119.2 2.0 fusion.122
  121.3 3.2 fusion.123
  124.5 3.6 fusion.125
  128.4 1.7 fusion.127
  130.2 1.9 fusion.64
  132.5 9.8 %multiply_convert_fusion = (bf16[160,3072]{1,0:T(8,128)(2,1)S(1)}, f32[160,3072]{1,0:T(8,128)}, f32[160,3072]{1,0:T(8,128)}) fusion(f32[3072]{0:T(1024)S(1)} %bitcast.209, bf16[160,768]{1,0:T(8,128)(2,1)S(1)} %fusion.50, bf16[768,3072]{1,0:T(8,128)(2,1)} %all-gather.21.cloned.1.call-done), kind=kOutput, calls=%fused_computation.45 | convolution fusion | flops 787415040 | bytes 9891840 | tf_op jit(solution)/shard_map/dot_general | solution.py:652
  143.1 3.5 fusion.65
  149.3 2.5 convert_reduce_fusion
  151.9 2.5 multiply_reduce_fusion
  158.9 4.2 broadcast_in_dim.44.clone
  163.0 50.3 %while.29 = (s32[]{:T(128)}, f32[160,12,64]{0,2,1:T(8,128)}, f32[1280,1536]{1,0:T(8,128)}, s32[2]{0:T(128)S(1)}, bf16[1280,1536]{0,1:T(8,128)(2,1)}, /*index=5*/...) while((s32[]{:T(128)}, f32[160,12,64]{0,2,1:T(8,128)}, ...), condition=%wide.region_13.14_spmd.clone, body=%wide.region_12.13_spmd.clone.sunk | while | flops 800665600 | bytes 101192928 | solution.py:55
  164.3 1.7 fusion.138
  167.2 2.1 fusion.140
  169.3 2.0 fusion.141
  172.0 2.3 fusion.142
  175.8 2.2 pad_maximum_fusion.13
  178.0 5.5 %copy.96 = f32[640,1536]{1,0:T(8,128)} copy(f32[640,1536]{0,1:T(8,128)} %pad_maximum_fusion.13) | data formatting | bytes 7864320 | tf_op jit(solution)/shard_map/while/body/eval_jaxpr/dynamic_update_slice | solution.py:704
  183.5 4.3 constant_dynamic-update-slice_fusion.2
  189.2 1.7 fusion.138
  192.0 2.1 fusion.140
  194.1 3.3 fusion.141
  197.4 2.3 fusion.142
  201.2 2.2 pad_maximum_fusion.13
  203.4 5.5 %copy.96 = f32[640,1536]{1,0:T(8,128)} copy(f32[640,1536]{0,1:T(8,128)} %pad_maximum_fusion.13) | data formatting | bytes 7864320 | tf_op jit(solution)/shard_map/while/body/eval_jaxpr/dynamic_update_slice | solution.py:704
  208.9 4.4 constant_dynamic-update-slice_fusion.2
  214.3 1.7 collective-permute-start.2
  216.7 5.7 %collective-permute-done.2 = bf16[160,768]{1,0:T(8,128)(2,1)S(1)} collective-permute-done((bf16[160,768]{1,0:T(8,128)(2,1)S(1)}, bf16[160,768]{1,0:T(8,128)(2,1)S(1)}, u32[]{:S(2)}, u32[]{:S(2)}) %collective-permute-start.2) | collective-permute-done | bytes 245792 | tf_op jit(solution)/shard_map/ppermute | solution.py:725
  223.3 1.7 collective-permute-start
  227.7 8.7 %dynamic-slice_reduce_fusion.1 = (bf16[160,16,96]{2,1,0:T(8,128)(2,1)S(1)}, bf16[160,16,96]{2,1,0:T(8,128)(2,1)S(1)}) fusion(bf16[160,16,2,96]{3,2,1,0:T(2,128)(2,1)S(1)} %reshape.220, s32[]{:T(128)S(6)} %select_n.48, s32[]{:T(128)S(6)} %select_n.49), kind=kLoop, calls=%fused_computation.60 | loop fusion | bytes 1966088 | tf_op jit(solution)/shard_map/jit(dynamic_index_in_dim)/dynamic_slice | solution.py:728
  237.9 1.7 collective-permute-start.1
  240.6 1.8 collective-permute-start.7
  249.5 8.6 %collective-permute-done.7 = bf16[160,384]{1,0:T(8,128)(2,1)} collective-permute-done((bf16[160,384]{1,0:T(8,128)(2,1)}, bf16[160,384]{1,0:T(8,128)(2,1)}, u32[]{:S(2)}, u32[]{:S(2)}) %collective-permute-start.7) | collective-permute-done | bytes 122912 | tf_op jit(solution)/shard_map/ppermute | solution.py:725
  258.1 1.7 collective-permute-start.4
  259.8 1.6 pad_maximum_fusion.11.refs_7_
  261.5 1.8 pad_maximum_fusion.7.refs_0_
  263.2 1.8 pad_maximum_fusion.9.refs_3_
  265.0 1.8 pad_maximum_fusion.10.refs_5_
  266.8 2.1 pad_maximum_fusion.2.refs_1_
  270.5 84.4 %reduce-scatter.2.cloned.1.call-done = f32[160,1536]{1,0:T(8,128)} async-done(((f32[1280,1536]{1,0:T(8,128)}), f32[160,1536]{1,0:T(8,128)}) %reduce-scatter.2.cloned.1.call-update) | async-done | bytes 983056 | tf_op jit(solution)/shard_map/reduce_scatter | solution.py:709
  356.9 2.0 fusion.51
  364.8 3.4 fusion.36
  368.6 1.9 pad_maximum_fusion.5.refs_6_
  370.5 68.4 %weight_grads.1 = (bf16[48,3072]{1,0:T(8,128)(2,1)}, bf16[192,768]{1,0:T(8,128)(2,1)}, bf16[48,2304]{1,0:T(8,128)(2,1)}, bf16[48,768]{1,0:T(8,128)(2,1)}, f32[8,128]{1,0:T(8,128)}) custom-call(bf16[320,768]{1,0:T(8,128)(2,1)} %pad_maximum_fusion.7.refs_0_, bf16[320,1536]{1,0:T(8,128)(2,1)} %pad_maximum_fusion.2.refs_1_, ...), custom_call_target="tpu_custom_call" | custom-call | tf_op jit(solution)/shard_map/weight_grads/pallas_call | solution.py:531
  439.0 1.6 fusion.63
  441.9 1.7 convert_element_type.156
  445.1 1.8 convert_element_type.158
  (265 shorter events, 51.5 us)
Async XLA Ops:
  7.2 17.8 %copy-start.18 = (bf16[1,160,768]{2,1,0:T(8,128)(2,1)S(1)}, bf16[1,160,768]{2,1,0:T(8,128)(2,1)}, u32[]{:S(2)}) copy-start(bf16[1,160,768]{2,1,0:T(8,128)(2,1)} %param.20) | copy-start | bytes 737284
  7.2 17.8 %all-gather.15.cloned.1.call-start = ((), (), s32[]{:S(2)}) async-start(), calls=%async_computation.1 | async-start | bytes 5308416 | tf_op jit(solution)/shard_map/all_gather | solution.py:578
  7.9 91.6 %all-gather.17.cloned.1.call-start = ((), (), s32[]{:S(2)}) async-start(), calls=%async_computation.2 | async-start | bytes 4423680 | tf_op jit(solution)/shard_map/all_gather | solution.py:612
  28.7 101.5 %all-gather.19.cloned.1.call-start = ((), (), s32[]{:S(2)}) async-start(), calls=%async_computation.3 | async-start | bytes 1769472 | tf_op jit(solution)/shard_map/all_gather | solution.py:581
  29.5 3.2 copy-start.38
  29.5 5.1 %copy-start.40 = (bf16[384]{0:T(512)(128)(2,1)S(1)}, bf16[384]{0:T(512)(128)(2,1)}, u32[]{:S(2)}) copy-start(bf16[384]{0:T(512)(128)(2,1)} %param.27) | copy-start | bytes 2308
  29.5 7.0 %copy-start.35 = (s32[1,1280]{1,0:T(1,128)S(1)}, s32[1,1280]{1,0:T(1,128)}, u32[]{:S(2)}) copy-start(s32[1,1280]{1,0:T(1,128)} %param.21) | copy-start | bytes 15364
  29.5 7.1 %copy-start.41 = (bf16[384]{0:T(512)(128)(2,1)S(1)}, bf16[384]{0:T(512)(128)(2,1)}, u32[]{:S(2)}) copy-start(bf16[384]{0:T(512)(128)(2,1)} %param.29) | copy-start | bytes 2308
  29.5 8.9 %copy-start.42 = (bf16[384]{0:T(512)(128)(2,1)S(1)}, bf16[384]{0:T(512)(128)(2,1)}, u32[]{:S(2)}) copy-start(bf16[384]{0:T(512)(128)(2,1)} %param.28) | copy-start | bytes 2308
  29.5 10.8 %copy-start.43 = (bf16[384]{0:T(512)(128)(2,1)S(1)}, bf16[384]{0:T(512)(128)(2,1)}, u32[]{:S(2)}) copy-start(bf16[384]{0:T(512)(128)(2,1)} %param.34) | copy-start | bytes 2308
  29.5 12.7 %copy-start.44 = (bf16[384]{0:T(512)(128)(2,1)S(1)}, bf16[384]{0:T(512)(128)(2,1)}, u32[]{:S(2)}) copy-start(bf16[384]{0:T(512)(128)(2,1)} %param.35) | copy-start | bytes 2308
  29.5 103.0 %all-gather.21.cloned.1.call-start = ((), (), s32[]{:S(2)}) async-start(), calls=%async_computation.4 | async-start | bytes 7077888 | tf_op jit(solution)/shard_map/all_gather | solution.py:585
  30.1 113.0 %all-gather.23.cloned.1.call-start = ((), (), s32[]{:S(2)}) async-start(), calls=%async_computation.5 | async-start | bytes 7077888 | tf_op jit(solution)/shard_map/all_gather | solution.py:587
  30.7 324.2 %reduce-scatter.2.cloned.1.call-start = ((), (), s32[]{:S(2)}) async-start(), calls=%async_computation.6 | async-start | bytes 8847360 | tf_op jit(solution)/shard_map/reduce_scatter | solution.py:709
  112.2 3.9 copy-start
  124.5 3.9 copy-start
  130.1 12.2 %copy-start.12 = (bf16[160,12,64]{0,2,1:T(8,128)(2,1)}, bf16[160,12,64]{0,2,1:T(8,128)(2,1)S(1)}, u32[]{:S(2)}) copy-start(bf16[160,12,64]{0,2,1:T(8,128)(2,1)S(1)} %fusion.53) | copy-start | bytes 737284
  132.5 9.9 %copy-start.24 = (bf16[160,768]{1,0:T(8,128)(2,1)}, bf16[160,768]{1,0:T(8,128)(2,1)S(1)}, u32[]{:S(2)}) copy-start(bf16[160,768]{1,0:T(8,128)(2,1)S(1)} %fusion.50) | copy-start | bytes 737284
  142.4 4.3 copy-start.10
  143.1 6.2 %slice-start = ((s8[4718592]{0:T(1024)(128)(4,1)}), s8[4194304]{0:T(1024)(128)(4,1)S(1)}, s32[]{:S(2)}) async-start(s8[4718592]{0:T(1024)(128)(4,1)} %bitcast.194), calls=%async_computation.7 | async-start | bytes 8388608
  143.1 3.8 copy-start.14
  143.1 6.2 %slice-start.1 = ((s8[4718592]{0:T(1024)(128)(4,1)}), s8[524288]{0:T(1024)(128)(4,1)S(1)}, s32[]{:S(2)}) async-start(s8[4718592]{0:T(1024)(128)(4,1)} %bitcast.194), calls=%async_computation.8 | async-start | bytes 1048576
  143.1 6.2 %copy-start.48 = (f32[160,3072]{1,0:T(8,128)S(1)}, f32[160,3072]{1,0:T(8,128)}, u32[]{:S(2)}) copy-start(f32[160,3072]{1,0:T(8,128)} %get-tuple-element.350) | copy-start | bytes 5898244
  146.7 2.6 copy-start.47
  147.7 4.1 slice-start.2
  149.3 2.6 copy-start.22
  149.3 2.5 slice-start.3
  151.8 2.5 copy-start.21
  163.0 3.0 copy-start.3
  166.9 2.4 copy-start.1
  169.3 2.7 copy-start.2
  169.3 2.7 copy-start.28
  183.5 4.4 copy-start.4
  183.5 4.4 copy-start.46
  187.8 3.0 copy-start.3
  194.1 3.3 copy-start.2
  194.1 3.3 copy-start.28
  208.9 4.4 copy-start.4
  208.9 4.4 copy-start.46
  213.3 2.7 copy-start.15
  213.4 9.9 %copy-start.25 = (bf16[160,768]{1,0:T(8,128)(2,1)S(1)}, bf16[160,768]{1,0:T(8,128)(2,1)}, u32[]{:S(2)}) copy-start(bf16[160,768]{1,0:T(8,128)(2,1)} %copy-done.24) | copy-start | bytes 737284
  213.4 11.6 %copy-start.11 = (bf16[160,3072]{1,0:T(8,128)(2,1)S(1)}, bf16[160,3072]{1,0:T(8,128)(2,1)}, u32[]{:S(2)}) copy-start(bf16[160,3072]{1,0:T(8,128)(2,1)} %copy-done.10) | copy-start | bytes 2949124
  213.4 13.1 %copy-start.13 = (bf16[160,12,64]{0,2,1:T(8,128)(2,1)S(1)}, bf16[160,12,64]{0,2,1:T(8,128)(2,1)}, u32[]{:S(2)}) copy-start(bf16[160,12,64]{0,2,1:T(8,128)(2,1)} %copy-done.12) | copy-start | bytes 737284
  214.3 8.1 %collective-permute-start.2 = (bf16[160,768]{1,0:T(8,128)(2,1)S(1)}, bf16[160,768]{1,0:T(8,128)(2,1)S(1)}, u32[]{:S(2)}, u32[]{:S(2)}) collective-permute-start(bf16[160,768]{1,0:T(8,128)(2,1)S(1)} %bitcast.200), channel_id=1, source_target_pairs={{0,16},{16,0},{1,17},{17,1},{2,18},{18,2},{3,19},{19,3},{4,20},{20... | collective-permute-start | bytes 737288 | tf_op jit(solution)/shard_map/ppermute | solution.py:725
  216.7 10.6 %copy-start.23 = (bf16[160,768]{1,0:T(8,128)(2,1)S(1)}, bf16[160,768]{1,0:T(8,128)(2,1)}, u32[]{:S(2)}) copy-start(bf16[160,768]{1,0:T(8,128)(2,1)} %copy-done.22) | copy-start | bytes 737284
  223.3 38.2 %collective-permute-start = (bf16[160,768]{1,0:T(8,128)(2,1)S(1)}, bf16[160,768]{1,0:T(8,128)(2,1)}, u32[]{:S(2)}, u32[]{:S(2)}) collective-permute-start(bf16[160,768]{1,0:T(8,128)(2,1)S(1)} %copy-done.25), channel_id=1, source_target_pairs={{0,16},{16,0},{1,17},{17,1},{2,18},{18,2},{3,19},{19,3},{4,20},{20... | collective-permute-start | bytes 737288 | tf_op jit(solution)/shard_map/ppermute | solution.py:725
  227.4 12.5 %copy-start.17 = (bf16[160,768]{1,0:T(8,128)(2,1)S(1)}, bf16[160,768]{1,0:T(8,128)(2,1)}, u32[]{:S(2)}) copy-start(bf16[160,768]{1,0:T(8,128)(2,1)} %copy-done.16) | copy-start | bytes 737284
  227.4 37.7 %collective-permute-start.5 = (bf16[160,768]{1,0:T(8,128)(2,1)S(1)}, bf16[160,768]{1,0:T(8,128)(2,1)}, u32[]{:S(2)}, u32[]{:S(2)}) collective-permute-start(bf16[160,768]{1,0:T(8,128)(2,1)S(1)} %copy-done.23), channel_id=1, source_target_pairs={{0,16},{16,0},{1,17},{17,1},{2,18},{18,2},{3,19},{19,3},{4,20},{20... | collective-permute-start | bytes 737288 | tf_op jit(solution)/shard_map/ppermute | solution.py:725
  236.4 7.3 %copy-start.5 = (f32[160,12,64]{0,2,1:T(8,128)S(1)}, f32[160,12,64]{0,2,1:T(8,128)}, u32[]{:S(2)}) copy-start(f32[160,12,64]{0,2,1:T(8,128)} %get-tuple-element.130) | copy-start | bytes 1474564
  237.9 28.9 %collective-permute-start.1 = (bf16[160,1536]{1,0:T(8,128)(2,1)}, bf16[160,1536]{1,0:T(8,128)(2,1)}, u32[]{:S(2)}, u32[]{:S(2)}) collective-permute-start(bf16[160,1536]{1,0:T(8,128)(2,1)} %reshape.222), channel_id=1, source_target_pairs={{0,16},{16,0},{1,17},{17,1},{2,18},{18,2},{3,19},{19,3},{4,20},{20... | collective-permute-start | bytes 1474568 | tf_op jit(solution)/shard_map/ppermute | solution.py:725
  239.6 23.6 %collective-permute-start.3 = (bf16[160,768]{1,0:T(8,128)(2,1)}, bf16[160,768]{1,0:T(8,128)(2,1)}, u32[]{:S(2)}, u32[]{:S(2)}) collective-permute-start(bf16[160,768]{1,0:T(8,128)(2,1)} %copy.59), channel_id=1, source_target_pairs={{0,16},{16,0},{1,17},{17,1},{2,18},{18,2},{3,19},{19,3},{4,20},{20... | collective-permute-start | bytes 737288 | tf_op jit(solution)/shard_map/ppermute | solution.py:725
  240.6 17.5 %collective-permute-start.7 = (bf16[160,384]{1,0:T(8,128)(2,1)}, bf16[160,384]{1,0:T(8,128)(2,1)}, u32[]{:S(2)}, u32[]{:S(2)}) collective-permute-start(bf16[160,384]{1,0:T(8,128)(2,1)} %get-tuple-element.339), channel_id=1, source_target_pairs={{0,16},{16,0},{1,17},{17,1},{2,18},{18,2},{3,19},{19,3},{4,20},{20... | collective-permute-start | bytes 368648 | tf_op jit(solution)/shard_map/ppermute | solution.py:725
  243.6 2.5 copy-start.32
  243.6 3.1 copy-start.37
  243.6 3.8 copy-start.36
  243.6 4.5 copy-start.34
  243.6 4.5 copy-start.31
  243.6 5.2 %copy-start.30 = (f32[768]{0:T(1024)S(1)}, f32[768]{0:T(1024)}, u32[]{:S(2)}) copy-start(f32[768]{0:T(1024)} %get-tuple-element.267) | copy-start | bytes 9220
  243.8 19.4 %copy-start.26 = (bf16[160,768]{1,0:T(8,128)(2,1)S(1)}, bf16[160,768]{1,0:T(8,128)(2,1)}, u32[]{:S(2)}) copy-start(bf16[160,768]{1,0:T(8,128)(2,1)} %copy.59) | copy-start | bytes 737284
  258.1 11.2 %collective-permute-start.4 = (bf16[160,1536]{1,0:T(8,128)(2,1)S(1)}, bf16[160,1536]{1,0:T(8,128)(2,1)S(1)}, u32[]{:S(2)}, u32[]{:S(2)}) collective-permute-start(bf16[160,1536]{1,0:T(8,128)(2,1)S(1)} %get-tuple-element.334), channel_id=1, source_target_pairs={{0,16},{16,0},{1,17},{17,1},{2,18},{18,2},{3,19},{19,3},{4,20},{20... | collective-permute-start | bytes 1474568 | tf_op jit(solution)/shard_map/ppermute | solution.py:725
  270.5 94.2 %copy-start.7 = (bf16[768,2304]{1,0:T(8,128)(2,1)S(1)}, bf16[768,2304]{1,0:T(8,128)(2,1)}, u32[]{:S(2)}) copy-start(bf16[768,2304]{1,0:T(8,128)(2,1)} %all-gather.15.cloned.1.call-done) | copy-start | bytes 10616836
  359.0 9.6 %collective-permute-start.6 = (bf16[160,1152]{1,0:T(8,128)(2,1)}, bf16[160,1152]{1,0:T(8,128)(2,1)}, u32[]{:S(2)}, u32[]{:S(2)}) collective-permute-start(bf16[160,1152]{1,0:T(8,128)(2,1)} %get-tuple-element.336), channel_id=1, source_target_pairs={{0,16},{16,0},{1,17},{17,1},{2,18},{18,2},{3,19},{19,3},{4,20},{20... | collective-permute-start | bytes 1105928 | tf_op jit(solution)/shard_map/ppermute | solution.py:725
  364.8 3.8 copy-start.20
  439.0 8.0 %copy-start.29 = (bf16[192,768]{1,0:T(8,128)(2,1)S(1)}, bf16[192,768]{1,0:T(8,128)(2,1)}, u32[]{:S(2)}) copy-start(bf16[192,768]{1,0:T(8,128)(2,1)} %get-tuple-element.136) | copy-start | bytes 884740
  (14 other events, 18.6 us)
Sparse Core Ops, SparseCore 0:
  9.5 15.4 all-gather.14
  28.8 70.6 all-gather.16
  101.1 7.8 all-gather.18
  110.4 15.5 all-gather.20
  127.4 15.6 all-gather.22
  213.5 141.3 reduce-scatter.1

commit v2 on v1

--- a/solution.py
+++ b/solution.py
@@ -305,10 +305,10 @@
 
 def weight_grad_kernel(dims, *refs):
     count = len(dims)
-    a_refs, b_refs, vec_ref = refs[:count], refs[count : 2 * count], refs[2 * count]
-    outs = refs[2 * count + 1 : 3 * count + 1]
-    vec_out = refs[3 * count + 1]
-    rest = refs[3 * count + 2 :]
+    operands, vec_ref = refs[: 4 * count], refs[4 * count]
+    outs = refs[4 * count + 1 : 5 * count + 1]
+    vec_out = refs[5 * count + 1]
+    rest = refs[5 * count + 2 :]
     units = count + 1
     parts, from_core = rest[:units], rest[units : 2 * units]
     from_pair, from_low = rest[2 * units : 3 * units], rest[3 * units : 4 * units]
@@ -389,12 +389,11 @@
             rows, columns, _ = dims[u]
             step = 384
             for first in range(0, columns, step):
-                product = lax.dot_general(
-                    a_refs[u][...],
-                    b_refs[u][:, first : first + step],
-                    (((0,), (0,)), ((), ())),
-                    preferred_element_type=jnp.float32,
-                ).astype(jnp.bfloat16)
+                a_own, a_pair, b_own, b_pair = operands[4 * u : 4 * u + 4]
+                span = slice(first, first + step)
+                own_b = b_own[group, :, span] if len(b_own.shape) == 3 else b_own[:, span]
+                own_a = a_own[group] if len(a_own.shape) == 3 else a_own[...]
+                product = (dot_tn(own_a, own_b) + dot_tn(a_pair[...], b_pair[:, span])).astype(BF16)
                 for j in range(4 * LINE):
                     parts[u][j % 2, j // 4, (j // 2) % 2, :, first : first + step] = product[
                         j * rows : (j + 1) * rows
@@ -511,12 +510,12 @@
                 down_copy(u, k).wait_send()
 
 
-def weight_grads(a_list, b_list, vec):
-    widths = [(a.shape[1], b.shape[1]) for a, b in zip(a_list, b_list)]
+def weight_grads(operands, vec):
+    widths = [(group[1].shape[1], group[3].shape[1]) for group in operands]
     dims, shapes = [], []
     for a_width, b_width in widths:
         rows = a_width // (4 * LINE)
-        wide = a_width == a_list[0].shape[1]
+        wide = a_width == widths[0][0]
         dims.append((rows, b_width, wide))
         shapes.append((rows, 2 * b_width) if wide else (2 * rows, b_width))
     blocks = [((rows, columns), jnp.bfloat16) for rows, columns, _ in dims]
@@ -532,14 +531,740 @@
         functools.partial(weight_grad_kernel, dims),
         out_shape=[jax.ShapeDtypeStruct(shape, jnp.bfloat16) for shape in shapes]
         + [jax.ShapeDtypeStruct((8, 128), jnp.float32)],
-        in_specs=[pl.BlockSpec(memory_space=pltpu.VMEM)] * (2 * len(dims) + 1),
+        in_specs=[pl.BlockSpec(memory_space=pltpu.VMEM)] * (4 * len(dims) + 1),
         out_specs=[pl.BlockSpec(memory_space=pltpu.VMEM)] * (len(dims) + 1),
         scratch_shapes=scratch,
         compiler_params=pltpu.CompilerParams(
             collective_id=0, has_side_effects=True, vmem_limit_bytes=60 << 20
         ),
         name="weight_grads",
-    )(*a_list, *b_list, vec)
+    )(*[a for group in operands for a in group], vec)
+
+
+HEADS_OWN = 3
+F32 = jnp.float32
+BF16 = jnp.bfloat16
+ANY = pl.BlockSpec(memory_space=pl.ANY)
+INNER = pl.BlockSpec(memory_space=pltpu.VMEM)
+
+
+def dot_nt(a, b):
+    return lax.dot_general(a, b, (((1,), (1,)), ((), ())), preferred_element_type=F32)
+
+
+def dot_tn(a, b):
+    return lax.dot_general(a, b, (((0,), (0,)), ((), ())), preferred_element_type=F32)
+
+
+def dot_nn(a, b):
+    return lax.dot_general(a, b, (((1,), (0,)), ((), ())), preferred_element_type=F32)
+
+
+def greet(targets):
+    barrier = pltpu.get_barrier_semaphore()
+    for target in targets:
+        pl.semaphore_signal(barrier, inc=1, device_id=target, device_id_type=MESH_ID)
+    pl.semaphore_wait(barrier, len(targets))
+
+
+def attend_kernel(
+    tok,
+    ids_row,
+    ids_col,
+    vec,
+    w_qkv,
+    w_out,
+    w_up,
+    w_down,
+    attended,
+    tok_pair,
+    vec_all,
+    w_full,
+    out_other,
+    up_other,
+    down_other,
+    q_heads,
+    k_heads,
+    v_heads,
+    att_full,
+    totals,
+    probs_out,
+    w_all,
+    mixed,
+    sent,
+    mine,
+    other,
+    att_sent,
+    att_land,
+    probs,
+    local_sem,
+    probs_sem,
+    core_out,
+    core_in,
+    line_out,
+    line_in,
+    pair_out,
+    pair_in,
+    back_out,
+    back_in,
+    seq_out,
+    seq_in,
+):
+    place = lax.axis_index("ctx")
+    core = lax.axis_index("fsdp")
+    group = lax.axis_index("seq")
+    line, side = place // 2, place % 2
+    to_core = {"fsdp": 1 - core}
+    to_pair = {"ctx": place + 1 - 2 * side}
+    to_seq = {"seq": 1 - group}
+    rows = tok.shape[0]
+    width = tok.shape[1]
+    half = width // 2
+    third = HEADS_OWN * HEAD
+
+    def ahead(k):
+        return lax.rem(line + k, LINE)
+
+    def behind(k):
+        return lax.rem(line + LINE - k, LINE)
+
+    def to_line(k):
+        return {"ctx": 2 * ahead(k) + side}
+
+    def block(which):
+        return pl.ds(pl.multiple_of(which * rows, 32), rows)
+
+    own_rows = pl.ds(pl.multiple_of(core * half, 128), half)
+    other_rows = pl.ds(pl.multiple_of((1 - core) * half, 128), half)
+
+    own_load = pltpu.make_async_copy(w_qkv, w_all.at[own_rows], local_sem.at[0])
+    own_load.start()
+    greet([to_core, to_pair, to_seq] + [to_line(k) for k in range(1, LINE)])
+    core_copies = [
+        remote(w_qkv, w_all.at[own_rows], core_out.at[0], core_in.at[0], to_core),
+        remote(vec, vec_all.at[:, own_rows], core_out.at[1], core_in.at[1], to_core),
+        remote(w_out, out_other, core_out.at[2], core_in.at[2], to_core),
+        remote(w_up, up_other, core_out.at[3], core_in.at[3], to_core),
+        remote(w_down, down_other, core_out.at[4], core_in.at[4], to_core),
+    ]
+    seq_copy = remote(tok, tok_pair, seq_out.at[0], seq_in.at[0], to_seq)
+    core_copies[0].start()
+    core_copies[1].start()
+    seq_copy.start()
+    vec_all[:, own_rows] = vec[...]
+    own_load.wait()
+    step = width // 2
+    for first in range(0, 3 * width, step):
+        mixed[:, first : first + step] = dot_nn(
+            tok[:, own_rows], w_all[own_rows, first : first + step]
+        )
+    core_copies[0].wait_recv()
+    core_copies[1].wait_recv()
+    for copy in core_copies[2:]:
+        copy.start()
+    bias = vec_all[...]
+    for part in (1, 2, 0):
+        for first in range(part * width, (part + 1) * width, step):
+            total = mixed[:, first : first + step] + dot_nn(
+                tok[:, other_rows], w_all[other_rows, first : first + step]
+            )
+            within = first - part * width
+            if part == 0:
+                total += bias[0:1, within : within + step]
+            if part == 2:
+                total += bias[1:2, within : within + step]
+            total = total.astype(BF16)
+            slot = (2, 0, 1)[part] * third
+            for j in range(2):
+                sent[within // third + j, :, slot : slot + third] = total[
+                    :, j * third : (j + 1) * third
+                ]
+
+    def line_copy(k):
+        return remote(
+            sent.at[ahead(k)], mine.at[block(line)], line_out.at[k - 1], line_in.at[k - 1], to_line(k)
+        )
+
+    def line_landed(k):
+        return remote(
+            sent.at[ahead(k)],
+            mine.at[block(behind(k))],
+            line_out.at[k - 1],
+            line_in.at[k - 1],
+            to_line(k),
+        )
+
+    def pair_copy(k):
+        where = block(behind(k))
+        return remote(
+            mine.at[where, 0 : 2 * third],
+            other.at[where],
+            pair_out.at[k],
+            pair_in.at[k],
+            to_pair,
+        )
+
+    for k in (3, 2, 1):
+        line_copy(k).start()
+    full_store = pltpu.make_async_copy(w_all, w_full, local_sem.at[1])
+    full_store.start()
+    mine[block(line)] = sent[line]
+    pair_copy(0).start()
+    for k in (1, 2, 3):
+        line_landed(k).wait_recv()
+        pair_copy(k).start()
+    seq_rows = 2 * LINE * rows
+    mid = LINE * rows
+    for h in range(HEADS_OWN):
+        q_heads[h] = mine[:, 2 * third + h * HEAD : 2 * third + (h + 1) * HEAD]
+        k_heads[h, 0:mid] = mine[:, h * HEAD : (h + 1) * HEAD]
+        v_heads[h, 0:mid] = mine[:, third + h * HEAD : third + (h + 1) * HEAD]
+    for k in range(LINE):
+        pair_copy(k).wait_recv()
+    for h in range(HEADS_OWN):
+        k_heads[h, mid:seq_rows] = other[:, h * HEAD : (h + 1) * HEAD]
+        v_heads[h, mid:seq_rows] = other[:, third + h * HEAD : third + (h + 1) * HEAD]
+
+    def back_copy(k):
+        return remote(
+            att_sent.at[ahead(k)],
+            att_land.at[line],
+            back_out.at[k - 1],
+            back_in.at[k - 1],
+            to_line(k),
+        )
+
+    def back_landed(k):
+        return remote(
+            att_sent.at[ahead(k)],
+            att_land.at[behind(k)],
+            back_out.at[k - 1],
+            back_in.at[k - 1],
+            to_line(k),
+        )
+
+    def probs_copy(k):
+        where = block(ahead(k))
+        return pltpu.make_async_copy(
+            probs.at[:, where], probs_out.at[:, where], probs_sem.at[k - 1]
+        )
+
+    def attend(k, carry):
+        which = ahead(k)
+        where = block(which)
+        allowed = ids_col[where] == ids_row[...]
+        for h in range(HEADS_OWN):
+            scores = dot_nt(q_heads[h, where], k_heads[h]) * 0.125
+            scores = jnp.where(allowed, scores, NEGATIVE)
+            level = jnp.ceil(jnp.max(scores, axis=-1, keepdims=True) * LOG2_E)
+            unnorm = jnp.exp(scores - LOG_TWO * level)
+            row_total = jnp.sum(unnorm, axis=-1, keepdims=True)
+            unnorm_b = unnorm.astype(BF16)
+            probs[h, where] = unnorm_b
+            value = dot_nn(unnorm_b, v_heads[h]) / row_total
+            att_full[where, h * HEAD : (h + 1) * HEAD] = value
+            totals[where, h : h + 1] = row_total
+            att_sent[which, :, h * HEAD : (h + 1) * HEAD] = value.astype(BF16)
+        probs_copy(k).start()
+
+        @pl.when(k < LINE)
+        def _():
+            back_copy(k).start()
+
+        return carry
+
+    lax.fori_loop(1, LINE + 1, attend, 0)
+    att_land[line] = att_sent[line]
+    for k in (1, 2, 3):
+        back_landed(k).wait_recv()
+    for d in range(LINE):
+        attended[:, d * third : (d + 1) * third] = att_land[d]
+    for k in (1, 2, 3):
+        line_copy(k).wait_send()
+        back_copy(k).wait_send()
+    for k in range(LINE):
+        pair_copy(k).wait_send()
+        probs_copy(k + 1).wait()
+    for copy in core_copies[2:]:
+        copy.wait_recv()
+    for copy in core_copies:
+        copy.wait_send()
+    seq_copy.wait()
+    full_store.wait()
+
+
+def attend_forward(tok, ids_row, ids_col, vec, w_qkv, w_out, w_up, w_down):
+    rows, width = tok.shape
+    third = HEADS_OWN * HEAD
+    mid, seq_rows = LINE * rows, 2 * LINE * rows
+    shape = jax.ShapeDtypeStruct
+    outs = [
+        (shape((rows, width), BF16), INNER),
+        (shape((rows, width), BF16), INNER),
+        (shape((16, width), F32), INNER),
+        (shape((width, 3 * width), BF16), ANY),
+        (shape(w_out.shape, BF16), ANY),
+        (shape(w_up.shape, BF16), ANY),
+        (shape(w_down.shape, BF16), ANY),
+        (shape((HEADS_OWN, mid, HEAD), BF16), INNER),
+        (shape((HEADS_OWN, seq_rows, HEAD), BF16), INNER),
+        (shape((HEADS_OWN, seq_rows, HEAD), BF16), INNER),
+        (shape((mid, third), F32), INNER),
+        (shape((mid, 128), F32), INNER),
+        (shape((HEADS_OWN, mid, seq_rows), BF16), ANY),
+    ]
+    dma = pltpu.SemaphoreType.DMA
+    return pl.pallas_call(
+        attend_kernel,
+        out_shape=[o[0] for o in outs],
+        in_specs=[INNER] * 4 + [ANY] * 4,
+        out_specs=[o[1] for o in outs],
+        scratch_shapes=[
+            pltpu.VMEM((width, 3 * width), BF16),
+            pltpu.VMEM((rows, 3 * width), F32),
+            pltpu.VMEM((LINE, rows, 3 * third), BF16),
+            pltpu.VMEM((mid, 3 * third), BF16),
+            pltpu.VMEM((mid, 2 * third), BF16),
+            pltpu.VMEM((LINE, rows, third), BF16),
+            pltpu.VMEM((LINE, rows, third), BF16),
+            pltpu.VMEM((HEADS_OWN, mid, seq_rows), BF16),
+            dma((2,)),
+            dma((LINE,)),
+            dma((5,)),
+            dma((5,)),
+            dma((3,)),
+            dma((3,)),
+            dma((LINE,)),
+            dma((LINE,)),
+            dma((3,)),
+            dma((3,)),
+            dma((1,)),
+            dma((1,)),
+        ],
+        compiler_params=pltpu.CompilerParams(
+            collective_id=1, has_side_effects=True, vmem_limit_bytes=50 << 20
+        ),
+        name="attend_forward",
+    )(tok, ids_row, ids_col, vec, w_qkv, w_out, w_up, w_down)
+
+
+def token_kernel(
+    attended,
+    tok,
+    grad_out,
+    vec,
+    w_out,
+    out_other,
+    w_up,
+    up_other,
+    w_down,
+    down_other,
+    result,
+    normed_o,
+    act_halves,
+    up_halves,
+    ffn_o,
+    first_o,
+    branch_halves,
+    att_grads,
+    vec_grads,
+    out_all,
+    up_all,
+    down_all,
+    active,
+    slope,
+    sem,
+):
+    core = lax.axis_index("fsdp")
+    rows, width = tok.shape
+    hidden_units = up_all.shape[1]
+    third = HEADS_OWN * HEAD
+
+    def place_of(which, size):
+        return pl.ds(pl.multiple_of(which * size, 128), size)
+
+    loads = []
+    for i, (own, far, full) in enumerate(
+        ((w_out, out_other, out_all), (w_up, up_other, up_all), (w_down, down_other, down_all))
+    ):
+        size = own.shape[0]
+        loads.append(
+            (
+                pltpu.make_async_copy(own, full.at[place_of(core, size)], sem.at[2 * i]),
+                pltpu.make_async_copy(far, full.at[place_of(1 - core, size)], sem.at[2 * i + 1]),
+            )
+        )
+    for pair in loads:
+        for load in pair:
+            load.start()
+
+    def arrived(i):
+        for load in loads[i]:
+            load.wait()
+
+    bias_out, gain_one, shift_one = vec[2:3], vec[3:4], vec[4:5]
+    bias_down, gain_two, shift_two = vec[5:6], vec[6:7], vec[7:8]
+    arrived(0)
+    branch = dot_nn(attended[...], out_all[...]) + bias_out
+    normed_one, norm_one, scale_one = norm_forward(tok[...].astype(F32) + branch, gain_one, shift_one)
+    normed_b = normed_one.astype(BF16)
+    normed_o[...] = normed_b
+    arrived(1)
+    step = width
+    half = width // 2
+    for c in range(hidden_units // step):
+        at, row = (c // 2) * half, 8 + 2 * (c % 2)
+        bias = jnp.concatenate([vec[row : row + 1, at : at + half], vec[row + 1 : row + 2, at : at + half]], axis=1)
+        up = dot_nn(normed_b, up_all[:, c * step : (c + 1) * step]) + bias
+        cdf = 0.5 * (1.0 + lax.erf(up * 0.7071067811865476))
+        active[:, c * step : (c + 1) * step] = (up * cdf).astype(BF16)
+        slope[:, c * step : (c + 1) * step] = cdf + up * (
+            0.3989422804014327 * jnp.exp(-0.5 * up * up)
+        )
+    arrived(2)
+    second = normed_one + bias_down
+    second += dot_nn(active[...], down_all[...])
+    final, norm_two, scale_two = norm_forward(second, gain_two, shift_two)
+    result[...] = final.astype(BF16)
+    grad_second, gain_grad, shift_grad = norm_backward(
+        grad_out[...].astype(F32), norm_two, scale_two, gain_two
+    )
+    grad_ffn = grad_second.astype(BF16)
+    ffn_o[...] = grad_ffn
+    vec_grads[...] = jnp.zeros(vec_grads.shape, F32)
+    vec_grads[3:4] = jnp.sum(grad_ffn.astype(F32), axis=0, keepdims=True)
+    vec_grads[4:5] = gain_grad[None]
+    vec_grads[5:6] = shift_grad[None]
+    grad_normed = grad_second
+    piece = hidden_units // (8 * LINE)
+    for c in range(hidden_units // step):
+        span = slice(c * step, (c + 1) * step)
+        grad_up = (dot_nt(grad_ffn, down_all[span]) * slope[:, span]).astype(BF16)
+        vec_grads[8 + c : 9 + c] = jnp.sum(grad_up.astype(F32), axis=0, keepdims=True)
+        grad_normed += dot_nt(grad_up, up_all[:, span])
+        up_halves[c // 2, :, (c % 2) * step : (c % 2 + 1) * step] = grad_up
+    for j in range(4 * LINE):
+        for g in range(2):
+            at = (2 * j + g) * piece
+            act_halves[g, :, j * piece : (j + 1) * piece] = active[:, at : at + piece]
+    grad_first, gain_grad, shift_grad = norm_backward(grad_normed, norm_one, scale_one, gain_one)
+    first_o[...] = grad_first
+    vec_grads[1:2] = gain_grad[None]
+    vec_grads[2:3] = shift_grad[None]
+    grad_branch = grad_first.astype(BF16)
+    vec_grads[0:1] = jnp.sum(grad_branch.astype(F32), axis=0, keepdims=True)
+    for g in range(2):
+        branch_halves[g] = grad_branch[:, g * half : (g + 1) * half]
+    grad_att = dot_nt(grad_branch, out_all[...]).astype(BF16)
+    for d in range(LINE):
+        att_grads[d] = grad_att[:, d * third : (d + 1) * third]
+
+
+def token_local(attended, tok, grad_out, vec, w_out, out_other, w_up, up_other, w_down, down_other):
+    rows, width = tok.shape
+    units = w_up.shape[1]
+    shape = jax.ShapeDtypeStruct
+    return pl.pallas_call(
+        token_kernel,
+        out_shape=[
+            shape((rows, width), BF16),
+            shape((rows, width), BF16),
+            shape((2, rows, units // 2), BF16),
+            shape((2, rows, units // 2), BF16),
+            shape((rows, width), BF16),
+            shape((rows, width), F32),
+            shape((2, rows, width // 2), BF16),
+            shape((LINE, rows, HEADS_OWN * HEAD), BF16),
+            shape((16, width), F32),
+        ],
+        in_specs=[INNER] * 4 + [ANY] * 6,
+        out_specs=[INNER] * 9,
+        scratch_shapes=[
+            pltpu.VMEM((width, width), BF16),
+            pltpu.VMEM((width, units), BF16),
+            pltpu.VMEM((units, width), BF16),
+            pltpu.VMEM((rows, units), BF16),
+            pltpu.VMEM((rows, units), F32),
+            pltpu.SemaphoreType.DMA((6,)),
+        ],
+        compiler_params=pltpu.CompilerParams(vmem_limit_bytes=50 << 20),
+        name="token_local",
+    )(attended, tok, grad_out, vec, w_out, out_other, w_up, up_other, w_down, down_other)
+
+
+def attend_grad_kernel(
+    att_grads,
+    q_heads,
+    k_heads,
+    v_heads,
+    att_full,
+    totals,
+    grad_first,
+    probs_in,
+    w_full,
+    normed_b,
+    act_halves,
+    up_halves,
+    grad_ffn,
+    attended,
+    branch_halves,
+    grad_hidden,
+    mixed_halves,
+    vec_grads,
+    normed_pair,
+    act_pair,
+    up_pair,
+    ffn_pair,
+    att_pair,
+    branch_pair,
+    mixed_pair,
+    w_all,
+    probs,
+    grad_land,
+    scaled,
+    score_grads,
+    query_grads,
+    kv_own,
+    kv_sent,
+    kv_pair,
+    kv_sum,
+    kv_land,
+    query_land,
+    mixed,
+    local_sem,
+    line_out,
+    line_in,
+    pair_out,
+    pair_in,
+    back_out,
+    back_in,
+    seq_out,
+    seq_in,
+):
+    place = lax.axis_index("ctx")
+    group = lax.axis_index("seq")
+    line, side = place // 2, place % 2
+    to_pair = {"ctx": place + 1 - 2 * side}
+    to_seq = {"seq": 1 - group}
+    rows, width = grad_hidden.shape
+    third = HEADS_OWN * HEAD
+    mid = LINE * rows
+
+    def ahead(k):
+        return lax.rem(line + k, LINE)
+
+    def behind(k):
+        return lax.rem(line + LINE - k, LINE)
+
+    def to_line(k):
+        return {"ctx": 2 * ahead(k) + side}
+
+    def block(which):
+        return pl.ds(pl.multiple_of(which * rows, 32), rows)
+
+    probs_load = pltpu.make_async_copy(probs_in, probs, local_sem.at[0])
+    w_load = pltpu.make_async_copy(w_full, w_all, local_sem.at[1])
+    probs_load.start()
+    greet([to_pair, to_seq] + [to_line(k) for k in range(1, LINE)])
+
+    def line_copy(k):
+        return remote(
+            att_grads.at[ahead(k)],
+            grad_land.at[block(line)],
+            line_out.at[k - 1],
+            line_in.at[k - 1],
+            to_line(k),
+        )
+
+    def line_landed(k):
+        return remote(
+            att_grads.at[ahead(k)],
+            grad_land.at[block(behind(k))],
+            line_out.at[k - 1],
+            line_in.at[k - 1],
+            to_line(k),
+        )
+
+    for k in (3, 2, 1):
+        line_copy(k).start()
+    seq_copies = []
+    for i, (src, dst) in enumerate(
+        (
+            (normed_b, normed_pair),
+            (up_halves.at[1 - group], up_pair),
+            (act_halves.at[1 - group], act_pair),
+            (grad_ffn, ffn_pair),
+            (attended, att_pair),
+            (branch_halves.at[1 - group], branch_pair),
+            (mixed_halves.at[1 - group], mixed_pair),
+        )
+    ):
+        seq_copies.append(remote(src, dst, seq_out.at[i], seq_in.at[i], to_seq))
+    for copy in seq_copies[:-1]:
+        copy.start()
+    w_load.start()
+    grad_land[block(line)] = att_grads[line]
+    for k in (1, 2, 3):
+        line_landed(k).wait_recv()
+    probs_load.wait()
+
+    def pair_copy(h):
+        return remote(kv_sent.at[h], kv_pair.at[h], pair_out.at[h], pair_in.at[h], to_pair)
+
+    for h in range(HEADS_OWN):
+        lanes = slice(h * HEAD, (h + 1) * HEAD)
+
+        def row_grads(i, carry, h=h, lanes=lanes):
+            where = block(i)
+            incoming = grad_land[where, lanes].astype(F32)
+            row_total = totals[where, h : h + 1]
+            delta = jnp.sum(incoming * att_full[where, lanes], axis=-1, keepdims=True)
+            grad_scaled = (incoming / row_total).astype(BF16)
+            scaled[where] = grad_scaled
+            weights = dot_nt(grad_scaled, v_heads[h])
+            ds = (probs[h, where].astype(F32) * (weights - delta / row_total)).astype(BF16)
+            score_grads[where] = ds
+            query_grads[where, lanes] = (dot_nn(ds, k_heads[h]) * 0.125).astype(BF16)
+            return carry
+
+        lax.fori_loop(0, LINE, row_grads, 0)
+        both = jnp.concatenate(
+            [dot_tn(q_heads[h], score_grads[...]) * 0.125, dot_tn(scaled[...], probs[h])], axis=0
+        )
+        both = jnp.transpose(both)
+        kv_sent[h] = both[mid:].astype(BF16)
+        pair_copy(h).start()
+        kv_own[h] = both[:mid]
+
+    def query_back(k):
+        return remote(
+            query_grads.at[block(ahead(k))],
+            query_land.at[line],
+            back_out.at[HEADS_OWN, k - 1],
+            back_in.at[HEADS_OWN, k - 1],
+            to_line(k),
+        )
+
+    def query_landed(k):
+        return remote(
+            query_grads.at[block(ahead(k))],
+            query_land.at[behind(k)],
+            back_out.at[HEADS_OWN, k - 1],
+            back_in.at[HEADS_OWN, k - 1],
+            to_line(k),
+        )
+
+    def kv_back(h, k):
+        return remote(
+            kv_sum.at[h, block(ahead(k))],
+            kv_land.at[h, line],
+            back_out.at[h, k - 1],
+            back_in.at[h, k - 1],
+            to_line(k),
+        )
+
+    def kv_landed(h, k):
+        return remote(
+            kv_sum.at[h, block(ahead(k))],
+            kv_land.at[h, behind(k)],
+            back_out.at[h, k - 1],
+            back_in.at[h, k - 1],
+            to_line(k),
+        )
+
+    for k in (3, 2, 1):
+        query_back(k).start()
+    query_land[line] = query_grads[block(line)]
+    for h in range(HEADS_OWN):
+        pair_copy(h).wait_recv()
+        kv_sum[h] = (kv_own[h] + kv_pair[h].astype(F32)).astype(BF16)
+        for k in (3, 2, 1):
+            kv_back(h, k).start()
+        kv_land[h, line] = kv_sum[h, block(line)]
+    for k in (1, 2, 3):
+        query_landed(k).wait_recv()
+    for d in range(LINE):
+        mixed[:, d * third : (d + 1) * third] = query_land[d]
+    for h in range(HEADS_OWN):
+        for k in (1, 2, 3):
+            kv_landed(h, k).wait_recv()
+        for d in range(LINE):
+            at = width + d * third + h * HEAD
+            mixed[:, at : at + HEAD] = kv_land[h, d, :, 0:HEAD]
+            mixed[:, width + at : width + at + HEAD] = kv_land[h, d, :, HEAD:]
+    middle = 3 * width // 2
+    for g in range(2):
+        mixed_halves[g] = mixed[:, g * middle : (g + 1) * middle]
+    seq_copies[-1].start()
+    w_load.wait()
+    grad_hidden[...] = grad_first[...] + dot_nt(mixed[...], w_all[...])
+    vec_grads[...] = jnp.zeros(vec_grads.shape, F32)
+    vec_grads[0:1] = jnp.sum(mixed[:, :width].astype(F32), axis=0, keepdims=True)
+    vec_grads[1:2] = jnp.sum(mixed[:, 2 * width :].astype(F32), axis=0, keepdims=True)
+    for k in (1, 2, 3):
+        line_copy(k).wait_send()
+        query_back(k).wait_send()
+        for h in range(HEADS_OWN):
+            kv_back(h, k).wait_send()
+    for h in range(HEADS_OWN):
+        pair_copy(h).wait_send()
+    for copy in seq_copies:
+        copy.wait()
+
+
+def attend_backward(*args):
+    rows, width = args[6].shape
+    units = args[10].shape[2]
+    third = HEADS_OWN * HEAD
+    mid, seq_rows = LINE * rows, 2 * LINE * rows
+    shape = jax.ShapeDtypeStruct
+    outs = [
+        (shape((rows, width), F32), INNER),
+        (shape((2, rows, 3 * width // 2), BF16), INNER),
+        (shape((8, width), F32), INNER),
+        (shape((rows, width), BF16), ANY),
+        (shape((rows, units), BF16), ANY),
+        (shape((rows, units), BF16), ANY),
+        (shape((rows, width), BF16), ANY),
+        (shape((rows, width), BF16), ANY),
+        (shape((rows, width // 2), BF16), ANY),
+        (shape((rows, 3 * width // 2), BF16), ANY),
+    ]
+    dma = pltpu.SemaphoreType.DMA
+    return pl.pallas_call(
+        attend_grad_kernel,
+        out_shape=[o[0] for o in outs],
+        in_specs=[INNER] * 7 + [ANY] * 8,
+        out_specs=[o[1] for o in outs],
+        scratch_shapes=[
+            pltpu.VMEM((width, 3 * width), BF16),
+            pltpu.VMEM((HEADS_OWN, mid, seq_rows), BF16),
+            pltpu.VMEM((mid, third), BF16),
+            pltpu.VMEM((mid, HEAD), BF16),
+            pltpu.VMEM((mid, seq_rows), BF16),
+            pltpu.VMEM((mid, third), BF16),
+            pltpu.VMEM((HEADS_OWN, mid, 128), F32),
+            pltpu.VMEM((HEADS_OWN, mid, 128), BF16),
+            pltpu.VMEM((HEADS_OWN, mid, 128), BF16),
+            pltpu.VMEM((HEADS_OWN, mid, 128), BF16),
+            pltpu.VMEM((HEADS_OWN, LINE, rows, 128), BF16),
+            pltpu.VMEM((LINE, rows, third), BF16),
+            pltpu.VMEM((rows, 3 * width), BF16),
+            dma((2,)),
+            dma((3,)),
+            dma((3,)),
+            dma((3,)),
+            dma((3,)),
+            dma((4, 3)),
+            dma((4, 3)),
+            dma((7,)),
+            dma((7,)),
+        ],
+        compiler_params=pltpu.CompilerParams(
+            collective_id=2, has_side_effects=True, vmem_limit_bytes=50 << 20
+        ),
+        name="attend_backward",
+    )(*args)
 
 
 def block_device(
@@ -560,218 +1285,125 @@
     gain_two,
     shift_two,
 ):
-    (
-        w_qkv,
+    tok, grad_out = hidden[0], out_grad[0]
+    rows, width = tok.shape
+    half = width // 2
+    side = lax.axis_index("ctx") % 2
+    ids = segment_ids[0].reshape(LINE, 2, rows)
+    own_ids = lax.dynamic_index_in_dim(ids, side, 1, False).reshape(-1)
+    far_ids = lax.dynamic_index_in_dim(ids, 1 - side, 1, False).reshape(-1)
+    ids_row = jnp.concatenate([own_ids, far_ids])[None, :]
+    ids_col = own_ids[:, None]
+    small = [
         bias_query,
         bias_value,
-        w_out,
         bias_out,
         gain_one,
         shift_one,
-        w_up,
-        bias_up,
-        w_down,
         bias_down,
         gain_two,
         shift_two,
-    ) = (
-        lax.all_gather(w_qkv, "fsdp", axis=0, tiled=True),
-        lax.all_gather(bias_query, "fsdp", axis=0, tiled=True),
-        lax.all_gather(bias_value, "fsdp", axis=0, tiled=True),
-        lax.all_gather(w_out, "fsdp", axis=0, tiled=True),
-        lax.all_gather(bias_out, "fsdp", axis=0, tiled=True),
-        lax.all_gather(gain_one, "fsdp", axis=0, tiled=True),
-        lax.all_gather(shift_one, "fsdp", axis=0, tiled=True),
-        lax.all_gather(w_up, "fsdp", axis=0, tiled=True),
-        lax.all_gather(bias_up, "fsdp", axis=0, tiled=True),
-        lax.all_gather(w_down, "fsdp", axis=0, tiled=True),
-        lax.all_gather(bias_down, "fsdp", axis=0, tiled=True),
-        lax.all_gather(gain_two, "fsdp", axis=0, tiled=True),
-        lax.all_gather(shift_two, "fsdp", axis=0, tiled=True),
-    )
-    f32 = jnp.float32
-    bf16 = jnp.bfloat16
-    tokens = hidden[0]
-    tok_rows = tokens.shape[0]
-    model_width = tokens.shape[1]
-    head_count = model_width // HEAD
-    seq_rows = tok_rows * lax.axis_size("ctx")
-    key_span = 4 * tok_rows
-    block_total = seq_rows // key_span
-    doc_ids = segment_ids[0]
-    own_ids = lax.dynamic_slice_in_dim(doc_ids, lax.axis_index("ctx") * tok_rows, tok_rows)
-    mixed_rows = jnp.dot(tokens, w_qkv, preferred_element_type=f32)
-    query_rows = (mixed_rows[:, :model_width] + bias_query.astype(f32)).astype(bf16)
-    key_value = jnp.concatenate(
-        [
-            mixed_rows[:, model_width : 2 * model_width],
-            mixed_rows[:, 2 * model_width :] + bias_value.astype(f32),
-        ],
-        axis=1,
-    ).astype(bf16)
-    all_kv = lax.all_gather(key_value, "ctx", axis=0, tiled=True)
-    query_heads = query_rows.reshape(tok_rows, head_count, HEAD)
-
-    def key_block(block_index):
-        kv_piece = lax.dynamic_slice_in_dim(all_kv, block_index * key_span, key_span, 0)
-        key_ids = lax.dynamic_slice_in_dim(doc_ids, block_index * key_span, key_span)
-        return (
-            kv_piece[:, :model_width].reshape(key_span, head_count, HEAD),
-            kv_piece[:, model_width:].reshape(key_span, head_count, HEAD),
-            key_ids,
-        )
-
-    def forward_step(running, block_index):
-        level_run, total_run, sum_run = running
-        key_heads, value_heads, key_ids = key_block(block_index)
-        allowed = (own_ids[:, None] == key_ids[None, :])[None]
-        scores = jnp.where(allowed, head_scores(query_heads, key_heads), NEGATIVE)
-        level_new = jnp.maximum(level_run, jnp.ceil(jnp.max(scores, axis=-1) * LOG2_E))
-        rescale = jnp.exp(LOG_TWO * (level_run - level_new))
-        unnorm = jnp.where(allowed, jnp.exp(scores - (LOG_TWO * level_new)[..., None]), 0.0)
-        total_new = total_run * rescale + jnp.sum(unnorm, axis=-1)
-        sum_new = sum_run * jnp.transpose(rescale)[:, :, None] + jnp.einsum(
-            "hqk,khd->qhd", unnorm.astype(bf16), value_heads, preferred_element_type=f32
-        )
-        return (level_new, total_new, sum_new)
-
-    start_state = (
-        jnp.full((head_count, tok_rows), NEGATIVE, f32),
-        jnp.zeros((head_count, tok_rows), f32),
-        jnp.zeros((tok_rows, head_count, HEAD), f32),
-    )
-    level_end, row_total, raw_sum = sweep(block_total, forward_step, start_state)
-    row_shift = LOG_TWO * level_end
-    att_sum = raw_sum / jnp.transpose(row_total)[:, :, None]
-    attended = att_sum.reshape(tok_rows, model_width).astype(bf16)
-    branch = jnp.dot(attended, w_out, preferred_element_type=f32) + bias_out.astype(f32)
-    normed_one, norm_one, scale_one = norm_forward(
-        tokens.astype(f32) + branch, gain_one.astype(f32), shift_one.astype(f32)
-    )
-    normed_b = normed_one.astype(bf16)
-    up_rows = jnp.dot(normed_b, w_up, preferred_element_type=f32) + bias_up.astype(f32)
-    active, gelu_back = jax.vjp(lambda pre_act: jax.nn.gelu(pre_act, approximate=False), up_rows)
-    active_b = active.astype(bf16)
-    second = (
-        normed_one + jnp.dot(active_b, w_down, preferred_element_type=f32) + bias_down.astype(f32)
-    )
-    result, norm_two, scale_two = norm_forward(second, gain_two.astype(f32), shift_two.astype(f32))
-    grad_second, grad_gain_two, grad_shift_two = norm_backward(
-        out_grad[0].astype(f32), norm_two, scale_two, gain_two.astype(f32)
-    )
-    grad_ffn = grad_second.astype(bf16)
-    grad_bias_down = column_sums(grad_ffn)
-    grad_active = jnp.dot(grad_ffn, w_down.T, preferred_element_type=f32)
-    grad_up = gelu_back(grad_active)[0].astype(bf16)
-    grad_bias_up = column_sums(grad_up)
-    grad_normed = grad_second + jnp.dot(grad_up, w_up.T, preferred_element_type=f32)
-    grad_first, grad_gain_one, grad_shift_one = norm_backward(
-        grad_normed, norm_one, scale_one, gain_one.astype(f32)
-    )
-    grad_branch = grad_first.astype(bf16)
-    grad_bias_out = column_sums(grad_branch)
-    grad_attended = jnp.dot(grad_branch, w_out.T, preferred_element_type=f32).astype(bf16)
-    grad_att_f32 = grad_attended.reshape(tok_rows, head_count, HEAD).astype(f32)
-    delta = jnp.einsum("qhd,qhd->hq", grad_att_f32, att_sum)
-    delta_ratio = delta / row_total
-    grad_scaled = (grad_att_f32 / jnp.transpose(row_total)[:, :, None]).astype(bf16)
-    zero_query = jnp.zeros((tok_rows, head_count, HEAD), f32)
-
-    def full_step(running, block_index):
-        grad_query, grad_kv = running
-        key_heads, value_heads, key_ids = key_block(block_index)
-        allowed = (own_ids[:, None] == key_ids[None, :])[None]
-        unnorm_b, grad_scores = local_grads(
-            head_scores(query_heads, key_heads),
-            allowed,
-            row_shift,
-            delta_ratio,
-            grad_scaled,
-            value_heads,
-        )
-        grad_query = (
-            grad_query
-            + jnp.einsum("hqk,khd->qhd", grad_scores, key_heads, preferred_element_type=f32) * 0.125
-        )
-        grad_keys = (
-            jnp.einsum("hqk,qhd->khd", grad_scores, query_heads, preferred_element_type=f32) * 0.125
-        )
-        grad_values = jnp.einsum("hqk,qhd->khd", unnorm_b, grad_scaled, preferred_element_type=f32)
-        both_grads = jnp.concatenate(
-            [grad_keys.reshape(key_span, model_width), grad_values.reshape(key_span, model_width)],
-            axis=1,
-        )
-        grad_kv = lax.dynamic_update_slice_in_dim(grad_kv, both_grads, block_index * key_span, 0)
-        return (grad_query, grad_kv)
-
-    start_full = (zero_query, jnp.zeros((seq_rows, 2 * model_width), f32))
-    grad_query, grad_kv = sweep(block_total, full_step, start_full)
-    own_kv = lax.psum_scatter(grad_kv, "ctx", scatter_dimension=0, tiled=True)
-    grad_query_b = grad_query.reshape(tok_rows, model_width).astype(bf16)
-    grad_kv_b = own_kv.astype(bf16)
-    grad_mixed = jnp.concatenate([grad_query_b, grad_kv_b], axis=1)
-    grad_tokens = grad_first + jnp.dot(grad_mixed, w_qkv.T, preferred_element_type=f32)
-    grad_bias_query = column_sums(grad_query_b)
-    grad_bias_value = column_sums(grad_kv_b[:, model_width:])
-    group = lax.axis_index("seq")
-    pick = active_b.reshape(tok_rows, 16, 2, active_b.shape[1] // 32)
-
-    def halves(values):
-        width = values.shape[1] // 2
-        own = lax.dynamic_slice_in_dim(values, group * width, width, 1)
-        return own, lax.dynamic_slice_in_dim(values, (1 - group) * width, width, 1)
-
-    def with_partner(own, sent):
-        return jnp.concatenate([own, lax.ppermute(sent, "seq", [(0, 1), (1, 0)])], axis=0)
-
-    def blocks_of(which):
-        return lax.dynamic_index_in_dim(pick, which, 2, False).reshape(tok_rows, -1)
-
-    a_list = [
-        with_partner(normed_b, normed_b),
-        with_partner(blocks_of(group), blocks_of(1 - group)),
-        with_partner(tokens, tokens),
-        with_partner(attended, attended),
+        bias_up,
     ]
-    b_list = [
-        with_partner(*halves(grad_up)),
-        with_partner(grad_ffn, grad_ffn),
-        with_partner(*halves(grad_mixed)),
-        with_partner(*halves(grad_branch)),
-    ]
+    vec = jnp.concatenate([v.reshape(-1, half) for v in small], axis=0).astype(F32)
+    vec = jnp.pad(vec, ((0, 16 - vec.shape[0]), (0, 0)))
+    (
+        attended,
+        tok_pair,
+        vec_all,
+        w_full,
+        out_other,
+        up_other,
+        down_other,
+        q_heads,
+        k_heads,
+        v_heads,
+        att_full,
+        totals,
+        probs,
+    ) = attend_forward(tok, ids_row, ids_col, vec, w_qkv, w_out, w_up, w_down)
+    (
+        result,
+        normed_b,
+        act_halves,
+        up_halves,
+        grad_ffn,
+        grad_first,
+        branch_halves,
+        att_grads,
+        vec_one,
+    ) = token_local(
+        attended, tok, grad_out, vec_all, w_out, out_other, w_up, up_other, w_down, down_other
+    )
+    (
+        grad_hidden,
+        mixed_halves,
+        vec_two,
+        normed_pair,
+        act_pair,
+        up_pair,
+        ffn_pair,
+        att_pair,
+        branch_pair,
+        mixed_pair,
+    ) = attend_backward(
+        att_grads,
+        q_heads,
+        k_heads,
+        v_heads,
+        att_full,
+        totals,
+        grad_first,
+        probs,
+        w_full,
+        normed_b,
+        act_halves,
+        up_halves,
+        grad_ffn,
+        attended,
+        branch_halves,
+    )
     vectors = [
-        grad_bias_query,
-        grad_bias_value,
-        grad_bias_out,
-        grad_gain_one,
-        grad_shift_one,
-        grad_bias_up,
-        grad_bias_down,
-        grad_gain_two,
-        grad_shift_two,
+        vec_two[0],
+        vec_two[1],
+        vec_one[0],
+        vec_one[1],
+        vec_one[2],
+        vec_one[8:12].reshape(-1),
+        vec_one[3],
+        vec_one[4],
+        vec_one[5],
     ]
     packed = jnp.concatenate([v.reshape(16, -1) for v in vectors], axis=1)
     packed = jnp.pad(packed, ((0, 0), (0, 1024 - packed.shape[1])))
     packed = jnp.transpose(packed.reshape(LINE, 2, 2, 8, 128), (2, 0, 1, 3, 4))
-    up_own, down_own, qkv_own, out_own, vec_own = weight_grads(a_list, b_list, packed)
+    up_own, down_own, qkv_own, out_own, vec_own = weight_grads(
+        [
+            (normed_b, normed_pair, up_halves, up_pair),
+            (act_halves, act_pair, grad_ffn, ffn_pair),
+            (tok, tok_pair, mixed_halves, mixed_pair),
+            (attended, att_pair, branch_halves, branch_pair),
+        ],
+        packed,
+    )
     flat = vec_own.reshape(-1)
     summed, at = [], 0
     for v in vectors:
         summed.append(lax.slice_in_dim(flat, at, at + v.shape[0] // 16))
         at += v.shape[0] // 16
     return (
-        result.astype(bf16)[None],
-        grad_tokens[None],
-        qkv_own.astype(f32),
+        result[None],
+        grad_hidden[None],
+        qkv_own.astype(F32),
         summed[0],
         summed[1],
-        out_own.astype(f32),
+        out_own.astype(F32),
         summed[2],
         summed[3],
         summed[4],
-        up_own.astype(f32),
+        up_own.astype(F32),
         summed[5],
-        down_own.astype(f32),
+        down_own.astype(F32),
         summed[6],
         summed[7],
         summed[8],

time: 464 us -> 210 us (0.45); the launches traced: 455 us -> 210 us
  waiting for transfers between devices: 170 us -> 0 us
  Pallas kernels: 68.4 us -> 180 us
  matrix products: 55.5 us -> 0 us
  local copies, waits for them, and re-layouts: 72.2 us -> 21.3 us
  other arithmetic: 43.3 us -> 7.64 us
  blocking collectives: 16.6 us -> 0 us
  between operations: 15.2 us -> 0.86 us
  starting transfers between devices: 11 us -> 0 us
    pallas_call x0 -> x3, Pallas kernels: none -> 113 us  [the longest x1 54.3 us: attend_backward(): pl.pallas_call(attend_grad_kernel, out_shape=[o[0] for o in outs], in_spe...]
    reduce_scatter x1 -> x0, waiting for transfers between devices: 84.4 us -> none  [block_device(): own_kv = lax.psum_scatter(grad_kv, 'ctx', scatter_dimension=0, tiled=True)]
    all_gather x5 -> x0, waiting for transfers between devices: 67.9 us -> none  [the longest x1 55.3 us: block_device(): all_kv = lax.all_gather(key_value, 'ctx', axis=0, tiled=True)]
    dot_general x22 -> x0, matrix products: 55.5 us -> none  [the longest x1 9.82 us: block_device(): jnp.dot(normed_b, w_up, preferred_element_type=f32) + bias_up.astype(f32)]
    concatenate x12 -> x1, other arithmetic: 20.3 us -> 0.01 us  [block_device(): ids_row = jnp.concatenate([own_ids, far_ids])[None, :]]
    dynamic_update_slice x4 -> x0, local copies, waits for them, and re-layouts: 19.7 us -> none  [full_step(): lax.dynamic_update_slice_in_dim(grad_kv, both_grads, block_index * key_sp...]
    all_gather x9 -> x0, blocking collectives: 16.6 us -> none  [the longest x1 1.96 us: block_device(): lax.all_gather(bias_query, 'fsdp', axis=0, tiled=True)]
    ppermute x8 -> x0, waiting for transfers between devices: 15.1 us -> none  [with_partner(): lax.ppermute(sent, 'seq', [(0, 1), (1, 0)])]
  transfers between devices with their start and end apart: 14 -> 0, of which waited for: 8 -> 0; matrix products, arithmetic and copies ran while one was open for 18% -> 0% of each run, Pallas kernels for 0% -> 0%
where the time goes in v2:
time: 210 us
  Pallas kernels  180 us (86%)
  local copies, waits for them, and re-layouts  21.3 us (10%)
  other arithmetic  7.64 us (4%)
    pallas_call x1, Pallas kernels, weight_grads(): pl.pallas_call(functools.partial(weight_grad_kernel, dims), out_shape=[ja...  66.8 us
    pallas_call x1, Pallas kernels, attend_backward(): pl.pallas_call(attend_grad_kernel, out_shape=[o[0] for o in outs], in_spe...  54.3 us
    pallas_call x1, Pallas kernels, attend_forward(): pl.pallas_call(attend_kernel, out_shape=[o[0] for o in outs], in_specs=[I...  48.4 us
    pallas_call x1, Pallas kernels, token_local(): pl.pallas_call(token_kernel, out_shape=[shape((rows, width), BF16), shape...  10.6 us
    unnamed x40, local copies, waits for them, and re-layouts  10.2 us
    reshape x9, local copies, waits for them, and re-layouts, block_device(): v.reshape(-1, half)  6.16 us

profile of v2, /device:TPU:0, one launch (start us, length us, event | category | flops | bytes accessed | tf_op | source)
XLA Modules:
  0.0 209.8 jit_solution(16234487865503790333)
XLA Ops:
  0.7 0.7 reshape.74
  1.3 0.7 reshape.75
  2.0 0.7 reshape.76
  2.7 0.7 reshape.77
  3.4 0.7 reshape.78
  4.1 0.7 reshape.79
  4.8 0.7 reshape.80
  5.4 0.7 reshape.81
  6.1 0.7 reshape.82
  6.8 0.1 concatenate.10
  6.9 0.7 reduce
  7.6 0.1 reshape_squeeze.27
  7.7 0.1 reshape.72
  7.8 0.1 reshape.73
  7.9 0.2 broadcast_in_dim_reshape.4.ids_col
  8.2 0.0 copy-start
  8.2 1.1 copy-done
  9.2 0.0 copy-start.2
  9.2 0.9 copy-done.2
  10.2 0.0 copy-start.1
  10.2 0.0 copy-start.12
  10.2 48.4 %attend_forward.1 = (bf16[160,768]{1,0:T(8,128)(2,1)S(1)}, bf16[160,768]{1,0:T(8,128)(2,1)S(1)}, f32[16,768]{1,0:T(8,128)S(1)}, bf16[768,2304]{1,0:T(8,128)(2,1)...) custom-call(bf16[160,768]{1,0:T(8,128)(2,1)S(1)} %bitcast.17, ...), custom_call_target="tpu_custom_call" | custom-call | tf_op jit(solution)/shard_map/attend_forward/pallas_call | solution.py:817
  58.6 0.0 copy-start.7
  58.6 0.8 copy-done.7
  59.4 0.8 copy-done.9
  60.2 0.0 copy-start.13
  60.2 0.7 copy-done.13
  60.9 0.0 copy-done.1
  60.9 0.0 copy-done.12
  60.9 10.6 %token_local.1 = (bf16[160,768]{1,0:T(8,128)(2,1)}, bf16[160,768]{1,0:T(8,128)(2,1)S(1)}, bf16[2,160,1536]{2,1,0:T(8,128)(2,1)}, bf16[2,160,1536]{2,1,0:T(8,128)...) custom-call(bf16[160,768]{1,0:T(8,128)(2,1)S(1)} %get-tuple-element., ...), custom_call_target="tpu_custom_call" | custom-call | tf_op jit(solution)/shard_map/token_local/pallas_call | solution.py:967
  71.5 0.0 copy-start.10
  71.5 0.8 copy-done.10
  72.3 0.0 copy-done.3
  72.3 54.3 %attend_backward.1 = (f32[160,768]{1,0:T(8,128)S(1)}, bf16[2,160,1152]{2,1,0:T(8,128)(2,1)}, f32[8,768]{1,0:T(8,128)S(1)}, bf16[160,768]{1,0:T(8,128)(2,1)S(1)},...) custom-call(bf16[4,160,192]{2,1,0:T(8,128)(2,1)S(1)} %get-tuple-elem, ...), custom_call_target="tpu_custom_call" | custom-call | tf_op jit(solution)/shard_map/attend_backward/pallas_call | solution.py:1234
  126.6 0.0 copy-done.4
  126.6 0.0 copy-done.5
  126.6 0.0 copy-done.6
  126.6 0.0 copy-start.8
  126.7 0.8 copy-done.8
  127.4 0.7 copy-done.11
  128.2 0.7 copy-done.14
  128.9 0.7 copy-done.15
  129.6 0.7 copy-done.16
  130.3 0.6 copy-done.17
  131.0 0.1 reshape_squeeze.29
  131.0 0.1 reshape_squeeze.28
  131.1 0.1 slice_reduce_fusion
  131.2 0.1 reshape_squeeze.35
  131.3 0.1 reshape_reshape.3
  131.3 0.1 reshape_squeeze.34
  131.4 0.1 reshape_squeeze.33
  131.5 0.1 reshape_squeeze.32
  131.6 0.1 reshape_squeeze.31
  131.6 0.1 reshape_squeeze.30
  131.7 0.1 concatenate.11
  131.9 0.6 copy.38
  132.5 66.8 %weight_grads.1 = (bf16[48,3072]{1,0:T(8,128)(2,1)}, bf16[192,768]{1,0:T(8,128)(2,1)}, bf16[48,2304]{1,0:T(8,128)(2,1)}, bf16[48,768]{1,0:T(8,128)(2,1)}, f32[8,128]{1,0:T(8,128)}) custom-call(bf16[160,768]{1,0:T(8,128)(2,1)} %copy-done.4, bf16[160,768]{1,0:T(8,128)(2,1)} %copy-done.14, bf16[2,160,1536]{2,1,0:T(8,128)(2,1)} %get-tuple-element.69.up_halves.refs_2_, ...), custom_call_target="tpu_custom_call" | custom-call | tf_op jit(solution)/shard_map/weight_grads/pallas_call | solution.py:530
  199.3 1.3 slice.68
  200.6 1.6 fusion
  202.2 1.6 convert_element_type.18
  203.7 1.7 convert_element_type.17
  205.4 1.8 convert_element_type.19
  207.3 1.8 convert_element_type.20
  209.1 0.8 copy.40
  (19 shorter events, 0.1 us)
Async XLA Ops:
  8.2 1.1 copy-start
  9.2 0.9 copy-start.2
  10.2 50.7 %copy-start.1 = (bf16[384,768]{1,0:T(8,128)(2,1)S(1)}, bf16[384,768]{1,0:T(8,128)(2,1)}, u32[]{:S(2)}) copy-start(bf16[384,768]{1,0:T(8,128)(2,1)} %w_out.3) | copy-start | bytes 1769476
  10.2 50.7 %copy-start.12 = (bf16[1,160,768]{2,1,0:T(8,128)(2,1)S(1)}, bf16[1,160,768]{2,1,0:T(8,128)(2,1)}, u32[]{:S(2)}) copy-start(bf16[1,160,768]{2,1,0:T(8,128)(2,1)} %param.18) | copy-start | bytes 737284
  58.6 0.8 copy-start.7
  59.4 0.8 copy-start.9
  60.2 0.7 copy-start.13
  60.9 11.4 %copy-start.3 = (bf16[160,768]{1,0:T(8,128)(2,1)}, bf16[160,768]{1,0:T(8,128)(2,1)S(1)}, u32[]{:S(2)}) copy-start(bf16[160,768]{1,0:T(8,128)(2,1)S(1)} %get-tuple-element.52.attended.refs_12_) | copy-start | bytes 737284
  71.5 0.8 copy-start.10
  72.2 54.4 %copy-start.4 = (bf16[160,768]{1,0:T(8,128)(2,1)}, bf16[160,768]{1,0:T(8,128)(2,1)S(1)}, u32[]{:S(2)}) copy-start(bf16[160,768]{1,0:T(8,128)(2,1)S(1)} %get-tuple-element.67.normed_b.refs_0_) | copy-start | bytes 737284
  72.2 54.4 %copy-start.5 = (bf16[160,768]{1,0:T(8,128)(2,1)}, bf16[160,768]{1,0:T(8,128)(2,1)S(1)}, u32[]{:S(2)}) copy-start(bf16[160,768]{1,0:T(8,128)(2,1)S(1)} %get-tuple-element.70.grad_ffn.refs_6_) | copy-start | bytes 737284
  72.3 54.4 %copy-start.6 = (bf16[2,160,384]{2,1,0:T(8,128)(2,1)}, bf16[2,160,384]{2,1,0:T(8,128)(2,1)S(1)}, u32[]{:S(2)}) copy-start(bf16[2,160,384]{2,1,0:T(8,128)(2,1)S(1)} %get-tuple-element.71.branch_halves.refs_14_) | copy-start | bytes 737284
  126.6 0.8 copy-start.8
  127.4 0.7 copy-start.11
  128.2 0.7 copy-start.14
  128.9 0.7 copy-start.15
  129.6 0.7 copy-start.16
  130.3 0.6 copy-start.17

commit v3 on v2

--- a/solution.py
+++ b/solution.py
@@ -303,244 +303,6 @@
     )
 
 
-def weight_grad_kernel(dims, *refs):
-    count = len(dims)
-    operands, vec_ref = refs[: 4 * count], refs[4 * count]
-    outs = refs[4 * count + 1 : 5 * count + 1]
-    vec_out = refs[5 * count + 1]
-    rest = refs[5 * count + 2 :]
-    units = count + 1
-    parts, from_core = rest[:units], rest[units : 2 * units]
-    from_pair, from_low = rest[2 * units : 3 * units], rest[3 * units : 4 * units]
-    from_high = rest[4 * units : 5 * units]
-    vec_seq = rest[5 * units]
-    sems = rest[5 * units + 1 :]
-    core_out, core_in, pair_out, pair_in, low_out, low_in, high_out, high_in, seq_out, seq_in = sems
-    place = lax.axis_index("ctx")
-    core = lax.axis_index("fsdp")
-    group = lax.axis_index("seq")
-    line = place // 2
-    side = place % 2
-    to_core = {"fsdp": 1 - core}
-    to_pair = {"ctx": place + 1 - 2 * side}
-    to_seq = {"seq": 1 - group}
-    to_up = {"ctx": lax.rem(place + 2, 2 * LINE)}
-    to_down = {"ctx": lax.rem(place + 2 * LINE - 2, 2 * LINE)}
-    has_low, has_high = line > 0, line < LINE - 1
-
-    barrier = pltpu.get_barrier_semaphore()
-    for target in (to_core, to_pair, to_seq):
-        pl.semaphore_signal(barrier, inc=1, device_id=target, device_id_type=MESH_ID)
-
-    @pl.when(has_high)
-    def _():
-        pl.semaphore_signal(barrier, inc=1, device_id=to_up, device_id_type=MESH_ID)
-
-    @pl.when(has_low)
-    def _():
-        pl.semaphore_signal(barrier, inc=1, device_id=to_down, device_id_type=MESH_ID)
-
-    pl.semaphore_wait(barrier, 3 + has_high.astype(jnp.int32) + has_low.astype(jnp.int32))
-
-    def core_copy(u):
-        return remote(parts[u].at[1 - core], from_core[u], core_out.at[u], core_in.at[u], to_core)
-
-    def pair_copy(u, k):
-        return remote(
-            parts[u].at[core, k, 1 - side],
-            from_pair[u].at[k],
-            pair_out.at[u, k],
-            pair_in.at[u, k],
-            to_pair,
-        )
-
-    def up_copy(u, k):
-        return remote(
-            parts[u].at[core, k, side],
-            from_low[u].at[k - 1],
-            low_out.at[u, k - 1],
-            low_in.at[u, k - 1],
-            to_up,
-        )
-
-    def down_copy(u, k):
-        return remote(
-            parts[u].at[core, k, side],
-            from_high[u].at[k],
-            high_out.at[u, k],
-            high_in.at[u, k],
-            to_down,
-        )
-
-    def seq_copy(u):
-        if u == count:
-            return remote(parts[u].at[core, line, side], vec_seq, seq_out.at[u], seq_in.at[u], to_seq)
-        rows, columns, wide = dims[u]
-        if wide:
-            where = outs[u].at[:, pl.ds(pl.multiple_of(group * columns, 128), columns)]
-        else:
-            where = outs[u].at[pl.ds(pl.multiple_of(group * rows, 16), rows)]
-        return remote(parts[u].at[core, line, side], where, seq_out.at[u], seq_in.at[u], to_seq)
-
-    def multiply(u):
-        if u == count:
-            parts[u][...] = vec_ref[...]
-        else:
-            rows, columns, _ = dims[u]
-            step = 384
-            for first in range(0, columns, step):
-                a_own, a_pair, b_own, b_pair = operands[4 * u : 4 * u + 4]
-                span = slice(first, first + step)
-                own_b = b_own[group, :, span] if len(b_own.shape) == 3 else b_own[:, span]
-                own_a = a_own[group] if len(a_own.shape) == 3 else a_own[...]
-                product = (dot_tn(own_a, own_b) + dot_tn(a_pair[...], b_pair[:, span])).astype(BF16)
-                for j in range(4 * LINE):
-                    parts[u][j % 2, j // 4, (j // 2) % 2, :, first : first + step] = product[
-                        j * rows : (j + 1) * rows
-                    ]
-        core_copy(u).start()
-
-    def add_core(u):
-        core_copy(u).wait_recv()
-        for k in (3, 0, 2, 1):
-            parts[u][core, k, 1 - side] += from_core[u][k, 1 - side]
-            pair_copy(u, k).start()
-        for k in range(LINE):
-            parts[u][core, k, side] += from_core[u][k, side]
-
-    def add_pair(u):
-        for k in (3, 0, 2, 1):
-            pair_copy(u, k).wait_recv()
-            parts[u][core, k, side] += from_pair[u][k]
-
-        @pl.when(line == 0)
-        def _():
-            for k in range(LINE - 1, 0, -1):
-                up_copy(u, k).start()
-
-        @pl.when(line == LINE - 1)
-        def _():
-            for k in range(LINE - 1):
-                down_copy(u, k).start()
-
-    def pass_up(u, k):
-        up_copy(u, k).wait_recv()
-        parts[u][core, k, side] += from_low[u][k - 1]
-        up_copy(u, k).start()
-
-    def pass_down(u, k):
-        down_copy(u, k).wait_recv()
-        parts[u][core, k, side] += from_high[u][k]
-        down_copy(u, k).start()
-
-    def first_hop(u):
-        @pl.when(line == 1)
-        def _():
-            pass_up(u, 3)
-            pass_up(u, 2)
-
-        @pl.when(line == 2)
-        def _():
-            pass_down(u, 0)
-            pass_down(u, 1)
-
-    def second_hop(u):
-        @pl.when(line == 2)
-        def _():
-            pass_up(u, 3)
-
-        @pl.when(line == 1)
-        def _():
-            pass_down(u, 0)
-
-    def finish(u):
-        for k in range(LINE):
-
-            @pl.when(line == k)
-            def _(k=k):
-                if k > 0:
-                    up_copy(u, k).wait_recv()
-                    parts[u][core, k, side] += from_low[u][k - 1]
-                if k < LINE - 1:
-                    down_copy(u, k).wait_recv()
-                    parts[u][core, k, side] += from_high[u][k]
-
-        seq_copy(u).start()
-        if u < count:
-            rows, columns, wide = dims[u]
-            if wide:
-                start = pl.multiple_of(group * columns, 128)
-                outs[u][:, pl.ds(start, columns)] = parts[u][core, line, side]
-            else:
-                start = pl.multiple_of(group * rows, 16)
-                outs[u][pl.ds(start, rows)] = parts[u][core, line, side]
-
-    multiply(0)
-    for u in range(units):
-        if u + 1 < units:
-            multiply(u + 1)
-        add_core(u)
-    for s in range(units + 3):
-        if s < units:
-            add_pair(s)
-        if 0 <= s - 1 < units:
-            first_hop(s - 1)
-        if 0 <= s - 2 < units:
-            second_hop(s - 2)
-        if 0 <= s - 3 < units:
-            finish(s - 3)
-    for u in range(units):
-        seq_copy(u).wait_recv()
-    vec_out[...] = parts[count][core, line, side] + vec_seq[...]
-    for u in range(units):
-        core_copy(u).wait_send()
-        seq_copy(u).wait_send()
-        for k in range(LINE):
-            pair_copy(u, k).wait_send()
-        for k in range(1, LINE):
-
-            @pl.when(line < k)
-            def _(k=k):
-                up_copy(u, k).wait_send()
-
-        for k in range(LINE - 1):
-
-            @pl.when(line > k)
-            def _(k=k):
-                down_copy(u, k).wait_send()
-
-
-def weight_grads(operands, vec):
-    widths = [(group[1].shape[1], group[3].shape[1]) for group in operands]
-    dims, shapes = [], []
-    for a_width, b_width in widths:
-        rows = a_width // (4 * LINE)
-        wide = a_width == widths[0][0]
-        dims.append((rows, b_width, wide))
-        shapes.append((rows, 2 * b_width) if wide else (2 * rows, b_width))
-    blocks = [((rows, columns), jnp.bfloat16) for rows, columns, _ in dims]
-    blocks.append(((8, 128), jnp.float32))
-    units = len(blocks)
-    scratch = []
-    for lead in ((2, LINE, 2), (LINE, 2), (LINE,), (LINE - 1,), (LINE - 1,)):
-        scratch += [pltpu.VMEM(lead + block, kind) for block, kind in blocks]
-    scratch.append(pltpu.VMEM((8, 128), jnp.float32))
-    for lead in ((), (LINE,), (LINE - 1,), (LINE - 1,), ()):
-        scratch += [pltpu.SemaphoreType.DMA((units,) + lead)] * 2
-    return pl.pallas_call(
-        functools.partial(weight_grad_kernel, dims),
-        out_shape=[jax.ShapeDtypeStruct(shape, jnp.bfloat16) for shape in shapes]
-        + [jax.ShapeDtypeStruct((8, 128), jnp.float32)],
-        in_specs=[pl.BlockSpec(memory_space=pltpu.VMEM)] * (4 * len(dims) + 1),
-        out_specs=[pl.BlockSpec(memory_space=pltpu.VMEM)] * (len(dims) + 1),
-        scratch_shapes=scratch,
-        compiler_params=pltpu.CompilerParams(
-            collective_id=0, has_side_effects=True, vmem_limit_bytes=60 << 20
-        ),
-        name="weight_grads",
-    )(*[a for group in operands for a in group], vec)
-
-
 HEADS_OWN = 3
 F32 = jnp.float32
 BF16 = jnp.bfloat16
@@ -569,9 +331,8 @@
 
 def attend_kernel(
     tok,
-    ids_row,
-    ids_col,
-    vec,
+    ids,
+    small,
     w_qkv,
     w_out,
     w_up,
@@ -597,6 +358,9 @@
     att_sent,
     att_land,
     probs,
+    vec,
+    ids_row,
+    ids_col,
     local_sem,
     probs_sem,
     core_out,
@@ -639,6 +403,12 @@
 
     own_load = pltpu.make_async_copy(w_qkv, w_all.at[own_rows], local_sem.at[0])
     own_load.start()
+    at = 0
+    for piece in small:
+        for first in range(0, piece.shape[0], half):
+            vec[at : at + 1] = piece[first : first + half].astype(F32)[None]
+            at += 1
+    vec[at:] = jnp.zeros((vec.shape[0] - at, half), F32)
     greet([to_core, to_pair, to_seq] + [to_line(k) for k in range(1, LINE)])
     core_copies = [
         remote(w_qkv, w_all.at[own_rows], core_out.at[0], core_in.at[0], to_core),
@@ -715,6 +485,12 @@
         pair_copy(k).start()
     seq_rows = 2 * LINE * rows
     mid = LINE * rows
+    for z in range(LINE):
+        even = ids[:, 2 * z * rows : (2 * z + 1) * rows].astype(F32)
+        odd = ids[:, (2 * z + 1) * rows : (2 * z + 2) * rows].astype(F32)
+        ids_row[:, z * rows : (z + 1) * rows] = jnp.where(side == 0, even, odd)
+        ids_row[:, mid + z * rows : mid + (z + 1) * rows] = jnp.where(side == 0, odd, even)
+    ids_col[...] = jnp.transpose(jnp.broadcast_to(ids_row[:, 0:mid], (8, mid)))[:, 0:1]
     for h in range(HEADS_OWN):
         q_heads[h] = mine[:, 2 * third + h * HEAD : 2 * third + (h + 1) * HEAD]
         k_heads[h, 0:mid] = mine[:, h * HEAD : (h + 1) * HEAD]
@@ -793,7 +569,7 @@
     full_store.wait()
 
 
-def attend_forward(tok, ids_row, ids_col, vec, w_qkv, w_out, w_up, w_down):
+def attend_forward(tok, ids, small, w_qkv, w_out, w_up, w_down):
     rows, width = tok.shape
     third = HEADS_OWN * HEAD
     mid, seq_rows = LINE * rows, 2 * LINE * rows
@@ -817,7 +593,7 @@
     return pl.pallas_call(
         attend_kernel,
         out_shape=[o[0] for o in outs],
-        in_specs=[INNER] * 4 + [ANY] * 4,
+        in_specs=[INNER, INNER, [INNER] * len(small)] + [ANY] * 4,
         out_specs=[o[1] for o in outs],
         scratch_shapes=[
             pltpu.VMEM((width, 3 * width), BF16),
@@ -828,6 +604,9 @@
             pltpu.VMEM((LINE, rows, third), BF16),
             pltpu.VMEM((LINE, rows, third), BF16),
             pltpu.VMEM((HEADS_OWN, mid, seq_rows), BF16),
+            pltpu.VMEM((16, width // 2), F32),
+            pltpu.VMEM((1, seq_rows), F32),
+            pltpu.VMEM((mid, 1), F32),
             dma((2,)),
             dma((LINE,)),
             dma((5,)),
@@ -842,10 +621,10 @@
             dma((1,)),
         ],
         compiler_params=pltpu.CompilerParams(
-            collective_id=1, has_side_effects=True, vmem_limit_bytes=50 << 20
+            collective_id=1, has_side_effects=True, vmem_limit_bytes=63 << 20
         ),
         name="attend_forward",
-    )(tok, ids_row, ids_col, vec, w_qkv, w_out, w_up, w_down)
+    )(tok, ids, small, w_qkv, w_out, w_up, w_down)
 
 
 def token_kernel(
@@ -987,12 +766,16 @@
             pltpu.VMEM((rows, units), F32),
             pltpu.SemaphoreType.DMA((6,)),
         ],
-        compiler_params=pltpu.CompilerParams(vmem_limit_bytes=50 << 20),
+        compiler_params=pltpu.CompilerParams(vmem_limit_bytes=63 << 20),
         name="token_local",
     )(attended, tok, grad_out, vec, w_out, out_other, w_up, up_other, w_down, down_other)
 
 
-def attend_grad_kernel(
+UP, DOWN, QKV, OUT, VEC = range(5)
+
+
+def backward_kernel(
+    dims,
     att_grads,
     q_heads,
     k_heads,
@@ -1000,6 +783,7 @@
     att_full,
     totals,
     grad_first,
+    vec_one,
     probs_in,
     w_full,
     normed_b,
@@ -1008,16 +792,14 @@
     grad_ffn,
     attended,
     branch_halves,
+    tok,
+    tok_pair,
     grad_hidden,
-    mixed_halves,
-    vec_grads,
-    normed_pair,
-    act_pair,
-    up_pair,
-    ffn_pair,
-    att_pair,
-    branch_pair,
-    mixed_pair,
+    up_own,
+    down_own,
+    qkv_own,
+    out_own,
+    vec_own,
     w_all,
     probs,
     grad_land,
@@ -1031,6 +813,13 @@
     kv_land,
     query_land,
     mixed,
+    operands,
+    parts,
+    from_core,
+    from_pair,
+    from_low,
+    from_high,
+    vec_seq,
     local_sem,
     line_out,
     line_in,
@@ -1040,15 +829,27 @@
     back_in,
     seq_out,
     seq_in,
+    core_sem,
+    side_sem,
+    low_sem,
+    high_sem,
+    last_sem,
 ):
     place = lax.axis_index("ctx")
+    core = lax.axis_index("fsdp")
     group = lax.axis_index("seq")
     line, side = place // 2, place % 2
+    to_core = {"fsdp": 1 - core}
     to_pair = {"ctx": place + 1 - 2 * side}
     to_seq = {"seq": 1 - group}
+    to_up = {"ctx": lax.rem(place + 2, 2 * LINE)}
+    to_down = {"ctx": lax.rem(place + 2 * LINE - 2, 2 * LINE)}
     rows, width = grad_hidden.shape
     third = HEADS_OWN * HEAD
     mid = LINE * rows
+    middle = 3 * width // 2
+    outs = (up_own, down_own, qkv_own, out_own)
+    units = (UP, DOWN, QKV, OUT, VEC)
 
     def ahead(k):
         return lax.rem(line + k, LINE)
@@ -1061,11 +862,149 @@
 
     def block(which):
         return pl.ds(pl.multiple_of(which * rows, 32), rows)
+
+    own_half = pl.ds(pl.multiple_of(group * middle, 128), middle)
+    far_half = pl.ds(pl.multiple_of((1 - group) * middle, 128), middle)
+
+
+    def core_copy(u):
+        return remote(
+            parts[u].at[1 - core], from_core[u], core_sem.at[0, u], core_sem.at[1, u], to_core
+        )
+
+    def side_copy(u, k):
+        return remote(
+            parts[u].at[core, k, 1 - side],
+            from_pair[u].at[k],
+            side_sem.at[0, u, k],
+            side_sem.at[1, u, k],
+            to_pair,
+        )
+
+    def up_copy(u, k):
+        return remote(
+            parts[u].at[core, k, side],
+            from_low[u].at[k - 1],
+            low_sem.at[0, u, k - 1],
+            low_sem.at[1, u, k - 1],
+            to_up,
+        )
+
+    def down_copy(u, k):
+        return remote(
+            parts[u].at[core, k, side],
+            from_high[u].at[k],
+            high_sem.at[0, u, k],
+            high_sem.at[1, u, k],
+            to_down,
+        )
+
+    def last_copy(u):
+        if u == VEC:
+            where = vec_seq
+        else:
+            size, columns, wide = dims[u]
+            if wide:
+                where = outs[u].at[:, pl.ds(pl.multiple_of(group * columns, 128), columns)]
+            else:
+                where = outs[u].at[pl.ds(pl.multiple_of(group * size, 16), size)]
+        return remote(
+            parts[u].at[core, line, side], where, last_sem.at[0, u], last_sem.at[1, u], to_seq
+        )
+
+    def multiply(u):
+        size, columns, _ = dims[u]
+        a_own, a_pair, b_own, b_pair = operands[u]
+        step = 384
+        for first in range(0, a_own.shape[1], step):
+            span = slice(first, first + step)
+            product = dot_tn(a_own[:, span], b_own[...]) + dot_tn(a_pair[:, span], b_pair[...])
+            product = product.astype(BF16)
+            for i in range(step // size):
+                j = first // size + i
+                parts[u][j % 2, j // 4, (j // 2) % 2] = product[i * size : (i + 1) * size]
+        core_copy(u).start()
+
+    def add_core(u):
+        core_copy(u).wait_recv()
+        for k in (3, 0, 2, 1):
+            parts[u][core, k, 1 - side] += from_core[u][k, 1 - side]
+            side_copy(u, k).start()
+        for k in range(LINE):
+            parts[u][core, k, side] += from_core[u][k, side]
+
+    def add_pair(u):
+        for k in (3, 0, 2, 1):
+            side_copy(u, k).wait_recv()
+            parts[u][core, k, side] += from_pair[u][k]
+
+        @pl.when(line == 0)
+        def _():
+            for k in range(LINE - 1, 0, -1):
+                up_copy(u, k).start()
+
+        @pl.when(line == LINE - 1)
+        def _():
+            for k in range(LINE - 1):
+                down_copy(u, k).start()
+
+    def pass_up(u, k):
+        up_copy(u, k).wait_recv()
+        parts[u][core, k, side] += from_low[u][k - 1]
+        up_copy(u, k).start()
+
+    def pass_down(u, k):
+        down_copy(u, k).wait_recv()
+        parts[u][core, k, side] += from_high[u][k]
+        down_copy(u, k).start()
+
+    def first_hop(u):
+        @pl.when(line == 1)
+        def _():
+            pass_up(u, 3)
+            pass_up(u, 2)
+
+        @pl.when(line == 2)
+        def _():
+            pass_down(u, 0)
+            pass_down(u, 1)
+
+    def second_hop(u):
+        @pl.when(line == 2)
+        def _():
+            pass_up(u, 3)
+
+        @pl.when(line == 1)
+        def _():
+            pass_down(u, 0)
+
+    def finish_unit(u):
+        for k in range(LINE):
+
+            @pl.when(line == k)
+            def _(k=k):
+                if k > 0:
+                    up_copy(u, k).wait_recv()
+                    parts[u][core, k, side] += from_low[u][k - 1]
+                if k < LINE - 1:
+                    down_copy(u, k).wait_recv()
+                    parts[u][core, k, side] += from_high[u][k]
+
+        last_copy(u).start()
+        if u != VEC:
+            size, columns, wide = dims[u]
+            if wide:
+                start = pl.multiple_of(group * columns, 128)
+                outs[u][:, pl.ds(start, columns)] = parts[u][core, line, side]
+            else:
+                start = pl.multiple_of(group * size, 16)
+                outs[u][pl.ds(start, size)] = parts[u][core, line, side]
+
 
     probs_load = pltpu.make_async_copy(probs_in, probs, local_sem.at[0])
     w_load = pltpu.make_async_copy(w_full, w_all, local_sem.at[1])
     probs_load.start()
-    greet([to_pair, to_seq] + [to_line(k) for k in range(1, LINE)])
+    greet([to_core, to_pair, to_seq] + [to_line(k) for k in range(1, LINE)])
 
     def line_copy(k):
         return remote(
@@ -1087,22 +1026,28 @@
 
     for k in (3, 2, 1):
         line_copy(k).start()
-    seq_copies = []
-    for i, (src, dst) in enumerate(
-        (
-            (normed_b, normed_pair),
-            (up_halves.at[1 - group], up_pair),
-            (act_halves.at[1 - group], act_pair),
-            (grad_ffn, ffn_pair),
-            (attended, att_pair),
-            (branch_halves.at[1 - group], branch_pair),
-            (mixed_halves.at[1 - group], mixed_pair),
-        )
-    ):
-        seq_copies.append(remote(src, dst, seq_out.at[i], seq_in.at[i], to_seq))
-    for copy in seq_copies[:-1]:
+    sources = (
+        (normed_b, normed_b, operands[UP][0], operands[UP][1]),
+        (up_halves.at[group], up_halves.at[1 - group], operands[UP][2], operands[UP][3]),
+        (act_halves.at[group], act_halves.at[1 - group], operands[DOWN][0], operands[DOWN][1]),
+        (grad_ffn, grad_ffn, operands[DOWN][2], operands[DOWN][3]),
+        (attended, attended, operands[OUT][0], operands[OUT][1]),
+        (branch_halves.at[group], branch_halves.at[1 - group], operands[OUT][2], operands[OUT][3]),
+    )
+    seq_copies, loads = [], []
+    for i, (own, far, here, there) in enumerate(sources):
+        seq_copies.append(remote(far, there, seq_out.at[i], seq_in.at[i], to_seq))
+        loads.append(pltpu.make_async_copy(own, here, local_sem.at[2 + i]))
+    for copy in seq_copies:
         copy.start()
+    tok_loads = [
+        pltpu.make_async_copy(tok, operands[QKV][0], local_sem.at[8]),
+        pltpu.make_async_copy(tok_pair, operands[QKV][1], local_sem.at[9]),
+    ]
+    mixed_copy = remote(mixed.at[:, far_half], operands[QKV][3], seq_out.at[6], seq_in.at[6], to_seq)
     w_load.start()
+    for load in loads + tok_loads:
+        load.start()
     grad_land[block(line)] = att_grads[line]
     for k in (1, 2, 3):
         line_landed(k).wait_recv()
@@ -1111,10 +1056,10 @@
     def pair_copy(h):
         return remote(kv_sent.at[h], kv_pair.at[h], pair_out.at[h], pair_in.at[h], to_pair)
 
-    for h in range(HEADS_OWN):
+    def head_grads(h):
         lanes = slice(h * HEAD, (h + 1) * HEAD)
 
-        def row_grads(i, carry, h=h, lanes=lanes):
+        def row_grads(i, carry):
             where = block(i)
             incoming = grad_land[where, lanes].astype(F32)
             row_total = totals[where, h : h + 1]
@@ -1172,15 +1117,34 @@
             to_line(k),
         )
 
-    for k in (3, 2, 1):
-        query_back(k).start()
-    query_land[line] = query_grads[block(line)]
-    for h in range(HEADS_OWN):
+    def ready(first, last):
+        for i in range(first, last):
+            seq_copies[i].wait_recv()
+            loads[i].wait()
+
+    def send_kv(h):
         pair_copy(h).wait_recv()
         kv_sum[h] = (kv_own[h] + kv_pair[h].astype(F32)).astype(BF16)
         for k in (3, 2, 1):
             kv_back(h, k).start()
         kv_land[h, line] = kv_sum[h, block(line)]
+
+    head_grads(0)
+    head_grads(1)
+    send_kv(0)
+    ready(0, 2)
+    multiply(UP)
+    head_grads(2)
+    send_kv(1)
+    for k in (3, 2, 1):
+        query_back(k).start()
+    query_land[line] = query_grads[block(line)]
+    ready(2, 4)
+    multiply(DOWN)
+    send_kv(2)
+    add_core(UP)
+    ready(4, 6)
+    multiply(OUT)
     for k in (1, 2, 3):
         query_landed(k).wait_recv()
     for d in range(LINE):
@@ -1192,15 +1156,44 @@
             at = width + d * third + h * HEAD
             mixed[:, at : at + HEAD] = kv_land[h, d, :, 0:HEAD]
             mixed[:, width + at : width + at + HEAD] = kv_land[h, d, :, HEAD:]
-    middle = 3 * width // 2
-    for g in range(2):
-        mixed_halves[g] = mixed[:, g * middle : (g + 1) * middle]
-    seq_copies[-1].start()
+    mixed_copy.start()
+    operands[QKV][2][...] = mixed[:, own_half]
+    add_core(DOWN)
+    parts[VEC][...] = jnp.zeros(parts[VEC].shape, F32)
+    for j in range(4 * LINE):
+        slot = parts[VEC].at[j % 2, j // 4, (j // 2) % 2]
+        size = width // (4 * LINE)
+        slot[0:8, 0:size] = vec_one[0:8, j * size : (j + 1) * size]
+        query_part = mixed[:, j * size : (j + 1) * size].astype(F32)
+        slot[8:9, 0:size] = jnp.sum(query_part, axis=0, keepdims=True)
+        value_part = mixed[:, 2 * width + j * size : 2 * width + (j + 1) * size].astype(F32)
+        slot[9:10, 0:size] = jnp.sum(value_part, axis=0, keepdims=True)
+        at = (j % 4) * 4 * size
+        slot[10:11, 0 : 4 * size] = vec_one[8 + j // 4 : 9 + j // 4, at : at + 4 * size]
     w_load.wait()
     grad_hidden[...] = grad_first[...] + dot_nt(mixed[...], w_all[...])
-    vec_grads[...] = jnp.zeros(vec_grads.shape, F32)
-    vec_grads[0:1] = jnp.sum(mixed[:, :width].astype(F32), axis=0, keepdims=True)
-    vec_grads[1:2] = jnp.sum(mixed[:, 2 * width :].astype(F32), axis=0, keepdims=True)
+    add_core(OUT)
+    mixed_copy.wait_recv()
+    for load in tok_loads:
+        load.wait()
+    multiply(QKV)
+    core_copy(VEC).start()
+    add_pair(UP)
+    add_core(QKV)
+    add_core(VEC)
+    order = (UP, DOWN, OUT, QKV, VEC)
+    for s in range(1, len(order) + 3):
+        if s < len(order):
+            add_pair(order[s])
+        if 0 <= s - 1 < len(order):
+            first_hop(order[s - 1])
+        if 0 <= s - 2 < len(order):
+            second_hop(order[s - 2])
+        if 0 <= s - 3 < len(order):
+            finish_unit(order[s - 3])
+    for u in units:
+        last_copy(u).wait_recv()
+    vec_own[...] = parts[VEC][core, line, side] + vec_seq[...]
     for k in (1, 2, 3):
         line_copy(k).wait_send()
         query_back(k).wait_send()
@@ -1208,49 +1201,67 @@
             kv_back(h, k).wait_send()
     for h in range(HEADS_OWN):
         pair_copy(h).wait_send()
-    for copy in seq_copies:
-        copy.wait()
-
-
-def attend_backward(*args):
+    for copy in seq_copies + [mixed_copy]:
+        copy.wait_send()
+    for u in units:
+        core_copy(u).wait_send()
+        last_copy(u).wait_send()
+        for k in range(LINE):
+            side_copy(u, k).wait_send()
+        for k in range(1, LINE):
+
+            @pl.when(line < k)
+            def _(k=k):
+                up_copy(u, k).wait_send()
+
+        for k in range(LINE - 1):
+
+            @pl.when(line > k)
+            def _(k=k):
+                down_copy(u, k).wait_send()
+
+
+def backward(*args):
     rows, width = args[6].shape
-    units = args[10].shape[2]
+    ffn = args[11].shape[2] * 2
     third = HEADS_OWN * HEAD
     mid, seq_rows = LINE * rows, 2 * LINE * rows
     shape = jax.ShapeDtypeStruct
-    outs = [
-        (shape((rows, width), F32), INNER),
-        (shape((2, rows, 3 * width // 2), BF16), INNER),
-        (shape((8, width), F32), INNER),
-        (shape((rows, width), BF16), ANY),
-        (shape((rows, units), BF16), ANY),
-        (shape((rows, units), BF16), ANY),
-        (shape((rows, width), BF16), ANY),
-        (shape((rows, width), BF16), ANY),
-        (shape((rows, width // 2), BF16), ANY),
-        (shape((rows, 3 * width // 2), BF16), ANY),
-    ]
-    dma = pltpu.SemaphoreType.DMA
+    widths = ((width, ffn // 2), (ffn // 2, width), (width, 3 * width // 2), (width, width // 2))
+    dims = [(a // (4 * LINE), b, a == width) for a, b in widths]
+    own_shapes = [(r, 2 * c) if wide else (2 * r, c) for r, c, wide in dims]
+    blocks = [((r, c), BF16) for r, c, _ in dims] + [((16, 256), F32)]
+    count = len(blocks)
+    vmem, dma = pltpu.VMEM, pltpu.SemaphoreType.DMA
+    outs = [shape((rows, width), F32)] + [shape(own, BF16) for own in own_shapes]
+    outs.append(shape((16, 256), F32))
     return pl.pallas_call(
-        attend_grad_kernel,
-        out_shape=[o[0] for o in outs],
-        in_specs=[INNER] * 7 + [ANY] * 8,
-        out_specs=[o[1] for o in outs],
+        functools.partial(backward_kernel, dims),
+        out_shape=outs,
+        in_specs=[INNER] * 8 + [ANY] * 10,
+        out_specs=[INNER] * len(outs),
         scratch_shapes=[
-            pltpu.VMEM((width, 3 * width), BF16),
-            pltpu.VMEM((HEADS_OWN, mid, seq_rows), BF16),
-            pltpu.VMEM((mid, third), BF16),
-            pltpu.VMEM((mid, HEAD), BF16),
-            pltpu.VMEM((mid, seq_rows), BF16),
-            pltpu.VMEM((mid, third), BF16),
-            pltpu.VMEM((HEADS_OWN, mid, 128), F32),
-            pltpu.VMEM((HEADS_OWN, mid, 128), BF16),
-            pltpu.VMEM((HEADS_OWN, mid, 128), BF16),
-            pltpu.VMEM((HEADS_OWN, mid, 128), BF16),
-            pltpu.VMEM((HEADS_OWN, LINE, rows, 128), BF16),
-            pltpu.VMEM((LINE, rows, third), BF16),
-            pltpu.VMEM((rows, 3 * width), BF16),
-            dma((2,)),
+            vmem((width, 3 * width), BF16),
+            vmem((HEADS_OWN, mid, seq_rows), BF16),
+            vmem((mid, third), BF16),
+            vmem((mid, HEAD), BF16),
+            vmem((mid, seq_rows), BF16),
+            vmem((mid, third), BF16),
+            vmem((HEADS_OWN, mid, 128), F32),
+            vmem((HEADS_OWN, mid, 128), BF16),
+            vmem((HEADS_OWN, mid, 128), BF16),
+            vmem((HEADS_OWN, mid, 128), BF16),
+            vmem((HEADS_OWN, LINE, rows, 128), BF16),
+            vmem((LINE, rows, third), BF16),
+            vmem((rows, 3 * width), BF16),
+            [[vmem((rows, w), BF16) for w in (a, a, b, b)] for a, b in widths],
+            [vmem((2, LINE, 2) + block, kind) for block, kind in blocks],
+            [vmem((LINE, 2) + block, kind) for block, kind in blocks],
+            [vmem((LINE,) + block, kind) for block, kind in blocks],
+            [vmem((LINE - 1,) + block, kind) for block, kind in blocks],
+            [vmem((LINE - 1,) + block, kind) for block, kind in blocks],
+            vmem((16, 256), F32),
+            dma((10,)),
             dma((3,)),
             dma((3,)),
             dma((3,)),
@@ -1259,11 +1270,39 @@
             dma((4, 3)),
             dma((7,)),
             dma((7,)),
+            dma((2, count)),
+            dma((2, count, LINE)),
+            dma((2, count, LINE - 1)),
+            dma((2, count, LINE - 1)),
+            dma((2, count)),
         ],
         compiler_params=pltpu.CompilerParams(
-            collective_id=2, has_side_effects=True, vmem_limit_bytes=50 << 20
+            collective_id=2, has_side_effects=True, vmem_limit_bytes=63 << 20
         ),
-        name="attend_backward",
+        name="backward",
+    )(*args)
+
+
+def finish_kernel(*refs):
+    for i in range(5):
+        refs[6 + i][...] = refs[i][...].astype(F32)
+    vec = refs[5]
+    for i, row in enumerate((8, 9, 0, 1, 2, 3, 4, 5, 10)):
+        out = refs[11 + i]
+        out[...] = vec[row, 0 : out.shape[0]]
+
+
+def finish(*args):
+    shape = jax.ShapeDtypeStruct
+    outs = [shape(a.shape, F32) for a in args[:5]]
+    size = args[2].shape[0]
+    outs += [shape((size,), F32)] * 8 + [shape((4 * size,), F32)]
+    return pl.pallas_call(
+        finish_kernel,
+        out_shape=outs,
+        in_specs=[INNER] * 6,
+        out_specs=[INNER] * len(outs),
+        name="finish",
     )(*args)
 
 
@@ -1286,14 +1325,6 @@
     shift_two,
 ):
     tok, grad_out = hidden[0], out_grad[0]
-    rows, width = tok.shape
-    half = width // 2
-    side = lax.axis_index("ctx") % 2
-    ids = segment_ids[0].reshape(LINE, 2, rows)
-    own_ids = lax.dynamic_index_in_dim(ids, side, 1, False).reshape(-1)
-    far_ids = lax.dynamic_index_in_dim(ids, 1 - side, 1, False).reshape(-1)
-    ids_row = jnp.concatenate([own_ids, far_ids])[None, :]
-    ids_col = own_ids[:, None]
     small = [
         bias_query,
         bias_value,
@@ -1305,8 +1336,6 @@
         shift_two,
         bias_up,
     ]
-    vec = jnp.concatenate([v.reshape(-1, half) for v in small], axis=0).astype(F32)
-    vec = jnp.pad(vec, ((0, 16 - vec.shape[0]), (0, 0)))
     (
         attended,
         tok_pair,
@@ -1321,7 +1350,7 @@
         att_full,
         totals,
         probs,
-    ) = attend_forward(tok, ids_row, ids_col, vec, w_qkv, w_out, w_up, w_down)
+    ) = attend_forward(tok, segment_ids, small, w_qkv, w_out, w_up, w_down)
     (
         result,
         normed_b,
@@ -1335,18 +1364,7 @@
     ) = token_local(
         attended, tok, grad_out, vec_all, w_out, out_other, w_up, up_other, w_down, down_other
     )
-    (
-        grad_hidden,
-        mixed_halves,
-        vec_two,
-        normed_pair,
-        act_pair,
-        up_pair,
-        ffn_pair,
-        att_pair,
-        branch_pair,
-        mixed_pair,
-    ) = attend_backward(
+    grad_hidden, up_own, down_own, qkv_own, out_own, vec_own = backward(
         att_grads,
         q_heads,
         k_heads,
@@ -1354,6 +1372,7 @@
         att_full,
         totals,
         grad_first,
+        vec_one,
         probs,
         w_full,
         normed_b,
@@ -1362,51 +1381,38 @@
         grad_ffn,
         attended,
         branch_halves,
-    )
-    vectors = [
-        vec_two[0],
-        vec_two[1],
-        vec_one[0],
-        vec_one[1],
-        vec_one[2],
-        vec_one[8:12].reshape(-1),
-        vec_one[3],
-        vec_one[4],
-        vec_one[5],
-    ]
-    packed = jnp.concatenate([v.reshape(16, -1) for v in vectors], axis=1)
-    packed = jnp.pad(packed, ((0, 0), (0, 1024 - packed.shape[1])))
-    packed = jnp.transpose(packed.reshape(LINE, 2, 2, 8, 128), (2, 0, 1, 3, 4))
-    up_own, down_own, qkv_own, out_own, vec_own = weight_grads(
-        [
-            (normed_b, normed_pair, up_halves, up_pair),
-            (act_halves, act_pair, grad_ffn, ffn_pair),
-            (tok, tok_pair, mixed_halves, mixed_pair),
-            (attended, att_pair, branch_halves, branch_pair),
-        ],
-        packed,
-    )
-    flat = vec_own.reshape(-1)
-    summed, at = [], 0
-    for v in vectors:
-        summed.append(lax.slice_in_dim(flat, at, at + v.shape[0] // 16))
-        at += v.shape[0] // 16
+        tok,
+        tok_pair,
+    )
+    grads = finish(up_own, down_own, qkv_own, out_own, grad_hidden, vec_own)
+    up_grad, down_grad, qkv_grad, out_grads, grad_hidden = grads[:5]
+    (
+        query_bias,
+        value_bias,
+        out_bias,
+        gain_first,
+        shift_first,
+        down_bias,
+        gain_second,
+        shift_second,
+        up_bias,
+    ) = grads[5:]
     return (
         result[None],
         grad_hidden[None],
-        qkv_own.astype(F32),
-        summed[0],
-        summed[1],
-        out_own.astype(F32),
-        summed[2],
-        summed[3],
-        summed[4],
-        up_own.astype(F32),
-        summed[5],
-        down_own.astype(F32),
-        summed[6],
-        summed[7],
-        summed[8],
+        qkv_grad,
+        query_bias,
+        value_bias,
+        out_grads,
+        out_bias,
+        gain_first,
+        shift_first,
+        up_grad,
+        up_bias,
+        down_grad,
+        down_bias,
+        gain_second,
+        shift_second,
     )
 
 

time: 210 us -> 163 us (0.78)
  local copies, waits for them, and re-layouts: 21.3 us -> 0 us
  Pallas kernels: 180 us -> 162 us
  other arithmetic: 7.64 us -> 0 us
    pallas_call x2, Pallas kernels: 121 us -> 99.6 us  [the longest x1 96.8 us: backward(): pl.pallas_call(functools.partial(backward_kernel, dims), out_shape=outs,...]
    unnamed x40 -> x0, local copies, waits for them, and re-layouts: 10.2 us -> none
    reshape x12 -> x0, local copies, waits for them, and re-layouts: 6.94 us -> none  [the longest x9 6.16 us: block_device(): v.reshape(-1, half)]
    convert_element_type x4 -> x0, other arithmetic: 6.91 us -> none  [the longest x1 1.81 us: block_device(): up_own.astype(F32)]
    slice x5 -> x0, local copies, waits for them, and re-layouts: 2.97 us -> none  [the longest x2 2.89 us: block_device(): summed.append(lax.slice_in_dim(flat, at, at + v.shape[0] // 16))]
where the time goes in v3:
time: 163 us
  Pallas kernels  162 us (99%)
    pallas_call x1, Pallas kernels, backward(): pl.pallas_call(functools.partial(backward_kernel, dims), out_shape=outs,...  96.8 us
    pallas_call x1, Pallas kernels, attend_forward(): pl.pallas_call(attend_kernel, out_shape=[o[0] for o in outs], in_specs=[I...  50.3 us
    pallas_call x1, Pallas kernels, token_local(): pl.pallas_call(token_kernel, out_shape=[shape((rows, width), BF16), shape...  11.9 us

profile of v3, /device:TPU:0, one launch (start us, length us, event | category | flops | bytes accessed | tf_op | source)
XLA Modules:
  0.0 162.6 jit_solution(8029246186259672142)
XLA Ops:
  0.7 50.3 %attend_forward.1 = (bf16[160,768]{1,0:T(8,128)(2,1)}, bf16[160,768]{1,0:T(8,128)(2,1)}, f32[16,768]{1,0:T(8,128)}, bf16[768,2304]{1,0:T(8,128)(2,1)}, bf16[384,...) custom-call(bf16[160,768]{1,0:T(8,128)(2,1)} %bitcast.4, ...), custom_call_target="tpu_custom_call" | custom-call | tf_op jit(solution)/shard_map/attend_forward/pallas_call | solution.py:593
  50.9 11.9 %token_local.1 = (bf16[160,768]{1,0:T(8,128)(2,1)}, bf16[160,768]{1,0:T(8,128)(2,1)}, bf16[2,160,1536]{2,1,0:T(8,128)(2,1)}, bf16[2,160,1536]{2,1,0:T(8,128)(2,1...) custom-call(bf16[160,768]{1,0:T(8,128)(2,1)} %get-tuple-element.57.a, ...), custom_call_target="tpu_custom_call" | custom-call | tf_op jit(solution)/shard_map/token_local/pallas_call | solution.py:746
  62.8 96.8 %backward.1 = (f32[160,768]{1,0:T(8,128)}, bf16[48,3072]{1,0:T(8,128)(2,1)}, bf16[192,768]{1,0:T(8,128)(2,1)}, bf16[48,2304]{1,0:T(8,128)(2,1)}, bf16[48,768]{1,0:T(8,128)(2,1)}, /*index=5*/f32[16,256]{1,0:T(8,128)}) custom-call(bf16[4,160,192]{2,1,0:T(8,128)(2,1)} %get-tuple-element.63.att_grads, bf16[3,640,64]{2,1,0:T(8,128)(2,1)} %get-tuple-element.64.q_heads, ...), custom_call_target="tpu_custom_call" | custom-call | tf_op jit(solution)/shard_map/backward/pallas_call | solution.py:1238
  159.6 2.7 %finish.1 = (f32[48,3072]{1,0:T(8,128)}, f32[192,768]{1,0:T(8,128)}, f32[48,2304]{1,0:T(8,128)}, f32[48,768]{1,0:T(8,128)}, f32[160,768]{1,0:T(8,128)}, /*index=...) custom-call(bf16[48,3072]{1,0:T(8,128)(2,1)} %get-tuple-element.79.r, ...), custom_call_target="tpu_custom_call" | custom-call | tf_op jit(solution)/shard_map/finish/pallas_call | solution.py:1300

commit v4 on v3

--- a/solution.py
+++ b/solution.py
@@ -352,8 +352,10 @@
     probs_out,
     w_all,
     mixed,
-    sent,
+    sent_kv,
+    sent_q,
     mine,
+    mine_q,
     other,
     att_sent,
     att_land,
@@ -398,6 +400,9 @@
     def block(which):
         return pl.ds(pl.multiple_of(which * rows, 32), rows)
 
+    def half_block(which):
+        return pl.ds(pl.multiple_of(which * (rows // 2), 16), rows // 2)
+
     own_rows = pl.ds(pl.multiple_of(core * half, 128), half)
     other_rows = pl.ds(pl.multiple_of((1 - core) * half, 128), half)
 
@@ -432,6 +437,29 @@
     core_copies[1].wait_recv()
     for copy in core_copies[2:]:
         copy.start()
+
+    def kv_copy(k, to):
+        return remote(
+            sent_kv.at[ahead(k)],
+            mine.at[block(to)],
+            line_out.at[0, k - 1],
+            line_in.at[0, k - 1],
+            to_line(k),
+        )
+
+    def q_copy(k, to):
+        return remote(
+            sent_q.at[ahead(k)],
+            mine_q.at[half_block(to)],
+            line_out.at[1, k - 1],
+            line_in.at[1, k - 1],
+            to_line(k),
+        )
+
+    def pair_copy(k):
+        where = block(behind(k))
+        return remote(mine.at[where], other.at[where], pair_out.at[k], pair_in.at[k], to_pair)
+
     bias = vec_all[...]
     for part in (1, 2, 0):
         for first in range(part * width, (part + 1) * width, step):
@@ -444,44 +472,26 @@
             if part == 2:
                 total += bias[1:2, within : within + step]
             total = total.astype(BF16)
-            slot = (2, 0, 1)[part] * third
             for j in range(2):
-                sent[within // third + j, :, slot : slot + third] = total[
-                    :, j * third : (j + 1) * third
-                ]
-
-    def line_copy(k):
-        return remote(
-            sent.at[ahead(k)], mine.at[block(line)], line_out.at[k - 1], line_in.at[k - 1], to_line(k)
-        )
-
-    def line_landed(k):
-        return remote(
-            sent.at[ahead(k)],
-            mine.at[block(behind(k))],
-            line_out.at[k - 1],
-            line_in.at[k - 1],
-            to_line(k),
-        )
-
-    def pair_copy(k):
-        where = block(behind(k))
-        return remote(
-            mine.at[where, 0 : 2 * third],
-            other.at[where],
-            pair_out.at[k],
-            pair_in.at[k],
-            to_pair,
-        )
-
-    for k in (3, 2, 1):
-        line_copy(k).start()
+                d, piece = within // third + j, total[:, j * third : (j + 1) * third]
+                if part == 0:
+                    sent_q[d, :, 0:third] = piece[: rows // 2]
+                    sent_q[d, :, third:] = piece[rows // 2 :]
+                else:
+                    sent_kv[d, :, (part - 1) * third : part * third] = piece
+        for k in (3, 2, 1):
+            if part == 2:
+                kv_copy(k, line).start()
+            if part == 0:
+                q_copy(k, line).start()
+        if part == 2:
+            mine[block(line)] = sent_kv[line]
+            pair_copy(0).start()
     full_store = pltpu.make_async_copy(w_all, w_full, local_sem.at[1])
     full_store.start()
-    mine[block(line)] = sent[line]
-    pair_copy(0).start()
+    mine_q[half_block(line)] = sent_q[line]
     for k in (1, 2, 3):
-        line_landed(k).wait_recv()
+        kv_copy(k, behind(k)).wait_recv()
         pair_copy(k).start()
     seq_rows = 2 * LINE * rows
     mid = LINE * rows
@@ -492,9 +502,15 @@
         ids_row[:, mid + z * rows : mid + (z + 1) * rows] = jnp.where(side == 0, odd, even)
     ids_col[...] = jnp.transpose(jnp.broadcast_to(ids_row[:, 0:mid], (8, mid)))[:, 0:1]
     for h in range(HEADS_OWN):
-        q_heads[h] = mine[:, 2 * third + h * HEAD : 2 * third + (h + 1) * HEAD]
         k_heads[h, 0:mid] = mine[:, h * HEAD : (h + 1) * HEAD]
         v_heads[h, 0:mid] = mine[:, third + h * HEAD : third + (h + 1) * HEAD]
+    for k in (1, 2, 3):
+        q_copy(k, behind(k)).wait_recv()
+    for h in range(HEADS_OWN):
+        for i in range(2 * LINE):
+            from_rows = slice((i // 2) * rows // 2, (i // 2 + 1) * rows // 2)
+            at = (i % 2) * third + h * HEAD
+            q_heads[h, i * rows // 2 : (i + 1) * rows // 2] = mine_q[from_rows, at : at + HEAD]
     for k in range(LINE):
         pair_copy(k).wait_recv()
     for h in range(HEADS_OWN):
@@ -540,7 +556,11 @@
             value = dot_nn(unnorm_b, v_heads[h]) / row_total
             att_full[where, h * HEAD : (h + 1) * HEAD] = value
             totals[where, h : h + 1] = row_total
-            att_sent[which, :, h * HEAD : (h + 1) * HEAD] = value.astype(BF16)
+            value_b = value.astype(BF16)
+            for i in range(2):
+                att_sent[which, :, i * third + h * HEAD : i * third + (h + 1) * HEAD] = value_b[
+                    i * rows // 2 : (i + 1) * rows // 2
+                ]
         probs_copy(k).start()
 
         @pl.when(k < LINE)
@@ -554,9 +574,13 @@
     for k in (1, 2, 3):
         back_landed(k).wait_recv()
     for d in range(LINE):
-        attended[:, d * third : (d + 1) * third] = att_land[d]
+        for i in range(2):
+            attended[i * rows // 2 : (i + 1) * rows // 2, d * third : (d + 1) * third] = att_land[
+                d, :, i * third : (i + 1) * third
+            ]
     for k in (1, 2, 3):
-        line_copy(k).wait_send()
+        kv_copy(k, line).wait_send()
+        q_copy(k, line).wait_send()
         back_copy(k).wait_send()
     for k in range(LINE):
         pair_copy(k).wait_send()
@@ -598,11 +622,13 @@
         scratch_shapes=[
             pltpu.VMEM((width, 3 * width), BF16),
             pltpu.VMEM((rows, 3 * width), F32),
-            pltpu.VMEM((LINE, rows, 3 * third), BF16),
-            pltpu.VMEM((mid, 3 * third), BF16),
+            pltpu.VMEM((LINE, rows, 2 * third), BF16),
+            pltpu.VMEM((LINE, rows // 2, 2 * third), BF16),
             pltpu.VMEM((mid, 2 * third), BF16),
-            pltpu.VMEM((LINE, rows, third), BF16),
-            pltpu.VMEM((LINE, rows, third), BF16),
+            pltpu.VMEM((mid // 2, 2 * third), BF16),
+            pltpu.VMEM((mid, 2 * third), BF16),
+            pltpu.VMEM((LINE, rows // 2, 2 * third), BF16),
+            pltpu.VMEM((LINE, rows // 2, 2 * third), BF16),
             pltpu.VMEM((HEADS_OWN, mid, seq_rows), BF16),
             pltpu.VMEM((16, width // 2), F32),
             pltpu.VMEM((1, seq_rows), F32),
@@ -611,8 +637,8 @@
             dma((LINE,)),
             dma((5,)),
             dma((5,)),
-            dma((3,)),
-            dma((3,)),
+            dma((2, 3)),
+            dma((2, 3)),
             dma((LINE,)),
             dma((LINE,)),
             dma((3,)),
@@ -627,179 +653,52 @@
     )(tok, ids, small, w_qkv, w_out, w_up, w_down)
 
 
-def token_kernel(
+DOWN, UP, OUT, QUERY, KEY, VALUE, VEC = range(7)
+
+
+def backward_kernel(
+    dims,
     attended,
     tok,
     grad_out,
-    vec,
+    vec_in,
     w_out,
     out_other,
     w_up,
     up_other,
     w_down,
     down_other,
+    q_in,
+    k_in,
+    v_in,
+    att_in,
+    totals_in,
+    probs_in,
+    w_full,
+    tok_pair,
     result,
-    normed_o,
-    act_halves,
-    up_halves,
-    ffn_o,
-    first_o,
-    branch_halves,
-    att_grads,
-    vec_grads,
+    grad_hidden,
+    down_own,
+    up_own,
+    qkv_own,
+    out_own,
+    vec_own,
     out_all,
     up_all,
     down_all,
     active,
     slope,
-    sem,
-):
-    core = lax.axis_index("fsdp")
-    rows, width = tok.shape
-    hidden_units = up_all.shape[1]
-    third = HEADS_OWN * HEAD
-
-    def place_of(which, size):
-        return pl.ds(pl.multiple_of(which * size, 128), size)
-
-    loads = []
-    for i, (own, far, full) in enumerate(
-        ((w_out, out_other, out_all), (w_up, up_other, up_all), (w_down, down_other, down_all))
-    ):
-        size = own.shape[0]
-        loads.append(
-            (
-                pltpu.make_async_copy(own, full.at[place_of(core, size)], sem.at[2 * i]),
-                pltpu.make_async_copy(far, full.at[place_of(1 - core, size)], sem.at[2 * i + 1]),
-            )
-        )
-    for pair in loads:
-        for load in pair:
-            load.start()
-
-    def arrived(i):
-        for load in loads[i]:
-            load.wait()
-
-    bias_out, gain_one, shift_one = vec[2:3], vec[3:4], vec[4:5]
-    bias_down, gain_two, shift_two = vec[5:6], vec[6:7], vec[7:8]
-    arrived(0)
-    branch = dot_nn(attended[...], out_all[...]) + bias_out
-    normed_one, norm_one, scale_one = norm_forward(tok[...].astype(F32) + branch, gain_one, shift_one)
-    normed_b = normed_one.astype(BF16)
-    normed_o[...] = normed_b
-    arrived(1)
-    step = width
-    half = width // 2
-    for c in range(hidden_units // step):
-        at, row = (c // 2) * half, 8 + 2 * (c % 2)
-        bias = jnp.concatenate([vec[row : row + 1, at : at + half], vec[row + 1 : row + 2, at : at + half]], axis=1)
-        up = dot_nn(normed_b, up_all[:, c * step : (c + 1) * step]) + bias
-        cdf = 0.5 * (1.0 + lax.erf(up * 0.7071067811865476))
-        active[:, c * step : (c + 1) * step] = (up * cdf).astype(BF16)
-        slope[:, c * step : (c + 1) * step] = cdf + up * (
-            0.3989422804014327 * jnp.exp(-0.5 * up * up)
-        )
-    arrived(2)
-    second = normed_one + bias_down
-    second += dot_nn(active[...], down_all[...])
-    final, norm_two, scale_two = norm_forward(second, gain_two, shift_two)
-    result[...] = final.astype(BF16)
-    grad_second, gain_grad, shift_grad = norm_backward(
-        grad_out[...].astype(F32), norm_two, scale_two, gain_two
-    )
-    grad_ffn = grad_second.astype(BF16)
-    ffn_o[...] = grad_ffn
-    vec_grads[...] = jnp.zeros(vec_grads.shape, F32)
-    vec_grads[3:4] = jnp.sum(grad_ffn.astype(F32), axis=0, keepdims=True)
-    vec_grads[4:5] = gain_grad[None]
-    vec_grads[5:6] = shift_grad[None]
-    grad_normed = grad_second
-    piece = hidden_units // (8 * LINE)
-    for c in range(hidden_units // step):
-        span = slice(c * step, (c + 1) * step)
-        grad_up = (dot_nt(grad_ffn, down_all[span]) * slope[:, span]).astype(BF16)
-        vec_grads[8 + c : 9 + c] = jnp.sum(grad_up.astype(F32), axis=0, keepdims=True)
-        grad_normed += dot_nt(grad_up, up_all[:, span])
-        up_halves[c // 2, :, (c % 2) * step : (c % 2 + 1) * step] = grad_up
-    for j in range(4 * LINE):
-        for g in range(2):
-            at = (2 * j + g) * piece
-            act_halves[g, :, j * piece : (j + 1) * piece] = active[:, at : at + piece]
-    grad_first, gain_grad, shift_grad = norm_backward(grad_normed, norm_one, scale_one, gain_one)
-    first_o[...] = grad_first
-    vec_grads[1:2] = gain_grad[None]
-    vec_grads[2:3] = shift_grad[None]
-    grad_branch = grad_first.astype(BF16)
-    vec_grads[0:1] = jnp.sum(grad_branch.astype(F32), axis=0, keepdims=True)
-    for g in range(2):
-        branch_halves[g] = grad_branch[:, g * half : (g + 1) * half]
-    grad_att = dot_nt(grad_branch, out_all[...]).astype(BF16)
-    for d in range(LINE):
-        att_grads[d] = grad_att[:, d * third : (d + 1) * third]
-
-
-def token_local(attended, tok, grad_out, vec, w_out, out_other, w_up, up_other, w_down, down_other):
-    rows, width = tok.shape
-    units = w_up.shape[1]
-    shape = jax.ShapeDtypeStruct
-    return pl.pallas_call(
-        token_kernel,
-        out_shape=[
-            shape((rows, width), BF16),
-            shape((rows, width), BF16),
-            shape((2, rows, units // 2), BF16),
-            shape((2, rows, units // 2), BF16),
-            shape((rows, width), BF16),
-            shape((rows, width), F32),
-            shape((2, rows, width // 2), BF16),
-            shape((LINE, rows, HEADS_OWN * HEAD), BF16),
-            shape((16, width), F32),
-        ],
-        in_specs=[INNER] * 4 + [ANY] * 6,
-        out_specs=[INNER] * 9,
-        scratch_shapes=[
-            pltpu.VMEM((width, width), BF16),
-            pltpu.VMEM((width, units), BF16),
-            pltpu.VMEM((units, width), BF16),
-            pltpu.VMEM((rows, units), BF16),
-            pltpu.VMEM((rows, units), F32),
-            pltpu.SemaphoreType.DMA((6,)),
-        ],
-        compiler_params=pltpu.CompilerParams(vmem_limit_bytes=63 << 20),
-        name="token_local",
-    )(attended, tok, grad_out, vec, w_out, out_other, w_up, up_other, w_down, down_other)
-
-
-UP, DOWN, QKV, OUT, VEC = range(5)
-
-
-def backward_kernel(
-    dims,
+    first,
+    vec_one,
     att_grads,
+    act_halves,
+    up_halves,
+    branch_halves,
     q_heads,
     k_heads,
     v_heads,
     att_full,
     totals,
-    grad_first,
-    vec_one,
-    probs_in,
-    w_full,
-    normed_b,
-    act_halves,
-    up_halves,
-    grad_ffn,
-    attended,
-    branch_halves,
-    tok,
-    tok_pair,
-    grad_hidden,
-    up_own,
-    down_own,
-    qkv_own,
-    out_own,
-    vec_own,
     w_all,
     probs,
     grad_land,
@@ -813,13 +712,15 @@
     kv_land,
     query_land,
     mixed,
-    operands,
+    left_refs,
+    right_refs,
     parts,
     from_core,
     from_pair,
     from_low,
     from_high,
     vec_seq,
+    sem,
     local_sem,
     line_out,
     line_in,
@@ -847,9 +748,21 @@
     rows, width = grad_hidden.shape
     third = HEADS_OWN * HEAD
     mid = LINE * rows
-    middle = 3 * width // 2
-    outs = (up_own, down_own, qkv_own, out_own)
-    units = (UP, DOWN, QKV, OUT, VEC)
+    half = width // 2
+    hidden_units = active.shape[1]
+    outs = (down_own, up_own, out_own, qkv_own, qkv_own, qkv_own)
+    left = [
+        (act_halves.at[group], left_refs[0]),
+        (left_refs[1], left_refs[2]),
+        (attended, left_refs[3]),
+        (tok, left_refs[4]),
+    ]
+    right = [
+        (right_refs[0], right_refs[1]),
+        (up_halves.at[group], right_refs[2]),
+        (branch_halves.at[group], right_refs[3]),
+    ]
+    units = range(VEC + 1)
 
     def ahead(k):
         return lax.rem(line + k, LINE)
@@ -863,9 +776,23 @@
     def block(which):
         return pl.ds(pl.multiple_of(which * rows, 32), rows)
 
-    own_half = pl.ds(pl.multiple_of(group * middle, 128), middle)
-    far_half = pl.ds(pl.multiple_of((1 - group) * middle, 128), middle)
-
+    def half_block(which):
+        return pl.ds(pl.multiple_of(which * (rows // 2), 16), rows // 2)
+
+    def half_of(part, which):
+        return pl.ds(pl.multiple_of(part * width + which * half, 128), half)
+
+    for part in range(3):
+        right.append((mixed.at[:, half_of(part, group)], right_refs[4 + part]))
+
+
+    def own_place(u):
+        size, columns, wide = dims[u]
+        if not wide:
+            return (pl.ds(pl.multiple_of(group * size, 16), size), slice(None))
+        if u >= QUERY:
+            return (slice(None), half_of(u - QUERY, group))
+        return (slice(None), pl.ds(pl.multiple_of(group * columns, 128), columns))
 
     def core_copy(u):
         return remote(
@@ -903,18 +830,14 @@
         if u == VEC:
             where = vec_seq
         else:
-            size, columns, wide = dims[u]
-            if wide:
-                where = outs[u].at[:, pl.ds(pl.multiple_of(group * columns, 128), columns)]
-            else:
-                where = outs[u].at[pl.ds(pl.multiple_of(group * size, 16), size)]
+            where = outs[u].at[own_place(u)]
         return remote(
             parts[u].at[core, line, side], where, last_sem.at[0, u], last_sem.at[1, u], to_seq
         )
 
     def multiply(u):
         size, columns, _ = dims[u]
-        a_own, a_pair, b_own, b_pair = operands[u]
+        (a_own, a_pair), (b_own, b_pair) = left[min(u, QUERY)], right[u]
         step = 384
         for first in range(0, a_own.shape[1], step):
             span = slice(first, first + step)
@@ -992,24 +915,131 @@
 
         last_copy(u).start()
         if u != VEC:
-            size, columns, wide = dims[u]
-            if wide:
-                start = pl.multiple_of(group * columns, 128)
-                outs[u][:, pl.ds(start, columns)] = parts[u][core, line, side]
-            else:
-                start = pl.multiple_of(group * size, 16)
-                outs[u][pl.ds(start, size)] = parts[u][core, line, side]
-
-
-    probs_load = pltpu.make_async_copy(probs_in, probs, local_sem.at[0])
-    w_load = pltpu.make_async_copy(w_full, w_all, local_sem.at[1])
-    probs_load.start()
+            outs[u][own_place(u)] = parts[u][core, line, side]
+
+
+    seq_copies = []
+    for i, (src, dst) in enumerate(
+        (
+            (act_halves.at[1 - group], left[DOWN][1]),
+            (right[DOWN][0], right[DOWN][1]),
+            (left[UP][0], left[UP][1]),
+            (up_halves.at[1 - group], right[UP][1]),
+            (attended, left[OUT][1]),
+            (branch_halves.at[1 - group], right[OUT][1]),
+        )
+    ):
+        seq_copies.append(remote(src, dst, seq_out.at[i], seq_in.at[i], to_seq))
+
+    def place_of(which, size):
+        return pl.ds(pl.multiple_of(which * size, 128), size)
+
+    loads = []
+    for i, (own, far, full) in enumerate(
+        ((w_out, out_other, out_all), (w_up, up_other, up_all), (w_down, down_other, down_all))
+    ):
+        size = own.shape[0]
+        loads.append(
+            (
+                pltpu.make_async_copy(own, full.at[place_of(core, size)], sem.at[2 * i]),
+                pltpu.make_async_copy(far, full.at[place_of(1 - core, size)], sem.at[2 * i + 1]),
+            )
+        )
+    for pair in loads:
+        for load in pair:
+            load.start()
+    late_loads = []
+    for i, (src, dst) in enumerate(
+        (
+            (q_in, q_heads),
+            (k_in, k_heads),
+            (v_in, v_heads),
+            (att_in, att_full),
+            (totals_in, totals),
+            (probs_in, probs),
+            (w_full, w_all),
+            (tok_pair, left[QUERY][1]),
+        )
+    ):
+        late_loads.append(pltpu.make_async_copy(src, dst, local_sem.at[i]))
+    for load in late_loads:
+        load.start()
     greet([to_core, to_pair, to_seq] + [to_line(k) for k in range(1, LINE)])
+
+    def arrived(i):
+        for load in loads[i]:
+            load.wait()
+
+    bias_out, gain_one, shift_one = vec_in[2:3], vec_in[3:4], vec_in[4:5]
+    bias_down, gain_two, shift_two = vec_in[5:6], vec_in[6:7], vec_in[7:8]
+    arrived(0)
+    branch = dot_nn(attended[...], out_all[...]) + bias_out
+    normed_one, norm_one, scale_one = norm_forward(tok[...].astype(F32) + branch, gain_one, shift_one)
+    normed_b = normed_one.astype(BF16)
+    left[UP][0][...] = normed_b
+    arrived(1)
+    step = width
+    for c in range(hidden_units // step):
+        at, row = (c // 2) * half, 8 + 2 * (c % 2)
+        bias = jnp.concatenate([vec_in[row : row + 1, at : at + half], vec_in[row + 1 : row + 2, at : at + half]], axis=1)
+        up = dot_nn(normed_b, up_all[:, c * step : (c + 1) * step]) + bias
+        cdf = 0.5 * (1.0 + lax.erf(up * 0.7071067811865476))
+        active[:, c * step : (c + 1) * step] = (up * cdf).astype(BF16)
+        slope[:, c * step : (c + 1) * step] = cdf + up * (
+            0.3989422804014327 * jnp.exp(-0.5 * up * up)
+        )
+    piece = hidden_units // (8 * LINE)
+    for j in range(4 * LINE):
+        for g in range(2):
+            at = (2 * j + g) * piece
+            act_halves[g, :, j * piece : (j + 1) * piece] = active[:, at : at + piece]
+    seq_copies[0].start()
+    arrived(2)
+    second = normed_one + bias_down
+    second += dot_nn(active[...], down_all[...])
+    final, norm_two, scale_two = norm_forward(second, gain_two, shift_two)
+    result[...] = final.astype(BF16)
+    grad_second, gain_grad, shift_grad = norm_backward(
+        grad_out[...].astype(F32), norm_two, scale_two, gain_two
+    )
+    grad_ffn = grad_second.astype(BF16)
+    right[DOWN][0][...] = grad_ffn
+    seq_copies[1].start()
+    seq_copies[2].start()
+    vec_one[...] = jnp.zeros(vec_one.shape, F32)
+    vec_one[3:4] = jnp.sum(grad_ffn.astype(F32), axis=0, keepdims=True)
+    vec_one[4:5] = gain_grad[None]
+    vec_one[5:6] = shift_grad[None]
+    grad_normed = grad_second
+    for c in range(hidden_units // step):
+        span = slice(c * step, (c + 1) * step)
+        grad_up = (dot_nt(grad_ffn, down_all[span]) * slope[:, span]).astype(BF16)
+        vec_one[8 + c : 9 + c] = jnp.sum(grad_up.astype(F32), axis=0, keepdims=True)
+        grad_normed += dot_nt(grad_up, up_all[:, span])
+        up_halves[c // 2, :, (c % 2) * step : (c % 2 + 1) * step] = grad_up
+    seq_copies[3].start()
+    seq_copies[4].start()
+    grad_first, gain_grad, shift_grad = norm_backward(grad_normed, norm_one, scale_one, gain_one)
+    first[...] = grad_first
+    vec_one[1:2] = gain_grad[None]
+    vec_one[2:3] = shift_grad[None]
+    grad_branch = grad_first.astype(BF16)
+    vec_one[0:1] = jnp.sum(grad_branch.astype(F32), axis=0, keepdims=True)
+    for g in range(2):
+        branch_halves[g] = grad_branch[:, g * half : (g + 1) * half]
+    seq_copies[5].start()
+    grad_att = dot_nt(grad_branch, out_all[...]).astype(BF16)
+    for d in range(LINE):
+        for i in range(2):
+            att_grads[d, :, i * third : (i + 1) * third] = grad_att[
+                i * rows // 2 : (i + 1) * rows // 2, d * third : (d + 1) * third
+            ]
+
 
     def line_copy(k):
         return remote(
             att_grads.at[ahead(k)],
-            grad_land.at[block(line)],
+            grad_land.at[half_block(line)],
             line_out.at[k - 1],
             line_in.at[k - 1],
             to_line(k),
@@ -1018,7 +1048,7 @@
     def line_landed(k):
         return remote(
             att_grads.at[ahead(k)],
-            grad_land.at[block(behind(k))],
+            grad_land.at[half_block(behind(k))],
             line_out.at[k - 1],
             line_in.at[k - 1],
             to_line(k),
@@ -1026,32 +1056,22 @@
 
     for k in (3, 2, 1):
         line_copy(k).start()
-    sources = (
-        (normed_b, normed_b, operands[UP][0], operands[UP][1]),
-        (up_halves.at[group], up_halves.at[1 - group], operands[UP][2], operands[UP][3]),
-        (act_halves.at[group], act_halves.at[1 - group], operands[DOWN][0], operands[DOWN][1]),
-        (grad_ffn, grad_ffn, operands[DOWN][2], operands[DOWN][3]),
-        (attended, attended, operands[OUT][0], operands[OUT][1]),
-        (branch_halves.at[group], branch_halves.at[1 - group], operands[OUT][2], operands[OUT][3]),
-    )
-    seq_copies, loads = [], []
-    for i, (own, far, here, there) in enumerate(sources):
-        seq_copies.append(remote(far, there, seq_out.at[i], seq_in.at[i], to_seq))
-        loads.append(pltpu.make_async_copy(own, here, local_sem.at[2 + i]))
-    for copy in seq_copies:
-        copy.start()
-    tok_loads = [
-        pltpu.make_async_copy(tok, operands[QKV][0], local_sem.at[8]),
-        pltpu.make_async_copy(tok_pair, operands[QKV][1], local_sem.at[9]),
-    ]
-    mixed_copy = remote(mixed.at[:, far_half], operands[QKV][3], seq_out.at[6], seq_in.at[6], to_seq)
-    w_load.start()
-    for load in loads + tok_loads:
-        load.start()
-    grad_land[block(line)] = att_grads[line]
+    mixed_copies = []
+    for part in range(3):
+        mixed_copies.append(
+            remote(
+                mixed.at[:, half_of(part, 1 - group)],
+                right[QUERY + part][1],
+                seq_out.at[6 + part],
+                seq_in.at[6 + part],
+                to_seq,
+            )
+        )
+    grad_land[half_block(line)] = att_grads[line]
     for k in (1, 2, 3):
         line_landed(k).wait_recv()
-    probs_load.wait()
+    for load in late_loads:
+        load.wait()
 
     def pair_copy(h):
         return remote(kv_sent.at[h], kv_pair.at[h], pair_out.at[h], pair_in.at[h], to_pair)
@@ -1061,7 +1081,9 @@
 
         def row_grads(i, carry):
             where = block(i)
-            incoming = grad_land[where, lanes].astype(F32)
+            packed = grad_land[half_block(i)]
+            far_lanes = slice(third + h * HEAD, third + (h + 1) * HEAD)
+            incoming = jnp.concatenate([packed[:, lanes], packed[:, far_lanes]], axis=0).astype(F32)
             row_total = totals[where, h : h + 1]
             delta = jnp.sum(incoming * att_full[where, lanes], axis=-1, keepdims=True)
             grad_scaled = (incoming / row_total).astype(BF16)
@@ -1069,7 +1091,9 @@
             weights = dot_nt(grad_scaled, v_heads[h])
             ds = (probs[h, where].astype(F32) * (weights - delta / row_total)).astype(BF16)
             score_grads[where] = ds
-            query_grads[where, lanes] = (dot_nn(ds, k_heads[h]) * 0.125).astype(BF16)
+            grad_query = (dot_nn(ds, k_heads[h]) * 0.125).astype(BF16)
+            query_grads[half_block(i), lanes] = grad_query[: rows // 2]
+            query_grads[half_block(i), far_lanes] = grad_query[rows // 2 :]
             return carry
 
         lax.fori_loop(0, LINE, row_grads, 0)
@@ -1083,7 +1107,7 @@
 
     def query_back(k):
         return remote(
-            query_grads.at[block(ahead(k))],
+            query_grads.at[half_block(ahead(k))],
             query_land.at[line],
             back_out.at[HEADS_OWN, k - 1],
             back_in.at[HEADS_OWN, k - 1],
@@ -1092,7 +1116,7 @@
 
     def query_landed(k):
         return remote(
-            query_grads.at[block(ahead(k))],
+            query_grads.at[half_block(ahead(k))],
             query_land.at[behind(k)],
             back_out.at[HEADS_OWN, k - 1],
             back_in.at[HEADS_OWN, k - 1],
@@ -1120,7 +1144,6 @@
     def ready(first, last):
         for i in range(first, last):
             seq_copies[i].wait_recv()
-            loads[i].wait()
 
     def send_kv(h):
         pair_copy(h).wait_recv()
@@ -1130,25 +1153,30 @@
         kv_land[h, line] = kv_sum[h, block(line)]
 
     head_grads(0)
+    ready(0, 2)
+    multiply(DOWN)
     head_grads(1)
     send_kv(0)
-    ready(0, 2)
-    multiply(UP)
+    add_core(DOWN)
     head_grads(2)
-    send_kv(1)
     for k in (3, 2, 1):
         query_back(k).start()
-    query_land[line] = query_grads[block(line)]
+    query_land[line] = query_grads[half_block(line)]
+    send_kv(1)
     ready(2, 4)
-    multiply(DOWN)
+    multiply(UP)
     send_kv(2)
+    for k in (1, 2, 3):
+        query_landed(k).wait_recv()
+    for d in range(LINE):
+        for i in range(2):
+            mixed[i * rows // 2 : (i + 1) * rows // 2, d * third : (d + 1) * third] = query_land[
+                d, :, i * third : (i + 1) * third
+            ]
+    mixed_copies[0].start()
     add_core(UP)
     ready(4, 6)
     multiply(OUT)
-    for k in (1, 2, 3):
-        query_landed(k).wait_recv()
-    for d in range(LINE):
-        mixed[:, d * third : (d + 1) * third] = query_land[d]
     for h in range(HEADS_OWN):
         for k in (1, 2, 3):
             kv_landed(h, k).wait_recv()
@@ -1156,9 +1184,13 @@
             at = width + d * third + h * HEAD
             mixed[:, at : at + HEAD] = kv_land[h, d, :, 0:HEAD]
             mixed[:, width + at : width + at + HEAD] = kv_land[h, d, :, HEAD:]
-    mixed_copy.start()
-    operands[QKV][2][...] = mixed[:, own_half]
-    add_core(DOWN)
+    for part in (1, 2):
+        mixed_copies[part].start()
+    add_pair(DOWN)
+    mixed_copies[0].wait_recv()
+    multiply(QUERY)
+    add_core(OUT)
+    first_hop(DOWN)
     parts[VEC][...] = jnp.zeros(parts[VEC].shape, F32)
     for j in range(4 * LINE):
         slot = parts[VEC].at[j % 2, j // 4, (j // 2) % 2]
@@ -1170,27 +1202,26 @@
         slot[9:10, 0:size] = jnp.sum(value_part, axis=0, keepdims=True)
         at = (j % 4) * 4 * size
         slot[10:11, 0 : 4 * size] = vec_one[8 + j // 4 : 9 + j // 4, at : at + 4 * size]
-    w_load.wait()
-    grad_hidden[...] = grad_first[...] + dot_nt(mixed[...], w_all[...])
-    add_core(OUT)
-    mixed_copy.wait_recv()
-    for load in tok_loads:
-        load.wait()
-    multiply(QKV)
     core_copy(VEC).start()
+    for part in (1, 2):
+        mixed_copies[part].wait_recv()
+        multiply(QUERY + part)
+    add_core(QUERY)
+    second_hop(DOWN)
+    add_core(KEY)
+    add_core(VALUE)
+    add_core(VEC)
+    grad_hidden[...] = first[...] + dot_nt(mixed[...], w_all[...])
     add_pair(UP)
-    add_core(QKV)
-    add_core(VEC)
-    order = (UP, DOWN, OUT, QKV, VEC)
-    for s in range(1, len(order) + 3):
-        if s < len(order):
-            add_pair(order[s])
-        if 0 <= s - 1 < len(order):
-            first_hop(order[s - 1])
-        if 0 <= s - 2 < len(order):
-            second_hop(order[s - 2])
-        if 0 <= s - 3 < len(order):
-            finish_unit(order[s - 3])
+    for s in range(2, VEC + 4):
+        if s <= VEC:
+            add_pair(s)
+        if 1 <= s - 1 <= VEC:
+            first_hop(s - 1)
+        if 1 <= s - 2 <= VEC:
+            second_hop(s - 2)
+        if s - 3 <= VEC and s >= 3:
+            finish_unit(s - 3)
     for u in units:
         last_copy(u).wait_recv()
     vec_own[...] = parts[VEC][core, line, side] + vec_seq[...]
@@ -1201,7 +1232,7 @@
             kv_back(h, k).wait_send()
     for h in range(HEADS_OWN):
         pair_copy(h).wait_send()
-    for copy in seq_copies + [mixed_copy]:
+    for copy in seq_copies + mixed_copies:
         copy.wait_send()
     for u in units:
         core_copy(u).wait_send()
@@ -1222,54 +1253,74 @@
 
 
 def backward(*args):
-    rows, width = args[6].shape
-    ffn = args[11].shape[2] * 2
+    rows, width = args[1].shape
+    ffn = args[6].shape[1]
     third = HEADS_OWN * HEAD
     mid, seq_rows = LINE * rows, 2 * LINE * rows
     shape = jax.ShapeDtypeStruct
-    widths = ((width, ffn // 2), (ffn // 2, width), (width, 3 * width // 2), (width, width // 2))
+    widths = ((ffn // 2, width), (width, ffn // 2)) + ((width, width // 2),) * 4
     dims = [(a // (4 * LINE), b, a == width) for a, b in widths]
-    own_shapes = [(r, 2 * c) if wide else (2 * r, c) for r, c, wide in dims]
+    own_shapes = [(r, 2 * c) if wide else (2 * r, c) for r, c, wide in dims[: OUT + 1]]
+    own_shapes.insert(OUT, (own_shapes[UP][0], 3 * width))
     blocks = [((r, c), BF16) for r, c, _ in dims] + [((16, 256), F32)]
     count = len(blocks)
     vmem, dma = pltpu.VMEM, pltpu.SemaphoreType.DMA
-    outs = [shape((rows, width), F32)] + [shape(own, BF16) for own in own_shapes]
+    outs = [shape((rows, width), BF16), shape((rows, width), F32)]
+    outs += [shape(own, BF16) for own in own_shapes]
     outs.append(shape((16, 256), F32))
     return pl.pallas_call(
         functools.partial(backward_kernel, dims),
         out_shape=outs,
-        in_specs=[INNER] * 8 + [ANY] * 10,
+        in_specs=[INNER] * 4 + [ANY] * 14,
         out_specs=[INNER] * len(outs),
         scratch_shapes=[
+            vmem((width, width), BF16),
+            vmem((width, ffn), BF16),
+            vmem((ffn, width), BF16),
+            vmem((rows, ffn), BF16),
+            vmem((rows, ffn), F32),
+            vmem((rows, width), F32),
+            vmem((16, width), F32),
+            vmem((LINE, rows // 2, 2 * third), BF16),
+            vmem((2, rows, ffn // 2), BF16),
+            vmem((2, rows, ffn // 2), BF16),
+            vmem((2, rows, width // 2), BF16),
+            vmem((HEADS_OWN, mid, HEAD), BF16),
+            vmem((HEADS_OWN, seq_rows, HEAD), BF16),
+            vmem((HEADS_OWN, seq_rows, HEAD), BF16),
+            vmem((mid, third), F32),
+            vmem((mid, 128), F32),
             vmem((width, 3 * width), BF16),
             vmem((HEADS_OWN, mid, seq_rows), BF16),
-            vmem((mid, third), BF16),
+            vmem((mid // 2, 2 * third), BF16),
             vmem((mid, HEAD), BF16),
             vmem((mid, seq_rows), BF16),
-            vmem((mid, third), BF16),
+            vmem((mid // 2, 2 * third), BF16),
             vmem((HEADS_OWN, mid, 128), F32),
             vmem((HEADS_OWN, mid, 128), BF16),
             vmem((HEADS_OWN, mid, 128), BF16),
             vmem((HEADS_OWN, mid, 128), BF16),
             vmem((HEADS_OWN, LINE, rows, 128), BF16),
-            vmem((LINE, rows, third), BF16),
+            vmem((LINE, rows // 2, 2 * third), BF16),
             vmem((rows, 3 * width), BF16),
-            [[vmem((rows, w), BF16) for w in (a, a, b, b)] for a, b in widths],
+            [vmem((rows, a), BF16) for a in (ffn // 2, width, width, width, width)],
+            [vmem((rows, b), BF16) for b in (width, width, ffn // 2) + (width // 2,) * 4],
             [vmem((2, LINE, 2) + block, kind) for block, kind in blocks],
             [vmem((LINE, 2) + block, kind) for block, kind in blocks],
             [vmem((LINE,) + block, kind) for block, kind in blocks],
             [vmem((LINE - 1,) + block, kind) for block, kind in blocks],
             [vmem((LINE - 1,) + block, kind) for block, kind in blocks],
             vmem((16, 256), F32),
-            dma((10,)),
+            dma((6,)),
+            dma((8,)),
             dma((3,)),
             dma((3,)),
             dma((3,)),
             dma((3,)),
             dma((4, 3)),
             dma((4, 3)),
-            dma((7,)),
-            dma((7,)),
+            dma((9,)),
+            dma((9,)),
             dma((2, count)),
             dma((2, count, LINE)),
             dma((2, count, LINE - 1)),
@@ -1284,23 +1335,23 @@
 
 
 def finish_kernel(*refs):
-    for i in range(5):
-        refs[6 + i][...] = refs[i][...].astype(F32)
-    vec = refs[5]
+    for i in range(6):
+        refs[7 + i][...] = refs[i][...].astype(refs[7 + i].dtype)
+    vec = refs[6]
     for i, row in enumerate((8, 9, 0, 1, 2, 3, 4, 5, 10)):
-        out = refs[11 + i]
+        out = refs[13 + i]
         out[...] = vec[row, 0 : out.shape[0]]
 
 
 def finish(*args):
     shape = jax.ShapeDtypeStruct
-    outs = [shape(a.shape, F32) for a in args[:5]]
+    outs = [shape(a.shape, F32) for a in args[:5]] + [shape(args[5].shape, BF16)]
     size = args[2].shape[0]
     outs += [shape((size,), F32)] * 8 + [shape((4 * size,), F32)]
     return pl.pallas_call(
         finish_kernel,
         out_shape=outs,
-        in_specs=[INNER] * 6,
+        in_specs=[INNER] * 7,
         out_specs=[INNER] * len(outs),
         name="finish",
     )(*args)
@@ -1351,41 +1402,28 @@
         totals,
         probs,
     ) = attend_forward(tok, segment_ids, small, w_qkv, w_out, w_up, w_down)
-    (
-        result,
-        normed_b,
-        act_halves,
-        up_halves,
-        grad_ffn,
-        grad_first,
-        branch_halves,
-        att_grads,
-        vec_one,
-    ) = token_local(
-        attended, tok, grad_out, vec_all, w_out, out_other, w_up, up_other, w_down, down_other
-    )
-    grad_hidden, up_own, down_own, qkv_own, out_own, vec_own = backward(
-        att_grads,
+    result, grad_hidden, down_own, up_own, qkv_own, out_own, vec_own = backward(
+        attended,
+        tok,
+        grad_out,
+        vec_all,
+        w_out,
+        out_other,
+        w_up,
+        up_other,
+        w_down,
+        down_other,
         q_heads,
         k_heads,
         v_heads,
         att_full,
         totals,
-        grad_first,
-        vec_one,
         probs,
         w_full,
-        normed_b,
-        act_halves,
-        up_halves,
-        grad_ffn,
-        attended,
-        branch_halves,
-        tok,
         tok_pair,
     )
-    grads = finish(up_own, down_own, qkv_own, out_own, grad_hidden, vec_own)
-    up_grad, down_grad, qkv_grad, out_grads, grad_hidden = grads[:5]
+    grads = finish(up_own, down_own, qkv_own, out_own, grad_hidden, result, vec_own)
+    up_grad, down_grad, qkv_grad, out_grads, grad_hidden, result = grads[:6]
     (
         query_bias,
         value_bias,
@@ -1396,7 +1434,7 @@
         gain_second,
         shift_second,
         up_bias,
-    ) = grads[5:]
+    ) = grads[6:]
     return (
         result[None],
         grad_hidden[None],

time: 163 us -> 150 us (0.920)
  Pallas kernels: 162 us -> 149 us
    pallas_call x2 -> x1, Pallas kernels: 14.6 us -> 2.98 us  [finish(): pl.pallas_call(finish_kernel, out_shape=outs, in_specs=[INNER] * 7, out_s...]
    pallas_call x1, Pallas kernels: 50.3 us -> 45.6 us  [attend_forward(): pl.pallas_call(attend_kernel, out_shape=[o[0] for o in outs], in_specs=[I...]
    pallas_call x1, Pallas kernels: 96.8 us -> 100 us  [backward(): pl.pallas_call(functools.partial(backward_kernel, dims), out_shape=outs,...]
where the time goes in v4:
time: 150 us
  Pallas kernels  149 us (99%)
    pallas_call x1, Pallas kernels, backward(): pl.pallas_call(functools.partial(backward_kernel, dims), out_shape=outs,...  100 us
    pallas_call x1, Pallas kernels, attend_forward(): pl.pallas_call(attend_kernel, out_shape=[o[0] for o in outs], in_specs=[I...  45.6 us

profile of v4, /device:TPU:0, one launch (start us, length us, event | category | flops | bytes accessed | tf_op | source)
XLA Modules:
  0.0 149.6 jit_solution(14812282874343975987)
XLA Ops:
  0.6 45.6 %attend_forward.1 = (bf16[160,768]{1,0:T(8,128)(2,1)}, bf16[160,768]{1,0:T(8,128)(2,1)}, f32[16,768]{1,0:T(8,128)}, bf16[768,2304]{1,0:T(8,128)(2,1)}, bf16[384,...) custom-call(bf16[160,768]{1,0:T(8,128)(2,1)} %bitcast.4, ...), custom_call_target="tpu_custom_call" | custom-call | tf_op jit(solution)/shard_map/attend_forward/pallas_call | solution.py:617
  46.2 100.3 %backward.1 = (bf16[160,768]{1,0:T(8,128)(2,1)}, f32[160,768]{1,0:T(8,128)}, bf16[192,768]{1,0:T(8,128)(2,1)}, bf16[48,3072]{1,0:T(8,128)(2,1)}, bf16[48,2304]{1...) custom-call(bf16[160,768]{1,0:T(8,128)(2,1)} %get-tuple-element.50.attended, bf16[160,768]{1,0:T(8,128)(2,1)} %bitcast.5, ...), custom_call_target="tpu_custom_call" | custom-call | tf_op jit(solution)/shard_map/backward/pallas_call | solution.py:1271
  146.5 3.0 %finish.1 = (f32[48,3072]{1,0:T(8,128)}, f32[192,768]{1,0:T(8,128)}, f32[48,2304]{1,0:T(8,128)}, f32[48,768]{1,0:T(8,128)}, f32[160,768]{1,0:T(8,128)}, /*index=...) custom-call(bf16[48,3072]{1,0:T(8,128)(2,1)} %get-tuple-element.63.r, ...), custom_call_target="tpu_custom_call" | custom-call | tf_op jit(solution)/shard_map/finish/pallas_call | solution.py:1351

commit v5 on v4

--- a/solution.py
+++ b/solution.py
@@ -653,7 +653,7 @@
     )(tok, ids, small, w_qkv, w_out, w_up, w_down)
 
 
-DOWN, UP, OUT, QUERY, KEY, VALUE, VEC = range(7)
+DOWN, DOWN_B, UP, UP_B, OUT, QUERY, KEY, VALUE, VEC = range(9)
 
 
 def backward_kernel(
@@ -750,20 +750,23 @@
     mid = LINE * rows
     half = width // 2
     hidden_units = active.shape[1]
-    outs = (down_own, up_own, out_own, qkv_own, qkv_own, qkv_own)
+    outs = (down_own, down_own, up_own, up_own, out_own, qkv_own, qkv_own, qkv_own)
     left = [
         (act_halves.at[group], left_refs[0]),
         (left_refs[1], left_refs[2]),
         (attended, left_refs[3]),
         (tok, left_refs[4]),
     ]
-    right = [
-        (right_refs[0], right_refs[1]),
-        (up_halves.at[group], right_refs[2]),
-        (branch_halves.at[group], right_refs[3]),
-    ]
+    grad_ffn_own, grad_ffn_pair, up_pair, branch_pair = right_refs[:4]
+    right = []
+    for i in range(2):
+        lanes = slice(i * half, (i + 1) * half)
+        right.append((grad_ffn_own.at[:, lanes], grad_ffn_pair.at[:, lanes]))
+    for i in range(2):
+        lanes = slice(i * width, (i + 1) * width)
+        right.append((up_halves.at[group, :, lanes], up_pair.at[:, lanes]))
+    right.append((branch_halves.at[group], branch_pair))
     units = range(VEC + 1)
-
     def ahead(k):
         return lax.rem(line + k, LINE)
 
@@ -789,10 +792,14 @@
     def own_place(u):
         size, columns, wide = dims[u]
         if not wide:
-            return (pl.ds(pl.multiple_of(group * size, 16), size), slice(None))
+            lanes = slice((u - DOWN) * columns, (u - DOWN + 1) * columns)
+            return (pl.ds(pl.multiple_of(group * size, 16), size), lanes)
         if u >= QUERY:
             return (slice(None), half_of(u - QUERY, group))
-        return (slice(None), pl.ds(pl.multiple_of(group * columns, 128), columns))
+        if u == OUT:
+            return (slice(None), half_of(0, group))
+        start = pl.multiple_of((2 * group + u - UP) * columns, 128)
+        return (slice(None), pl.ds(start, columns))
 
     def core_copy(u):
         return remote(
@@ -837,7 +844,7 @@
 
     def multiply(u):
         size, columns, _ = dims[u]
-        (a_own, a_pair), (b_own, b_pair) = left[min(u, QUERY)], right[u]
+        (a_own, a_pair), (b_own, b_pair) = left[(0, 0, 1, 1, 2, 3, 3, 3)[u]], right[u]
         step = 384
         for first in range(0, a_own.shape[1], step):
             span = slice(first, first + step)
@@ -848,6 +855,17 @@
                 parts[u][j % 2, j // 4, (j // 2) % 2] = product[i * size : (i + 1) * size]
         core_copy(u).start()
 
+    def line_start(u):
+        @pl.when(line == 0)
+        def _():
+            for k in range(LINE - 1, 0, -1):
+                up_copy(u, k).start()
+
+        @pl.when(line == LINE - 1)
+        def _():
+            for k in range(LINE - 1):
+                down_copy(u, k).start()
+
     def add_core(u):
         core_copy(u).wait_recv()
         for k in (3, 0, 2, 1):
@@ -860,16 +878,7 @@
         for k in (3, 0, 2, 1):
             side_copy(u, k).wait_recv()
             parts[u][core, k, side] += from_pair[u][k]
-
-        @pl.when(line == 0)
-        def _():
-            for k in range(LINE - 1, 0, -1):
-                up_copy(u, k).start()
-
-        @pl.when(line == LINE - 1)
-        def _():
-            for k in range(LINE - 1):
-                down_copy(u, k).start()
+        line_start(u)
 
     def pass_up(u, k):
         up_copy(u, k).wait_recv()
@@ -901,7 +910,7 @@
         def _():
             pass_down(u, 0)
 
-    def finish_unit(u):
+    def line_end(u):
         for k in range(LINE):
 
             @pl.when(line == k)
@@ -913,20 +922,33 @@
                     down_copy(u, k).wait_recv()
                     parts[u][core, k, side] += from_high[u][k]
 
+    def last_start(u):
         last_copy(u).start()
         if u != VEC:
             outs[u][own_place(u)] = parts[u][core, line, side]
 
+    def stage(u, n):
+        if n == 1:
+            add_pair(u)
+        if n == 2:
+            first_hop(u)
+        if n == 3:
+            second_hop(u)
+        if n == 4:
+            line_end(u)
+            last_start(u)
+
 
     seq_copies = []
     for i, (src, dst) in enumerate(
         (
-            (act_halves.at[1 - group], left[DOWN][1]),
-            (right[DOWN][0], right[DOWN][1]),
-            (left[UP][0], left[UP][1]),
-            (up_halves.at[1 - group], right[UP][1]),
-            (attended, left[OUT][1]),
-            (branch_halves.at[1 - group], right[OUT][1]),
+            (left[1][0], left[1][1]),
+            (act_halves.at[1 - group], left[0][1]),
+            (grad_ffn_own, grad_ffn_pair),
+            (up_halves.at[1 - group, :, 0:width], up_pair.at[:, 0:width]),
+            (up_halves.at[1 - group, :, width:], up_pair.at[:, width:]),
+            (branch_halves.at[1 - group], branch_pair),
+            (attended, left[2][1]),
         )
     ):
         seq_copies.append(remote(src, dst, seq_out.at[i], seq_in.at[i], to_seq))
@@ -958,7 +980,7 @@
             (totals_in, totals),
             (probs_in, probs),
             (w_full, w_all),
-            (tok_pair, left[QUERY][1]),
+            (tok_pair, left[3][1]),
         )
     ):
         late_loads.append(pltpu.make_async_copy(src, dst, local_sem.at[i]))
@@ -976,7 +998,8 @@
     branch = dot_nn(attended[...], out_all[...]) + bias_out
     normed_one, norm_one, scale_one = norm_forward(tok[...].astype(F32) + branch, gain_one, shift_one)
     normed_b = normed_one.astype(BF16)
-    left[UP][0][...] = normed_b
+    left[1][0][...] = normed_b
+    seq_copies[0].start()
     arrived(1)
     step = width
     for c in range(hidden_units // step):
@@ -993,7 +1016,7 @@
         for g in range(2):
             at = (2 * j + g) * piece
             act_halves[g, :, j * piece : (j + 1) * piece] = active[:, at : at + piece]
-    seq_copies[0].start()
+    seq_copies[1].start()
     arrived(2)
     second = normed_one + bias_down
     second += dot_nn(active[...], down_all[...])
@@ -1003,8 +1026,7 @@
         grad_out[...].astype(F32), norm_two, scale_two, gain_two
     )
     grad_ffn = grad_second.astype(BF16)
-    right[DOWN][0][...] = grad_ffn
-    seq_copies[1].start()
+    grad_ffn_own[...] = grad_ffn
     seq_copies[2].start()
     vec_one[...] = jnp.zeros(vec_one.shape, F32)
     vec_one[3:4] = jnp.sum(grad_ffn.astype(F32), axis=0, keepdims=True)
@@ -1028,6 +1050,7 @@
     for g in range(2):
         branch_halves[g] = grad_branch[:, g * half : (g + 1) * half]
     seq_copies[5].start()
+    seq_copies[6].start()
     grad_att = dot_nt(grad_branch, out_all[...]).astype(BF16)
     for d in range(LINE):
         for i in range(2):
@@ -1062,8 +1085,8 @@
             remote(
                 mixed.at[:, half_of(part, 1 - group)],
                 right[QUERY + part][1],
-                seq_out.at[6 + part],
-                seq_in.at[6 + part],
+                seq_out.at[7 + part],
+                seq_in.at[7 + part],
                 to_seq,
             )
         )
@@ -1152,10 +1175,46 @@
             kv_back(h, k).start()
         kv_land[h, line] = kv_sum[h, block(line)]
 
+    def query_done():
+        for k in (1, 2, 3):
+            query_landed(k).wait_recv()
+        for d in range(LINE):
+            for i in range(2):
+                mixed[i * rows // 2 : (i + 1) * rows // 2, d * third : (d + 1) * third] = query_land[
+                    d, :, i * third : (i + 1) * third
+                ]
+        mixed_copies[0].start()
+
+    def kv_done():
+        for h in range(HEADS_OWN):
+            for k in (1, 2, 3):
+                kv_landed(h, k).wait_recv()
+            for d in range(LINE):
+                at = width + d * third + h * HEAD
+                mixed[:, at : at + HEAD] = kv_land[h, d, :, 0:HEAD]
+                mixed[:, width + at : width + at + HEAD] = kv_land[h, d, :, HEAD:]
+        for part in (1, 2):
+            mixed_copies[part].start()
+
+    def pack_vectors():
+        parts[VEC][...] = jnp.zeros(parts[VEC].shape, F32)
+        for j in range(4 * LINE):
+            slot = parts[VEC].at[j % 2, j // 4, (j // 2) % 2]
+            size = width // (4 * LINE)
+            slot[0:8, 0:size] = vec_one[0:8, j * size : (j + 1) * size]
+            query_part = mixed[:, j * size : (j + 1) * size].astype(F32)
+            slot[8:9, 0:size] = jnp.sum(query_part, axis=0, keepdims=True)
+            value_part = mixed[:, 2 * width + j * size : 2 * width + (j + 1) * size].astype(F32)
+            slot[9:10, 0:size] = jnp.sum(value_part, axis=0, keepdims=True)
+            at = (j % 4) * 4 * size
+            slot[10:11, 0 : 4 * size] = vec_one[8 + j // 4 : 9 + j // 4, at : at + 4 * size]
+        core_copy(VEC).start()
+
     head_grads(0)
-    ready(0, 2)
+    head_grads(1)
+    ready(0, 3)
     multiply(DOWN)
-    head_grads(1)
+    multiply(DOWN_B)
     send_kv(0)
     add_core(DOWN)
     head_grads(2)
@@ -1163,65 +1222,53 @@
         query_back(k).start()
     query_land[line] = query_grads[half_block(line)]
     send_kv(1)
-    ready(2, 4)
+    add_core(DOWN_B)
+    ready(3, 4)
     multiply(UP)
+    stage(DOWN, 1)
     send_kv(2)
-    for k in (1, 2, 3):
-        query_landed(k).wait_recv()
-    for d in range(LINE):
-        for i in range(2):
-            mixed[i * rows // 2 : (i + 1) * rows // 2, d * third : (d + 1) * third] = query_land[
-                d, :, i * third : (i + 1) * third
-            ]
-    mixed_copies[0].start()
+    ready(4, 5)
+    multiply(UP_B)
     add_core(UP)
-    ready(4, 6)
+    query_done()
+    stage(DOWN_B, 1)
+    stage(DOWN, 2)
+    add_core(UP_B)
+    ready(5, 7)
     multiply(OUT)
-    for h in range(HEADS_OWN):
-        for k in (1, 2, 3):
-            kv_landed(h, k).wait_recv()
-        for d in range(LINE):
-            at = width + d * third + h * HEAD
-            mixed[:, at : at + HEAD] = kv_land[h, d, :, 0:HEAD]
-            mixed[:, width + at : width + at + HEAD] = kv_land[h, d, :, HEAD:]
-    for part in (1, 2):
-        mixed_copies[part].start()
-    add_pair(DOWN)
+    kv_done()
+    stage(DOWN, 3)
+    stage(DOWN_B, 2)
     mixed_copies[0].wait_recv()
     multiply(QUERY)
     add_core(OUT)
-    first_hop(DOWN)
-    parts[VEC][...] = jnp.zeros(parts[VEC].shape, F32)
-    for j in range(4 * LINE):
-        slot = parts[VEC].at[j % 2, j // 4, (j // 2) % 2]
-        size = width // (4 * LINE)
-        slot[0:8, 0:size] = vec_one[0:8, j * size : (j + 1) * size]
-        query_part = mixed[:, j * size : (j + 1) * size].astype(F32)
-        slot[8:9, 0:size] = jnp.sum(query_part, axis=0, keepdims=True)
-        value_part = mixed[:, 2 * width + j * size : 2 * width + (j + 1) * size].astype(F32)
-        slot[9:10, 0:size] = jnp.sum(value_part, axis=0, keepdims=True)
-        at = (j % 4) * 4 * size
-        slot[10:11, 0 : 4 * size] = vec_one[8 + j // 4 : 9 + j // 4, at : at + 4 * size]
-    core_copy(VEC).start()
-    for part in (1, 2):
-        mixed_copies[part].wait_recv()
-        multiply(QUERY + part)
+    stage(UP, 1)
+    stage(DOWN_B, 3)
+    stage(DOWN, 4)
+    pack_vectors()
+    mixed_copies[1].wait_recv()
+    multiply(KEY)
     add_core(QUERY)
-    second_hop(DOWN)
+    stage(UP, 2)
+    stage(DOWN_B, 4)
+    mixed_copies[2].wait_recv()
+    multiply(VALUE)
     add_core(KEY)
+    stage(UP_B, 1)
+    stage(UP, 3)
     add_core(VALUE)
     add_core(VEC)
+    stage(OUT, 1)
+    stage(UP_B, 2)
     grad_hidden[...] = first[...] + dot_nt(mixed[...], w_all[...])
-    add_pair(UP)
-    for s in range(2, VEC + 4):
-        if s <= VEC:
-            add_pair(s)
-        if 1 <= s - 1 <= VEC:
-            first_hop(s - 1)
-        if 1 <= s - 2 <= VEC:
-            second_hop(s - 2)
-        if s - 3 <= VEC and s >= 3:
-            finish_unit(s - 3)
+    stage(UP, 4)
+    stage(UP_B, 3)
+    for s in range(QUERY, VEC + 4):
+        for n in (1, 2, 3, 4):
+            if OUT <= s + 1 - n <= VEC:
+                stage(s + 1 - n, n)
+        if s == QUERY:
+            stage(UP_B, 4)
     for u in units:
         last_copy(u).wait_recv()
     vec_own[...] = parts[VEC][core, line, side] + vec_seq[...]
@@ -1258,10 +1305,10 @@
     third = HEADS_OWN * HEAD
     mid, seq_rows = LINE * rows, 2 * LINE * rows
     shape = jax.ShapeDtypeStruct
-    widths = ((ffn // 2, width), (width, ffn // 2)) + ((width, width // 2),) * 4
+    widths = ((ffn // 2, width // 2),) * 2 + ((width, ffn // 4),) * 2 + ((width, width // 2),) * 4
     dims = [(a // (4 * LINE), b, a == width) for a, b in widths]
-    own_shapes = [(r, 2 * c) if wide else (2 * r, c) for r, c, wide in dims[: OUT + 1]]
-    own_shapes.insert(OUT, (own_shapes[UP][0], 3 * width))
+    shard, ffn_shard = width // (4 * LINE), ffn // (4 * LINE)
+    own_shapes = [(ffn_shard, width), (shard, ffn), (shard, 3 * width), (shard, width)]
     blocks = [((r, c), BF16) for r, c, _ in dims] + [((16, 256), F32)]
     count = len(blocks)
     vmem, dma = pltpu.VMEM, pltpu.SemaphoreType.DMA
@@ -1319,8 +1366,8 @@
             dma((3,)),
             dma((4, 3)),
             dma((4, 3)),
-            dma((9,)),
-            dma((9,)),
+            dma((10,)),
+            dma((10,)),
             dma((2, count)),
             dma((2, count, LINE)),
             dma((2, count, LINE - 1)),

time: 150 us -> 142 us (0.947)
  Pallas kernels: 149 us -> 141 us
    pallas_call x1, Pallas kernels: 100 us -> 92.1 us  [backward(): pl.pallas_call(functools.partial(backward_kernel, dims), out_shape=outs,...]
where the time goes in v5:
time: 142 us; the launch traced here: 141 us
  Pallas kernels  141 us (99%)
    pallas_call x1, Pallas kernels, backward(): pl.pallas_call(functools.partial(backward_kernel, dims), out_shape=outs,...  92.1 us
    pallas_call x1, Pallas kernels, attend_forward(): pl.pallas_call(attend_kernel, out_shape=[o[0] for o in outs], in_specs=[I...  45.6 us
    pallas_call x1, Pallas kernels, finish(): pl.pallas_call(finish_kernel, out_shape=outs, in_specs=[INNER] * 7, out_s...  2.98 us

profile of v5, /device:TPU:0, one launch (start us, length us, event | category | flops | bytes accessed | tf_op | source)
XLA Modules:
  0.0 141.5 jit_solution(17733382499249562341)
XLA Ops:
  0.6 45.6 %attend_forward.1 = (bf16[160,768]{1,0:T(8,128)(2,1)}, bf16[160,768]{1,0:T(8,128)(2,1)}, f32[16,768]{1,0:T(8,128)}, bf16[768,2304]{1,0:T(8,128)(2,1)}, bf16[384,...) custom-call(bf16[160,768]{1,0:T(8,128)(2,1)} %bitcast.4, ...), custom_call_target="tpu_custom_call" | custom-call | tf_op jit(solution)/shard_map/attend_forward/pallas_call | solution.py:617
  46.2 92.1 %backward.1 = (bf16[160,768]{1,0:T(8,128)(2,1)}, f32[160,768]{1,0:T(8,128)}, bf16[192,768]{1,0:T(8,128)(2,1)}, bf16[48,3072]{1,0:T(8,128)(2,1)}, bf16[48,2304]{1...) custom-call(bf16[160,768]{1,0:T(8,128)(2,1)} %get-tuple-element.50.attended, bf16[160,768]{1,0:T(8,128)(2,1)} %bitcast.5, ...), custom_call_target="tpu_custom_call" | custom-call | tf_op jit(solution)/shard_map/backward/pallas_call | solution.py:1318
  138.3 3.0 %finish.1 = (f32[48,3072]{1,0:T(8,128)}, f32[192,768]{1,0:T(8,128)}, f32[48,2304]{1,0:T(8,128)}, f32[48,768]{1,0:T(8,128)}, f32[160,768]{1,0:T(8,128)}, /*index=...) custom-call(bf16[48,3072]{1,0:T(8,128)(2,1)} %get-tuple-element.63.r, ...), custom_call_target="tpu_custom_call" | custom-call | tf_op jit(solution)/shard_map/finish/pallas_call | solution.py:1398

commit v6 on v5

--- a/solution.py
+++ b/solution.py
@@ -344,12 +344,15 @@
     out_other,
     up_other,
     down_other,
+    q_out,
+    k_out,
+    v_out,
+    att_full,
+    totals,
+    probs_out,
     q_heads,
     k_heads,
     v_heads,
-    att_full,
-    totals,
-    probs_out,
     w_all,
     mixed,
     sent_kv,
@@ -416,15 +419,20 @@
     vec[at:] = jnp.zeros((vec.shape[0] - at, half), F32)
     greet([to_core, to_pair, to_seq] + [to_line(k) for k in range(1, LINE)])
     core_copies = [
-        remote(w_qkv, w_all.at[own_rows], core_out.at[0], core_in.at[0], to_core),
-        remote(vec, vec_all.at[:, own_rows], core_out.at[1], core_in.at[1], to_core),
-        remote(w_out, out_other, core_out.at[2], core_in.at[2], to_core),
-        remote(w_up, up_other, core_out.at[3], core_in.at[3], to_core),
-        remote(w_down, down_other, core_out.at[4], core_in.at[4], to_core),
+        remote(vec, vec_all.at[:, own_rows], core_out.at[0], core_in.at[0], to_core),
+        remote(w_out, out_other, core_out.at[1], core_in.at[1], to_core),
+        remote(w_up, up_other, core_out.at[2], core_in.at[2], to_core),
+        remote(w_down, down_other, core_out.at[3], core_in.at[3], to_core),
     ]
+    qkv_copies = []
+    for part in range(3):
+        lanes = slice(part * width, (part + 1) * width)
+        sems = core_out.at[4 + part], core_in.at[4 + part]
+        qkv_copies.append(remote(w_qkv.at[:, lanes], w_all.at[own_rows, lanes], *sems, to_core))
     seq_copy = remote(tok, tok_pair, seq_out.at[0], seq_in.at[0], to_seq)
     core_copies[0].start()
-    core_copies[1].start()
+    for part in (1, 2, 0):
+        qkv_copies[part].start()
     seq_copy.start()
     vec_all[:, own_rows] = vec[...]
     own_load.wait()
@@ -434,9 +442,6 @@
             tok[:, own_rows], w_all[own_rows, first : first + step]
         )
     core_copies[0].wait_recv()
-    core_copies[1].wait_recv()
-    for copy in core_copies[2:]:
-        copy.start()
 
     def kv_copy(k, to):
         return remote(
@@ -462,6 +467,7 @@
 
     bias = vec_all[...]
     for part in (1, 2, 0):
+        qkv_copies[part].wait_recv()
         for first in range(part * width, (part + 1) * width, step):
             total = mixed[:, first : first + step] + dot_nn(
                 tok[:, other_rows], w_all[other_rows, first : first + step]
@@ -479,7 +485,7 @@
                     sent_q[d, :, third:] = piece[rows // 2 :]
                 else:
                     sent_kv[d, :, (part - 1) * third : part * third] = piece
-        for k in (3, 2, 1):
+        for k in (1, 2, 3):
             if part == 2:
                 kv_copy(k, line).start()
             if part == 0:
@@ -487,6 +493,8 @@
         if part == 2:
             mine[block(line)] = sent_kv[line]
             pair_copy(0).start()
+    for copy in core_copies[1:]:
+        copy.start()
     full_store = pltpu.make_async_copy(w_all, w_full, local_sem.at[1])
     full_store.start()
     mine_q[half_block(line)] = sent_q[line]
@@ -517,6 +525,11 @@
         k_heads[h, mid:seq_rows] = other[:, h * HEAD : (h + 1) * HEAD]
         v_heads[h, mid:seq_rows] = other[:, third + h * HEAD : third + (h + 1) * HEAD]
 
+    head_stores = []
+    for i, (src, dst) in enumerate(((q_heads, q_out), (k_heads, k_out), (v_heads, v_out))):
+        head_stores.append(pltpu.make_async_copy(src, dst, local_sem.at[2 + i]))
+        head_stores[i].start()
+
     def back_copy(k):
         return remote(
             att_sent.at[ahead(k)],
@@ -585,10 +598,12 @@
     for k in range(LINE):
         pair_copy(k).wait_send()
         probs_copy(k + 1).wait()
-    for copy in core_copies[2:]:
+    for copy in core_copies[1:]:
         copy.wait_recv()
-    for copy in core_copies:
+    for copy in core_copies + qkv_copies:
         copy.wait_send()
+    for store in head_stores:
+        store.wait()
     seq_copy.wait()
     full_store.wait()
 
@@ -606,9 +621,9 @@
         (shape(w_out.shape, BF16), ANY),
         (shape(w_up.shape, BF16), ANY),
         (shape(w_down.shape, BF16), ANY),
-        (shape((HEADS_OWN, mid, HEAD), BF16), INNER),
-        (shape((HEADS_OWN, seq_rows, HEAD), BF16), INNER),
-        (shape((HEADS_OWN, seq_rows, HEAD), BF16), INNER),
+        (shape((HEADS_OWN, mid, HEAD), BF16), ANY),
+        (shape((HEADS_OWN, seq_rows, HEAD), BF16), ANY),
+        (shape((HEADS_OWN, seq_rows, HEAD), BF16), ANY),
         (shape((mid, third), F32), INNER),
         (shape((mid, 128), F32), INNER),
         (shape((HEADS_OWN, mid, seq_rows), BF16), ANY),
@@ -620,6 +635,9 @@
         in_specs=[INNER, INNER, [INNER] * len(small)] + [ANY] * 4,
         out_specs=[o[1] for o in outs],
         scratch_shapes=[
+            pltpu.VMEM((HEADS_OWN, mid, HEAD), BF16),
+            pltpu.VMEM((HEADS_OWN, seq_rows, HEAD), BF16),
+            pltpu.VMEM((HEADS_OWN, seq_rows, HEAD), BF16),
             pltpu.VMEM((width, 3 * width), BF16),
             pltpu.VMEM((rows, 3 * width), F32),
             pltpu.VMEM((LINE, rows, 2 * third), BF16),
@@ -633,10 +651,10 @@
             pltpu.VMEM((16, width // 2), F32),
             pltpu.VMEM((1, seq_rows), F32),
             pltpu.VMEM((mid, 1), F32),
-            dma((2,)),
+            dma((5,)),
             dma((LINE,)),
-            dma((5,)),
-            dma((5,)),
+            dma((7,)),
+            dma((7,)),
             dma((2, 3)),
             dma((2, 3)),
             dma((LINE,)),
@@ -984,8 +1002,6 @@
         )
     ):
         late_loads.append(pltpu.make_async_copy(src, dst, local_sem.at[i]))
-    for load in late_loads:
-        load.start()
     greet([to_core, to_pair, to_seq] + [to_line(k) for k in range(1, LINE)])
 
     def arrived(i):
@@ -1018,6 +1034,8 @@
             act_halves[g, :, j * piece : (j + 1) * piece] = active[:, at : at + piece]
     seq_copies[1].start()
     arrived(2)
+    for load in late_loads:
+        load.start()
     second = normed_one + bias_down
     second += dot_nn(active[...], down_all[...])
     final, norm_two, scale_two = norm_forward(second, gain_two, shift_two)
@@ -1077,7 +1095,7 @@
             to_line(k),
         )
 
-    for k in (3, 2, 1):
+    for k in (1, 2, 3):
         line_copy(k).start()
     mixed_copies = []
     for part in range(3):
@@ -1171,7 +1189,7 @@
     def send_kv(h):
         pair_copy(h).wait_recv()
         kv_sum[h] = (kv_own[h] + kv_pair[h].astype(F32)).astype(BF16)
-        for k in (3, 2, 1):
+        for k in (1, 2, 3):
             kv_back(h, k).start()
         kv_land[h, line] = kv_sum[h, block(line)]
 
@@ -1218,7 +1236,7 @@
     send_kv(0)
     add_core(DOWN)
     head_grads(2)
-    for k in (3, 2, 1):
+    for k in (1, 2, 3):
         query_back(k).start()
     query_land[line] = query_grads[half_block(line)]
     send_kv(1)

time: 142 us -> 136 us (0.958)
  Pallas kernels: 141 us -> 135 us
    pallas_call x1, Pallas kernels: 45.6 us -> 40.6 us  [attend_forward(): pl.pallas_call(attend_kernel, out_shape=[o[0] for o in outs], in_specs=[I...]
where the time goes in v6:
time: 136 us
  Pallas kernels  135 us (99%)
    pallas_call x1, Pallas kernels, backward(): pl.pallas_call(functools.partial(backward_kernel, dims), out_shape=outs,...  91.5 us
    pallas_call x1, Pallas kernels, attend_forward(): pl.pallas_call(attend_kernel, out_shape=[o[0] for o in outs], in_specs=[I...  40.6 us
    pallas_call x1, Pallas kernels, finish(): pl.pallas_call(finish_kernel, out_shape=outs, in_specs=[INNER] * 7, out_s...  2.98 us

profile of v6, /device:TPU:0, one launch (start us, length us, event | category | flops | bytes accessed | tf_op | source)
XLA Modules:
  0.0 135.9 jit_solution(11969461689294257150)
XLA Ops:
  0.6 40.6 %attend_forward.1 = (bf16[160,768]{1,0:T(8,128)(2,1)}, bf16[160,768]{1,0:T(8,128)(2,1)}, f32[16,768]{1,0:T(8,128)}, bf16[768,2304]{1,0:T(8,128)(2,1)}, bf16[384,...) custom-call(bf16[160,768]{1,0:T(8,128)(2,1)} %bitcast.4, ...), custom_call_target="tpu_custom_call" | custom-call | tf_op jit(solution)/shard_map/attend_forward/pallas_call | solution.py:632
  41.3 91.5 %backward.1 = (bf16[160,768]{1,0:T(8,128)(2,1)}, f32[160,768]{1,0:T(8,128)}, bf16[192,768]{1,0:T(8,128)(2,1)}, bf16[48,3072]{1,0:T(8,128)(2,1)}, bf16[48,2304]{1...) custom-call(bf16[160,768]{1,0:T(8,128)(2,1)} %get-tuple-element.50.attended, bf16[160,768]{1,0:T(8,128)(2,1)} %bitcast.5, ...), custom_call_target="tpu_custom_call" | custom-call | tf_op jit(solution)/shard_map/backward/pallas_call | solution.py:1336
  132.7 3.0 %finish.1 = (f32[48,3072]{1,0:T(8,128)}, f32[192,768]{1,0:T(8,128)}, f32[48,2304]{1,0:T(8,128)}, f32[48,768]{1,0:T(8,128)}, f32[160,768]{1,0:T(8,128)}, /*index=...) custom-call(bf16[48,3072]{1,0:T(8,128)(2,1)} %get-tuple-element.63.r, ...), custom_call_target="tpu_custom_call" | custom-call | tf_op jit(solution)/shard_map/finish/pallas_call | solution.py:1416

commit v7 on v6

--- a/solution.py
+++ b/solution.py
@@ -347,9 +347,11 @@
     q_out,
     k_out,
     v_out,
+    att_out,
+    totals_out,
+    probs_out,
     att_full,
     totals,
-    probs_out,
     q_heads,
     k_heads,
     v_heads,
@@ -583,6 +585,9 @@
         return carry
 
     lax.fori_loop(1, LINE + 1, attend, 0)
+    for i, (src, dst) in enumerate(((att_full, att_out), (totals, totals_out))):
+        head_stores.append(pltpu.make_async_copy(src, dst, local_sem.at[5 + i]))
+        head_stores[-1].start()
     att_land[line] = att_sent[line]
     for k in (1, 2, 3):
         back_landed(k).wait_recv()
@@ -624,8 +629,8 @@
         (shape((HEADS_OWN, mid, HEAD), BF16), ANY),
         (shape((HEADS_OWN, seq_rows, HEAD), BF16), ANY),
         (shape((HEADS_OWN, seq_rows, HEAD), BF16), ANY),
-        (shape((mid, third), F32), INNER),
-        (shape((mid, 128), F32), INNER),
+        (shape((mid, third), F32), ANY),
+        (shape((mid, 128), F32), ANY),
         (shape((HEADS_OWN, mid, seq_rows), BF16), ANY),
     ]
     dma = pltpu.SemaphoreType.DMA
@@ -635,6 +640,8 @@
         in_specs=[INNER, INNER, [INNER] * len(small)] + [ANY] * 4,
         out_specs=[o[1] for o in outs],
         scratch_shapes=[
+            pltpu.VMEM((mid, third), F32),
+            pltpu.VMEM((mid, 128), F32),
             pltpu.VMEM((HEADS_OWN, mid, HEAD), BF16),
             pltpu.VMEM((HEADS_OWN, seq_rows, HEAD), BF16),
             pltpu.VMEM((HEADS_OWN, seq_rows, HEAD), BF16),
@@ -651,7 +658,7 @@
             pltpu.VMEM((16, width // 2), F32),
             pltpu.VMEM((1, seq_rows), F32),
             pltpu.VMEM((mid, 1), F32),
-            dma((5,)),
+            dma((7,)),
             dma((LINE,)),
             dma((7,)),
             dma((7,)),
@@ -701,6 +708,8 @@
     qkv_own,
     out_own,
     vec_own,
+    result_rows,
+    hidden_rows,
     out_all,
     up_all,
     down_all,
@@ -1039,7 +1048,12 @@
     second = normed_one + bias_down
     second += dot_nn(active[...], down_all[...])
     final, norm_two, scale_two = norm_forward(second, gain_two, shift_two)
-    result[...] = final.astype(BF16)
+    result_rows[...] = final.astype(BF16)
+    stores = [
+        pltpu.make_async_copy(result_rows, result, local_sem.at[8]),
+        pltpu.make_async_copy(hidden_rows, grad_hidden, local_sem.at[9]),
+    ]
+    stores[0].start()
     grad_second, gain_grad, shift_grad = norm_backward(
         grad_out[...].astype(F32), norm_two, scale_two, gain_two
     )
@@ -1278,7 +1292,8 @@
     add_core(VEC)
     stage(OUT, 1)
     stage(UP_B, 2)
-    grad_hidden[...] = first[...] + dot_nt(mixed[...], w_all[...])
+    hidden_rows[...] = first[...] + dot_nt(mixed[...], w_all[...])
+    stores[1].start()
     stage(UP, 4)
     stage(UP_B, 3)
     for s in range(QUERY, VEC + 4):
@@ -1289,6 +1304,8 @@
             stage(UP_B, 4)
     for u in units:
         last_copy(u).wait_recv()
+    for store in stores:
+        store.wait()
     vec_own[...] = parts[VEC][core, line, side] + vec_seq[...]
     for k in (1, 2, 3):
         line_copy(k).wait_send()
@@ -1337,8 +1354,10 @@
         functools.partial(backward_kernel, dims),
         out_shape=outs,
         in_specs=[INNER] * 4 + [ANY] * 14,
-        out_specs=[INNER] * len(outs),
+        out_specs=[ANY] * 2 + [INNER] * (len(outs) - 2),
         scratch_shapes=[
+            vmem((rows, width), BF16),
+            vmem((rows, width), F32),
             vmem((width, width), BF16),
             vmem((width, ffn), BF16),
             vmem((ffn, width), BF16),
@@ -1377,7 +1396,7 @@
             [vmem((LINE - 1,) + block, kind) for block, kind in blocks],
             vmem((16, 256), F32),
             dma((6,)),
-            dma((8,)),
+            dma((10,)),
             dma((3,)),
             dma((3,)),
             dma((3,)),

time: 136 us -> 136 us (level)
  no operation moved by 1% of the time
where the time goes in v7:
time: 136 us; the launch traced here: 135 us
  Pallas kernels  134 us (99%)
    pallas_call x1, Pallas kernels, backward(): pl.pallas_call(functools.partial(backward_kernel, dims), out_shape=outs,...  91.2 us
    pallas_call x1, Pallas kernels, attend_forward(): pl.pallas_call(attend_kernel, out_shape=[o[0] for o in outs], in_specs=[I...  40.3 us
    pallas_call x1, Pallas kernels, finish(): pl.pallas_call(finish_kernel, out_shape=outs, in_specs=[INNER] * 7, out_s...  2.98 us

profile of v7, /device:TPU:0, one launch (start us, length us, event | category | flops | bytes accessed | tf_op | source)
XLA Modules:
  0.0 135.3 jit_solution(5575321759428980842)
XLA Ops:
  0.6 40.3 %attend_forward.1 = (bf16[160,768]{1,0:T(8,128)(2,1)}, bf16[160,768]{1,0:T(8,128)(2,1)}, f32[16,768]{1,0:T(8,128)}, bf16[768,2304]{1,0:T(8,128)(2,1)}, bf16[384,...) custom-call(bf16[160,768]{1,0:T(8,128)(2,1)} %bitcast.4, ...), custom_call_target="tpu_custom_call" | custom-call | tf_op jit(solution)/shard_map/attend_forward/pallas_call | solution.py:637
  41.0 91.2 %backward.1 = (bf16[160,768]{1,0:T(8,128)(2,1)}, f32[160,768]{1,0:T(8,128)}, bf16[192,768]{1,0:T(8,128)(2,1)}, bf16[48,3072]{1,0:T(8,128)(2,1)}, bf16[48,2304]{1...) custom-call(bf16[160,768]{1,0:T(8,128)(2,1)} %get-tuple-element.50.attended, bf16[160,768]{1,0:T(8,128)(2,1)} %bitcast.5, ...), custom_call_target="tpu_custom_call" | custom-call | tf_op jit(solution)/shard_map/backward/pallas_call | solution.py:1353
  132.2 3.0 %finish.1 = (f32[48,3072]{1,0:T(8,128)}, f32[192,768]{1,0:T(8,128)}, f32[48,2304]{1,0:T(8,128)}, f32[48,768]{1,0:T(8,128)}, f32[160,768]{1,0:T(8,128)}, /*index=...) custom-call(bf16[48,3072]{1,0:T(8,128)(2,1)} %get-tuple-element.63.r, ...), custom_call_target="tpu_custom_call" | custom-call | tf_op jit(solution)/shard_map/finish/pallas_call | solution.py:1435
